TPU v7x, 256 devices: a whole 4x4x8 slice. The times are simulated.
256 devices in a mesh: dp: 32 (over z, y), ep: 8 (over x, core).
Axes of the slice: x: 4, y: 4, z: 8, core: 2. Of those that a mesh axis runs over, the one named last changes fastest.
Arguments:
- states: bfloat16 [2048, 16, 128, 128], P(('dp', 'ep')), may hold values from -4 to 4
- query_rows: bfloat16 [2048, 4, 1024], P(('dp', 'ep')), may hold values from -6 to 6
- key_rows: bfloat16 [2048, 4, 1024], P(('dp', 'ep')), may hold values from -6 to 6
- value_rows: bfloat16 [2048, 4, 2048], P(('dp', 'ep')), may hold values from -6 to 6
- gate_rows: bfloat16 [2048, 4, 2048], P(('dp', 'ep')), may hold values from -6 to 6
- beta_logit: bfloat16 [2048, 4, 16], P(('dp', 'ep')), may hold values from -6 to 6
- decay_logit: bfloat16 [2048, 4, 16], P(('dp', 'ep')), may hold values from -8 to 8
- residual: bfloat16 [2048, 4, 2048], P(('dp', 'ep')), may hold values from -6 to 6
- route_ids: int32 [2048, 4, 10], P(('dp', 'ep')), may hold values from 0 to 255, all different within a row; in each aligned block of 32 rows (0 to 31, 32 to 63, ..., all dimensions but the last counted through in order) at most 3 rows name the same one
- route_prob: float32 [2048, 4, 10], P(('dp', 'ep')), may hold values from 0.05 to 1
- out_weight: bfloat16 [2048, 2048], P(None, 'ep'), may hold values from -0.125 to 0.125
- core_gain: float32 [128], replicated, may hold values from 0.1 to 1.9
- moe_gain: float32 [2048], replicated, may hold values from 0.1 to 1.9
- gate_up: bfloat16 [256, 2048, 512], P(('dp', 'ep')), may hold values from -0.125 to 0.125
- down_weight: bfloat16 [256, 256, 2048], P(('dp', 'ep')), may hold values from -0.375 to 0.375
- new_home: int32 [2048], P(('dp', 'ep')), may hold values from 0 to 2047, as said below
Outputs:
- mixed_out: bfloat16 [2048, 4, 2048], P(('dp', 'ep'))
- moved_out: bfloat16 [2048, 16, 128, 128], P(('dp', 'ep'))
Inputs may be any that keep to these rules, and one draw needn't show every extreme that they name: `route_ids`: each row names 10 different experts; among the 32 rows of one device (its requests, each with its 4 tokens) no expert is named more than 3 times, a bound that some block reaches. `new_home`: A permutation of the request positions; a request stays among the 8 devices of its dp index, and every device hands exactly 1 of its requests to each device of that group, itself included.
All inputs are finite; a program needn't handle non-finite values.
Results may differ from a plain program's by a relative error of at most 0.01.
Values may be sent and summed in bfloat16 or wider, within the bound.
A program may use at most 128 MiB of HBM per device.

v0:
```python
import jax
import jax.numpy as jnp
from jax import lax
from jax.sharding import PartitionSpec as P

epsilon = 1e-06


def unit_rows(values):
    return values * lax.rsqrt(jnp.sum(values * values, -1, keepdims=True) + epsilon)


def delta_block(
    state_in, query_rows, key_rows, value_rows, gate_rows, beta_logit, decay_logit, core_gain
):
    batch_size = state_in.shape[0]
    head_count = decay_logit.shape[-1]
    head_width = state_in.shape[-1]
    key_heads = query_rows.shape[-1] // head_width
    repeats = head_count // key_heads
    memory_state = state_in.astype(jnp.float32)
    outputs = []
    for position in range(query_rows.shape[1]):
        queries = unit_rows(
            query_rows[:, position].astype(jnp.float32).reshape(batch_size, key_heads, head_width)
        )
        queries = jnp.repeat(queries, repeats, axis=1) * head_width ** (-0.5)
        key_units = unit_rows(
            key_rows[:, position].astype(jnp.float32).reshape(batch_size, key_heads, head_width)
        )
        key_units = jnp.repeat(key_units, repeats, axis=1)
        values = (
            value_rows[:, position].astype(jnp.float32).reshape(batch_size, head_count, head_width)
        )
        decays = jax.nn.sigmoid(decay_logit[:, position].astype(jnp.float32))
        strength = jax.nn.sigmoid(beta_logit[:, position].astype(jnp.float32))
        memory_state = memory_state * decays[:, :, None, None]
        memory = jnp.einsum(
            "bhkv,bhk->bhv", memory_state, key_units, precision=lax.Precision.HIGHEST
        )
        update = (values - memory) * strength[:, :, None]
        memory_state = memory_state + key_units[:, :, :, None] * update[:, :, None, :]
        reading = jnp.einsum(
            "bhkv,bhk->bhv", memory_state, queries, precision=lax.Precision.HIGHEST
        )
        scaled = reading * lax.rsqrt(jnp.mean(reading * reading, -1, keepdims=True) + epsilon)
        gate_vals = (
            gate_rows[:, position].astype(jnp.float32).reshape(batch_size, head_count, head_width)
        )
        gated_out = scaled * core_gain * jax.nn.silu(gate_vals)
        outputs.append(gated_out.reshape(batch_size, head_count * head_width).astype(jnp.bfloat16))
    return (memory_state.astype(jnp.bfloat16), jnp.stack(outputs, axis=1))


def rms_scale(values, gain):
    return values * lax.rsqrt(jnp.mean(values * values, -1, keepdims=True) + epsilon) * gain


def expert_apply(chosen_rows, gate_up, down_weight):
    hidden_units = down_weight.shape[0]
    joined = jnp.dot(chosen_rows, gate_up, preferred_element_type=jnp.float32)
    active = (jax.nn.silu(joined[:, :hidden_units]) * joined[:, hidden_units:]).astype(jnp.bfloat16)
    return jnp.dot(active, down_weight, preferred_element_type=jnp.float32).astype(jnp.bfloat16)


def pack(values, positions, lane_count):
    zeroed = jnp.zeros(values.shape, values.dtype)
    placed = zeroed.at[positions].set(values)
    return placed.reshape((lane_count, values.shape[0] // lane_count) + values.shape[1:])


def unpack(values):
    return values.reshape((values.shape[0] * values.shape[1],) + values.shape[2:])


def shards(
    states,
    query_rows,
    key_rows,
    value_rows,
    gate_rows,
    beta_logit,
    decay_logit,
    residual,
    route_ids,
    route_prob,
    out_weight,
    core_gain,
    moe_gain,
    gate_up,
    down_weight,
    new_home,
):
    req_count = states.shape[0]
    step_count = query_rows.shape[1]
    model_width = residual.shape[-1]
    ep_size = lax.axis_size("ep")
    dp_size = lax.axis_size("dp")
    target = new_home // req_count % ep_size
    new_place = new_home % req_count
    order_ids = jnp.arange(req_count, dtype=jnp.int32)
    earlier = (target[:, None] == target[None, :]) & (order_ids[None, :] < order_ids[:, None])
    lane_rank = jnp.sum(earlier.astype(jnp.int32), axis=1)
    lane_cap = req_count // ep_size
    buffer_index = target * lane_cap + lane_rank
    fresh_states, core_out = delta_block(
        states, query_rows, key_rows, value_rows, gate_rows, beta_logit, decay_logit, core_gain
    )
    received = (
        lax.all_to_all(
            pack(fresh_states, buffer_index, ep_size), "ep", split_axis=0, concat_axis=0, tiled=True
        ),
        lax.all_to_all(
            pack(new_place, buffer_index, ep_size), "ep", split_axis=0, concat_axis=0, tiled=True
        ),
    )
    moved_out = jnp.zeros_like(states).at[unpack(received[1])].set(unpack(received[0]), mode="drop")
    token_count = req_count * step_count
    core_flat = core_out.reshape(token_count, core_out.shape[-1])
    columns = jnp.dot(
        lax.all_gather(core_flat, "ep", axis=0, tiled=True),
        out_weight,
        preferred_element_type=jnp.float32,
    ).astype(jnp.bfloat16)
    attention = lax.all_to_all(columns, "ep", split_axis=0, concat_axis=1, tiled=True)
    hidden = (
        residual.reshape(token_count, model_width).astype(jnp.float32)
        + attention.astype(jnp.float32)
    ).astype(jnp.bfloat16)
    normed = rms_scale(hidden.astype(jnp.float32), moe_gain).astype(jnp.bfloat16)
    top_count = route_ids.shape[-1]
    experts = dp_size * ep_size
    capacity = (token_count * top_count + experts - 1) // experts + 1
    flat_ids = route_ids.reshape(-1)
    onehot = (flat_ids[:, None] == jnp.arange(experts, dtype=jnp.int32)[None, :]).astype(jnp.int32)
    route_rank = jnp.sum(jnp.cumsum(onehot, axis=0) * onehot, axis=1) - 1
    slot_index = flat_ids * capacity + route_rank
    outgoing = (
        jnp.zeros((experts * capacity, model_width), jnp.bfloat16)
        .at[slot_index]
        .set(jnp.repeat(normed, top_count, axis=0))
    )
    arrived = lax.all_to_all(
        lax.all_to_all(
            outgoing.reshape(dp_size, ep_size, capacity, model_width),
            "dp",
            split_axis=0,
            concat_axis=0,
            tiled=True,
        ),
        "ep",
        split_axis=1,
        concat_axis=1,
        tiled=True,
    )
    result = expert_apply(arrived.reshape(-1, model_width), gate_up[0], down_weight[0]).reshape(
        dp_size, ep_size, capacity, model_width
    )
    returned = lax.all_to_all(
        lax.all_to_all(result, "dp", split_axis=0, concat_axis=0, tiled=True),
        "ep",
        split_axis=1,
        concat_axis=1,
        tiled=True,
    )
    routed = returned.reshape(experts * capacity, model_width)[slot_index]
    weights = route_prob.reshape(token_count, top_count)
    weights = weights / jnp.sum(weights, -1, keepdims=True)
    combined = jnp.sum(
        routed.reshape(token_count, top_count, model_width).astype(jnp.float32)
        * weights[:, :, None],
        axis=1,
    )
    mixed_out = (
        (hidden.astype(jnp.float32) + combined)
        .astype(jnp.bfloat16)
        .reshape(req_count, step_count, model_width)
    )
    return (mixed_out, moved_out)


def solution(mesh):
    placed = (
        P(("dp", "ep"), None, None, None),
        P(("dp", "ep"), None, None),
        P(("dp", "ep"), None, None),
        P(("dp", "ep"), None, None),
        P(("dp", "ep"), None, None),
        P(("dp", "ep"), None, None),
        P(("dp", "ep"), None, None),
        P(("dp", "ep"), None, None),
        P(("dp", "ep"), None, None),
        P(("dp", "ep"), None, None),
        P(None, "ep"),
        P(),
        P(),
        P(("dp", "ep"), None, None),
        P(("dp", "ep"), None, None),
        P(("dp", "ep")),
    )
    return jax.shard_map(
        shards,
        mesh=mesh,
        in_specs=placed,
        out_specs=(P(("dp", "ep"), None, None), P(("dp", "ep"), None, None, None)),
        check_vma=False,
    )
```

profile of v0, /device:TPU:1, one launch (start us, length us, event | category | flops | bytes accessed | tf_op | source)
XLA Modules:
  0.0 570.6 jit_solution(461292190551067246)
XLA Ops:
  14.3 9.7 %fusion = f32[8,16,1,128]{3,2,1,0:T(1,128)S(1)} fusion(f32[8,16,128,1]{2,3,1,0:T(1,128)S(1)} %bitcast.152, bf16[8,16,128,128]{3,2,1,0:T(8,128)(2,1)} %param.16, f32[8,16]{1,0:T(8,128)S(1)} %get-tuple-element.37), kind=kOutput, calls=%fused_computation.10 | convolution fusion | flops 29360128 | bytes 4325888 | tf_op jit(solution)/shard_map/bhkv,bhk->bhv/dot_general | solution.py:38
  24.1 8.3 %fusion.2 = f32[8,16,1,128]{3,2,1,0:T(1,128)S(1)} fusion(f32[8,16,128,1]{2,3,1,0:T(1,128)S(1)} %bitcast.196, bf16[8,16,128,128]{3,2,1,0:T(8,128)(2,1)S(1)} %copy-done.1, f32[8,16,128]{2,1,0:T(8,128)S(1)} %subtract_multiply_fusion.3, f32[8,16,128]{2,1,0:T(8,128)S(1)} %bitcast.153, f32[8,16]{1,0:T(8,128)S(1)} %get-tuple-element.37), kind=kOutput, calls=%fused_computation.12 | convolution fusion | flops 33554432 | bytes 4456960 | tf_op jit(solution)/shard_map/bhkv,bhk->bhv/dot_general | solution.py:43
  32.6 9.0 %fusion.3 = f32[8,16,1,128]{3,2,1,0:T(1,128)S(1)} fusion(f32[8,16,128,1]{2,3,1,0:T(1,128)S(1)} %bitcast.161, bf16[8,16,128,128]{3,2,1,0:T(8,128)(2,1)S(1)} %copy-done.1, f32[8,16]{1,0:T(8,128)S(1)} %get-tuple-element.36, f32[8,16,128]{2,1,0:T(8,128)S(1)} %subtract_multiply_fusion.3, f32[8,16,128]{2,1,0:T(8,128)S(1)} %bitcast.154, ...), kind=kOutput, calls=%fused_computation.13 | convolution fusion | flops 35651584 | bytes 4457472 | tf_op jit(solution)/shard_map/bhkv,bhk->bhv/dot_general | solution.py:38
  41.7 11.6 %fusion.11 = f32[8,16,1,128]{3,2,1,0:T(1,128)S(1)} fusion(f32[8,16,128,1]{2,3,1,0:T(1,128)S(1)} %bitcast.197, bf16[8,16,128,128]{3,2,1,0:T(8,128)(2,1)S(1)} %copy-done.1, f32[8,16,128]{2,1,0:T(8,128)S(1)} %subtract_multiply_fusion.2, f32[8,16,128]{2,1,0:T(8,128)S(1)} %bitcast.162, f32[8,16]{1,0:T(8,128)S(1)} %get-tuple-element.36, ...), kind=kOutput, calls=%fused_computation.20 | convolution fusion | flops 39845888 | bytes 4588544 | tf_op jit(solution)/shard_map/bhkv,bhk->bhv/dot_general | solution.py:43
  53.4 11.7 %fusion.7 = f32[8,16,1,128]{3,2,1,0:T(1,128)S(1)} fusion(f32[8,16,128,1]{2,3,1,0:T(1,128)S(1)} %bitcast.168, bf16[8,16,128,128]{3,2,1,0:T(8,128)(2,1)S(1)} %copy-done.1, f32[8,16]{1,0:T(8,128)S(1)} %get-tuple-element.35, f32[8,16,128]{2,1,0:T(8,128)S(1)} %subtract_multiply_fusion.2, f32[8,16,128]{2,1,0:T(8,128)S(1)} %bitcast.163, ...), kind=kOutput, calls=%fused_computation.16 | convolution fusion | flops 41943040 | bytes 4589056 | tf_op jit(solution)/shard_map/bhkv,bhk->bhv/dot_general | solution.py:38
  65.2 15.5 %fusion.43 = f32[8,16,1,128]{3,2,1,0:T(1,128)S(1)} fusion(f32[8,16,128,1]{2,3,1,0:T(1,128)S(1)} %bitcast.198, bf16[8,16,128,128]{3,2,1,0:T(8,128)(2,1)S(1)} %copy-done.1, f32[8,16,128]{2,1,0:T(8,128)S(1)} %subtract_multiply_fusion.1, f32[8,16,128]{2,1,0:T(8,128)S(1)} %bitcast.169, f32[8,16]{1,0:T(8,128)S(1)} %get-tuple-element.35, ...), kind=kOutput, calls=%fused_computation.56 | convolution fusion | flops 46137344 | bytes 4720128 | tf_op jit(solution)/shard_map/bhkv,bhk->bhv/dot_general | solution.py:43
  80.9 15.6 %fusion.5 = f32[8,16,1,128]{3,2,1,0:T(1,128)S(1)} fusion(f32[8,16,128,1]{2,3,1,0:T(1,128)S(1)} %bitcast.173, f32[8,16]{1,0:T(8,128)S(1)} %get-tuple-element.34, bf16[8,16,128,128]{3,2,1,0:T(8,128)(2,1)S(1)} %copy-done.1, f32[8,16,128]{2,1,0:T(8,128)S(1)} %subtract_multiply_fusion.1, f32[8,16,128]{2,1,0:T(8,128)S(1)} %bitcast.170, ...), kind=kOutput, calls=%fused_computation.14 | convolution fusion | flops 48234496 | bytes 4720640 | tf_op jit(solution)/shard_map/bhkv,bhk->bhv/dot_general | solution.py:38
  96.8 21.1 %fusion.10 = f32[8,16,1,128]{3,2,1,0:T(1,128)S(1)} fusion(f32[8,16,128,1]{2,3,1,0:T(1,128)S(1)} %bitcast.199, f32[8,16,128]{2,1,0:T(8,128)S(1)} %subtract_multiply_fusion, f32[8,16,128]{2,1,0:T(8,128)S(1)} %bitcast.174, f32[8,16]{1,0:T(8,128)S(1)} %get-tuple-element.34, bf16[8,16,128,128]{3,2,1,0:T(8,128)(2,1)S(1)} %copy-done.1, ...), kind=kOutput, calls=%fused_computation.19 | convolution fusion | flops 52428800 | bytes 4851712 | tf_op jit(solution)/shard_map/bhkv,bhk->bhv/dot_general | solution.py:43
  120.4 29.2 %all-gather.2.cloned.1.call-done = bf16[256,2048]{1,0:T(8,128)(2,1)} async-done(((bf16[32,2048]{1,0:T(8,128)(2,1)}), bf16[256,2048]{1,0:T(8,128)(2,1)}) %all-gather.2.cloned.1.call-update) | async-done | bytes 1048592 | tf_op jit(solution)/shard_map/all_gather | solution.py:121
  167.8 5.4 scatter_custom_fusion
  173.2 9.1 %reshape.504 = bf16[32,8,3,2048]{3,2,1,0:T(4,128)(2,1)} reshape(bf16[768,2048]{1,0:T(8,128)(2,1)} %scatter_custom_fusion) | data formatting | bytes 6291456 | tf_op jit(solution)/shard_map/reshape | solution.py:145
  182.3 5.5 copy.104
  187.8 80.3 %all_to_all.50 = bf16[32,8,3,2048]{3,1,2,0:T(8,128)(2,1)S(1)} all-to-all(bf16[32,8,3,2048]{3,1,2,0:T(8,128)(2,1)S(1)} %copy.104), channel_id=1, replica_groups=mesh['dp'=32,'ep'=8] {'dp'}, dimensions={0} | all-to-all | bytes 6291456 | tf_op jit(solution)/shard_map/all_to_all | solution.py:144
  271.6 7.4 %all-to-all-start.2 = ((bf16[32,8,3,2048]{3,0,2,1:T(8,128)(2,1)}), bf16[32,8,3,2048]{3,0,2,1:T(8,128)(2,1)}, u32[]{:S(2)}, u32[]{:S(2)}) async-start(bf16[32,8,3,2048]{3,0,2,1:T(8,128)(2,1)} %copy.105), calls=%async_computation.2 | async-start | bytes 6291456 | tf_op jit(solution)/shard_map/all_to_all | solution.py:143
  280.5 36.2 %all-to-all-done.2 = bf16[32,8,3,2048]{3,0,2,1:T(8,128)(2,1)} async-done(((bf16[32,8,3,2048]{3,0,2,1:T(8,128)(2,1)}), bf16[32,8,3,2048]{3,0,2,1:T(8,128)(2,1)}, u32[]{:S(2)}, u32[]{:S(2)}) %all-to-all-start.2) | async-done | bytes 3145760 | tf_op jit(solution)/shard_map/all_to_all | solution.py:143
  321.0 6.6 %copy.106 = bf16[32,8,3,2048]{3,2,1,0:T(4,128)(2,1)} copy(bf16[32,8,3,2048]{3,0,2,1:T(8,128)(2,1)} %all-to-all-done.2) | data formatting | bytes 6291456 | tf_op jit(solution)/shard_map/all_to_all | solution.py:143
  327.6 8.8 %reshape.505 = bf16[768,2048]{1,0:T(8,128)(2,1)} reshape(bf16[32,8,3,2048]{3,2,1,0:T(4,128)(2,1)} %copy.106) | data formatting | bytes 6291456 | tf_op jit(solution)/shard_map/reshape | solution.py:156
  342.9 9.1 %reshape.506 = bf16[32,8,3,2048]{3,2,1,0:T(4,128)(2,1)} reshape(bf16[768,2048]{1,0:T(8,128)(2,1)} %convolution_convert_fusion) | data formatting | bytes 6291456 | tf_op jit(solution)/shard_map/reshape | solution.py:156
  352.0 7.2 %copy.107 = bf16[32,8,3,2048]{3,1,2,0:T(8,128)(2,1)} copy(bf16[32,8,3,2048]{3,2,1,0:T(4,128)(2,1)} %reshape.506) | data formatting | bytes 6291456 | tf_op jit(solution)/shard_map/reshape | solution.py:156
  359.3 5.6 all-to-all-start.3
  364.9 13.3 %fusion.9 = bf16[8,16,128,128]{3,2,1,0:T(8,128)(2,1)} fusion(f32[8,16,128]{2,1,0:T(8,128)S(1)} %copy-done.13, f32[8,16,128]{2,1,0:T(8,128)S(1)} %bitcast.175, f32[8,16]{1,0:T(8,128)S(1)} %get-tuple-element.34, f32[8,16,128]{2,1,0:T(8,128)S(1)} %copy-done.11, f32[8,16,128]{2,1,0:T(8,128)S(1)} %bitcast.172, f32[8,16]{1,0:T(8,128)S(1)} %get-tuple-element.35, ...), kind=kLoop, calls=%fused_computation.18 | loop fusion | flops 29360128 | bytes 8914944 | tf_op jit(solution)/shard_map/convert_element_type | solution.py:52
  381.3 10.9 %scatter_fusion = bf16[8,16,128,128]{3,2,1,0:T(8,128)(2,1)} fusion(bf16[8,16,128,128]{3,2,1,0:T(8,128)(2,1)} %broadcast.332.clone, s32[8]{0:T(128)S(1)} %compare_select_fusion.2, bf16[8,16,128,128]{3,2,1,0:T(8,128)(2,1)} %fusion.9), kind=kCustom, calls=%fused_computation.3 | custom fusion | bytes 12582944 | tf_op jit(solution)/shard_map/scatter | solution.py:68
  392.1 43.9 %all-to-all-done.3 = bf16[32,8,3,2048]{3,1,2,0:T(8,128)(2,1)} async-done(((bf16[32,8,3,2048]{3,1,2,0:T(8,128)(2,1)}), bf16[32,8,3,2048]{3,1,2,0:T(8,128)(2,1)}, u32[]{:S(2)}, u32[]{:S(2)}) %all-to-all-start.3) | async-done | bytes 3145760 | tf_op jit(solution)/shard_map/all_to_all | solution.py:160
  436.0 6.8 %all-to-all-start.6 = ((bf16[8,1,16,128,128]{4,3,2,1,0:T(8,128)(2,1)}), bf16[8,1,16,128,128]{4,3,2,1,0:T(8,128)(2,1)}, u32[]{:S(2)}, u32[]{:S(2)}) async-start(bf16[8,1,16,128,128]{4,3,2,1,0:T(8,128)(2,1)} %bitcast.132), calls=%async_computation.6 | async-start | bytes 8388608 | tf_op jit(solution)/shard_map/all_to_all | solution.py:110
  442.8 5.3 copy.108
  448.2 43.5 %all-to-all-done.6 = bf16[8,1,16,128,128]{4,3,2,1,0:T(8,128)(2,1)} async-done(((bf16[8,1,16,128,128]{4,3,2,1,0:T(8,128)(2,1)}), bf16[8,1,16,128,128]{4,3,2,1,0:T(8,128)(2,1)}, u32[]{:S(2)}, u32[]{:S(2)}) %all-to-all-start.6) | async-done | bytes 4194336 | tf_op jit(solution)/shard_map/all_to_all | solution.py:110
  491.7 5.2 all-to-all-start.4
  501.0 10.9 %scatter_fusion.1 = bf16[8,16,128,128]{3,2,1,0:T(8,128)(2,1)} fusion(bf16[8,16,128,128]{3,2,1,0:T(8,128)(2,1)} %broadcast.332, s32[8]{0:T(128)S(1)} %fusion.54, bf16[8,16,128,128]{3,2,1,0:T(8,128)(2,1)} %bitcast.77), kind=kCustom, calls=%fused_computation.4 | custom fusion | bytes 12582944 | tf_op jit(solution)/shard_map/scatter | solution.py:117
  511.9 22.7 %all-to-all-done.4 = bf16[32,8,3,2048]{3,0,2,1:T(8,128)(2,1)} async-done(((bf16[32,8,3,2048]{3,0,2,1:T(8,128)(2,1)}), bf16[32,8,3,2048]{3,0,2,1:T(8,128)(2,1)}, u32[]{:S(2)}, u32[]{:S(2)}) %all-to-all-start.4) | async-done | bytes 3145760 | tf_op jit(solution)/shard_map/all_to_all | solution.py:159
  534.5 6.5 %copy.109 = bf16[32,8,3,2048]{3,2,1,0:T(4,128)(2,1)} copy(bf16[32,8,3,2048]{3,0,2,1:T(8,128)(2,1)} %all-to-all-done.4) | data formatting | bytes 6291456 | tf_op jit(solution)/shard_map/all_to_all | solution.py:159
  541.1 8.8 %reshape.507 = bf16[768,2048]{1,0:T(8,128)(2,1)} reshape(bf16[32,8,3,2048]{3,2,1,0:T(4,128)(2,1)} %copy.109) | data formatting | bytes 6291456 | tf_op jit(solution)/shard_map/reshape | solution.py:166
  549.9 6.8 %gather_fusion = bf16[320,2048]{1,0:T(8,128)(2,1)S(1)} fusion(bf16[768,2048]{1,0:T(8,128)(2,1)} %reshape.507, s32[1024]{0:T(1024)} %pad_clamp_fusion), kind=kCustom, calls=%fused_computation | custom fusion | bytes 2622720 | tf_op jit(solution)/shard_map/gather | solution.py:166
  (169 shorter events, 57.7 us)
Async XLA Ops:
  7.2 329.3 %copy-start = (bf16[1,2048,512]{2,1,0:T(8,128)(2,1)S(1)}, bf16[1,2048,512]{2,1,0:T(8,128)(2,1)}, u32[]{:S(2)}) copy-start(bf16[1,2048,512]{2,1,0:T(8,128)(2,1)} %param.29) | copy-start | bytes 6291460
  7.2 142.5 %all-gather.2.cloned.1.call-start = ((), (), s32[]{:S(2)}) async-start(), calls=%async_computation.7 | async-start | bytes 1179648 | tf_op jit(solution)/shard_map/all_gather | solution.py:121
  9.0 15.1 %copy-start.1 = (bf16[8,16,128,128]{3,2,1,0:T(8,128)(2,1)S(1)}, bf16[8,16,128,128]{3,2,1,0:T(8,128)(2,1)}, u32[]{:S(2)}) copy-start(bf16[8,16,128,128]{3,2,1,0:T(8,128)(2,1)} %param.16) | copy-start | bytes 12582916
  14.3 82.4 %copy-start.14 = (f32[8,8,2,128]{3,2,1,0:T(2,128)}, f32[8,8,2,128]{3,2,1,0:T(2,128)S(1)}, u32[]{:S(2)}) copy-start(f32[8,8,2,128]{3,2,1,0:T(2,128)S(1)} %broadcast_in_dim.22) | copy-start | bytes 196612
  24.1 72.6 %copy-start.6 = (f32[8,16,128]{2,1,0:T(8,128)}, f32[8,16,128]{2,1,0:T(8,128)S(1)}, u32[]{:S(2)}) copy-start(f32[8,16,128]{2,1,0:T(8,128)S(1)} %subtract_multiply_fusion.3) | copy-start | bytes 196612
  32.6 64.1 %copy-start.16 = (f32[8,8,2,128]{3,2,1,0:T(2,128)}, f32[8,8,2,128]{3,2,1,0:T(2,128)S(1)}, u32[]{:S(2)}) copy-start(f32[8,8,2,128]{3,2,1,0:T(2,128)S(1)} %broadcast_in_dim.24) | copy-start | bytes 196612
  41.6 55.1 %copy-start.8 = (f32[8,16,128]{2,1,0:T(8,128)}, f32[8,16,128]{2,1,0:T(8,128)S(1)}, u32[]{:S(2)}) copy-start(f32[8,16,128]{2,1,0:T(8,128)S(1)} %subtract_multiply_fusion.2) | copy-start | bytes 196612
  53.4 43.3 %copy-start.18 = (f32[8,8,2,128]{3,2,1,0:T(2,128)}, f32[8,8,2,128]{3,2,1,0:T(2,128)S(1)}, u32[]{:S(2)}) copy-start(f32[8,8,2,128]{3,2,1,0:T(2,128)S(1)} %broadcast_in_dim.26) | copy-start | bytes 196612
  65.2 31.5 %copy-start.10 = (f32[8,16,128]{2,1,0:T(8,128)}, f32[8,16,128]{2,1,0:T(8,128)S(1)}, u32[]{:S(2)}) copy-start(f32[8,16,128]{2,1,0:T(8,128)S(1)} %subtract_multiply_fusion.1) | copy-start | bytes 196612
  80.9 15.8 %copy-start.20 = (f32[8,8,2,128]{3,2,1,0:T(2,128)}, f32[8,8,2,128]{3,2,1,0:T(2,128)S(1)}, u32[]{:S(2)}) copy-start(f32[8,8,2,128]{3,2,1,0:T(2,128)S(1)} %broadcast_in_dim.28) | copy-start | bytes 196612
  96.6 21.3 %copy-start.12 = (f32[8,16,128]{2,1,0:T(8,128)}, f32[8,16,128]{2,1,0:T(8,128)S(1)}, u32[]{:S(2)}) copy-start(f32[8,16,128]{2,1,0:T(8,128)S(1)} %subtract_multiply_fusion) | copy-start | bytes 196612
  96.7 21.3 %copy-start.5 = (bf16[8,4,2048]{2,1,0:T(4,128)(2,1)S(1)}, bf16[8,4,2048]{2,1,0:T(4,128)(2,1)}, u32[]{:S(2)}) copy-start(bf16[8,4,2048]{2,1,0:T(4,128)(2,1)} %param.20) | copy-start | bytes 393220
  96.8 21.5 %copy-start.25 = (f32[128]{0:T(128)S(1)}, f32[128]{0:T(128)}, u32[]{:S(2)}) copy-start(f32[128]{0:T(128)} %param.27) | copy-start | bytes 1540
  96.8 22.6 %copy-start.22 = (s32[8,4,10]{2,1,0:T(4,128)S(1)}, s32[8,4,10]{2,1,0:T(4,128)}, u32[]{:S(2)}) copy-start(s32[8,4,10]{2,1,0:T(4,128)} %param.24) | copy-start | bytes 3844
  118.2 37.9 %copy-start.4 = (bf16[8,4,2048]{2,1,0:T(4,128)(2,1)S(1)}, bf16[8,4,2048]{2,1,0:T(4,128)(2,1)}, u32[]{:S(2)}) copy-start(bf16[8,4,2048]{2,1,0:T(4,128)(2,1)} %param.23) | copy-start | bytes 393220
  152.3 9.0 %all-to-all-start = ((bf16[8,32,256]{2,1,0:T(8,128)(2,1)}), bf16[8,32,256]{2,1,0:T(8,128)(2,1)S(1)}, u32[]{:S(2)}, u32[]{:S(2)}) async-start(bf16[8,32,256]{2,1,0:T(8,128)(2,1)} %bitcast.64), calls=%async_computation | async-start | bytes 262144 | tf_op jit(solution)/shard_map/all_to_all | solution.py:125
  161.6 11.7 %copy-start.2 = (f32[8,4,2048]{2,1,0:T(4,128)}, f32[8,4,2048]{2,1,0:T(4,128)S(1)}, u32[]{:S(2)}) copy-start(f32[8,4,2048]{2,1,0:T(4,128)S(1)} %reshape.543) | copy-start | bytes 786436
  271.6 7.4 %copy-start.27 = (s32[8]{0:T(128)S(1)}, s32[8]{0:T(128)}, u32[]{:S(2)}) copy-start(s32[8]{0:T(128)} %param.31) | copy-start | bytes 100
  271.6 45.1 %all-to-all-start.2 = ((bf16[32,8,3,2048]{3,0,2,1:T(8,128)(2,1)}), bf16[32,8,3,2048]{3,0,2,1:T(8,128)(2,1)}, u32[]{:S(2)}, u32[]{:S(2)}) async-start(bf16[32,8,3,2048]{3,0,2,1:T(8,128)(2,1)} %copy.105), calls=%async_computation.2 | async-start | bytes 6291456 | tf_op jit(solution)/shard_map/all_to_all | solution.py:143
  316.7 42.6 %all-to-all-start.5 = ((s32[8,1,1]{2,1,0:T(1,128)}), s32[8,1,1]{2,1,0:T(1,128)S(1)}, u32[]{:S(2)}, u32[]{:S(2)}) async-start(s32[8,1,1]{2,1,0:T(1,128)} %copy.110), calls=%async_computation.5 | async-start | bytes 8192 | tf_op jit(solution)/shard_map/all_to_all | solution.py:113
  359.2 5.7 copy-start.9
  359.2 5.7 copy-start.11
  359.2 5.7 copy-start.13
  359.2 5.7 copy-start.15
  359.2 5.7 copy-start.17
  359.2 5.7 copy-start.19
  359.3 5.7 copy-start.21
  359.3 76.7 %all-to-all-start.3 = ((bf16[32,8,3,2048]{3,1,2,0:T(8,128)(2,1)}), bf16[32,8,3,2048]{3,1,2,0:T(8,128)(2,1)}, u32[]{:S(2)}, u32[]{:S(2)}) async-start(bf16[32,8,3,2048]{3,1,2,0:T(8,128)(2,1)} %copy.107), calls=%async_computation.3 | async-start | bytes 6291456 | tf_op jit(solution)/shard_map/all_to_all | solution.py:160
  436.0 55.7 %all-to-all-start.6 = ((bf16[8,1,16,128,128]{4,3,2,1,0:T(8,128)(2,1)}), bf16[8,1,16,128,128]{4,3,2,1,0:T(8,128)(2,1)}, u32[]{:S(2)}, u32[]{:S(2)}) async-start(bf16[8,1,16,128,128]{4,3,2,1,0:T(8,128)(2,1)} %bitcast.132), calls=%async_computation.6 | async-start | bytes 8388608 | tf_op jit(solution)/shard_map/all_to_all | solution.py:110
  448.1 48.7 %copy-start.23 = (f32[8,4,10]{2,1,0:T(4,128)S(1)}, f32[8,4,10]{2,1,0:T(4,128)}, u32[]{:S(2)}) copy-start(f32[8,4,10]{2,1,0:T(4,128)} %param.25) | copy-start | bytes 3844
  448.1 48.9 %copy-start.24 = (s32[320]{0:T(512)S(1)}, s32[320]{0:T(512)}, u32[]{:S(2)}) copy-start(s32[320]{0:T(512)} %fusion.52) | copy-start | bytes 3844
  491.7 42.9 %all-to-all-start.4 = ((bf16[32,8,3,2048]{3,0,2,1:T(8,128)(2,1)}), bf16[32,8,3,2048]{3,0,2,1:T(8,128)(2,1)}, u32[]{:S(2)}, u32[]{:S(2)}) async-start(bf16[32,8,3,2048]{3,0,2,1:T(8,128)(2,1)} %copy.108), calls=%async_computation.4 | async-start | bytes 6291456 | tf_op jit(solution)/shard_map/all_to_all | solution.py:159
  (3 other events, 13.1 us)
Sparse Core Ops, SparseCore 0:
  119.5 30.1 all-gather.1
where the time goes:
time: 577 us; the launch traced here: 571 us
  waiting for transfers between devices  180 us (31%)
  local copies, waits for them, and re-layouts  123 us (21%)
  matrix products  112 us (19%)
  blocking collectives  80.3 us (14%)
  starting transfers between devices  33.1 us (6%)
  other arithmetic  27.5 us (5%)
  between operations  15.4 us (3%)
    all_to_all x1, blocking collectives, shards(): lax.all_to_all(outgoing.reshape(dp_size, ep_size, capacity, model_width),...  80.3 us
    dot_general x4, matrix products, delta_block(): jnp.einsum('bhkv,bhk->bhv', memory_state, queries, precision=lax.Precisio...  56.5 us
    dot_general x4, matrix products, delta_block(): jnp.einsum('bhkv,bhk->bhv', memory_state, key_units, precision=lax.Precis...  45.9 us
    all_to_all x1, waiting for transfers between devices, shards(): lax.all_to_all(result, 'dp', split_axis=0, concat_axis=0, tiled=True)  43.9 us
    all_to_all x1, waiting for transfers between devices, shards(): lax.all_to_all(pack(fresh_states, buffer_index, ep_size), 'ep', split_axi...  43.5 us
    all_to_all x1, waiting for transfers between devices, shards(): lax.all_to_all(lax.all_to_all(outgoing.reshape(dp_size, ep_size, capacity...  36.2 us
    all_gather x1, waiting for transfers between devices, shards(): lax.all_gather(core_flat, 'ep', axis=0, tiled=True)  29.2 us
    all_to_all x1, waiting for transfers between devices, shards(): lax.all_to_all(lax.all_to_all(result, 'dp', split_axis=0, concat_axis=0,...  22.7 us
  transfers between devices with their start and end apart: 7, of which 6 were waited for; matrix products, arithmetic and copies ran while one was open for 16% of the time, Pallas kernels for 0%

commit v1 on v0

--- a/solution.py
+++ b/solution.py
@@ -3,7 +3,123 @@
 from jax import lax
 from jax.sharding import PartitionSpec as P
 
+import functools
+from jax.experimental import pallas as pl
+from jax.experimental.pallas import tpu as pltpu
+
 epsilon = 1e-06
+f32 = jnp.float32
+bf16 = jnp.bfloat16
+
+
+def split2(x):
+    hi = x.astype(bf16)
+    lo = (x - hi.astype(f32)).astype(bf16)
+    return hi, lo
+
+
+def recur_kernel(s_ref, kq_ref, v_ref, g_ref, dec_ref, beta_ref, gain_ref, so_ref, co_ref, n_ref, r_ref, u_ref):
+    heads = s_ref.shape[1]
+    width = s_ref.shape[-1]
+    steps = v_ref.shape[1]
+    span = 2 * steps
+    kq = kq_ref[0].astype(f32)
+    kq = kq * lax.rsqrt(jnp.sum(kq * kq, -1, keepdims=True) + epsilon)
+    row = lax.broadcasted_iota(jnp.int32, kq.shape, 0)
+    kq = jnp.where(row % span >= steps, kq * width ** (-0.5), kq)
+    n_ref[...] = kq
+    for h in range(heads):
+        p = n_ref[pl.ds(h * span, span), :]
+        hi = p.astype(bf16).astype(f32)
+        rest = p - hi
+        mid = rest.astype(bf16).astype(f32)
+        lo = rest - mid
+        lhs = jnp.concatenate([hi, mid, lo], axis=0).astype(bf16)
+        res = jnp.dot(lhs, s_ref[0, h], preferred_element_type=f32)
+        r_ref[pl.ds(h * span, span), :] = (res[0:span] + res[span:2 * span]) + res[2 * span:3 * span]
+    decay = jax.nn.sigmoid(dec_ref[0])
+    strength = jax.nn.sigmoid(beta_ref[0])
+    gain = gain_ref[...]
+    keys = [n_ref[pl.ds(t, heads, stride=span), :] for t in range(steps)]
+    queries = [n_ref[pl.ds(steps + t, heads, stride=span), :] for t in range(steps)]
+    u_ref[...] = jnp.zeros(u_ref.shape, f32)
+    updates = []
+    carried = []
+    total = None
+    for t in range(steps):
+        a_t = decay[:, t:t + 1]
+        b_t = strength[:, t:t + 1]
+        total = a_t if t == 0 else total * a_t
+        carried = [c * a_t for c in carried]
+        memory = total * r_ref[pl.ds(t, heads, stride=span), :]
+        for j in range(t):
+            kk = jnp.sum(keys[j] * keys[t], -1, keepdims=True)
+            memory = memory + (carried[j] * kk) * updates[j]
+        values = v_ref[0, t].astype(f32)
+        update = (values - memory) * b_t
+        updates.append(update)
+        carried.append(jnp.ones_like(a_t))
+        reading = total * r_ref[pl.ds(steps + t, heads, stride=span), :]
+        for j in range(t + 1):
+            qk = jnp.sum(keys[j] * queries[t], -1, keepdims=True)
+            coef = qk if j == t else carried[j] * qk
+            reading = reading + coef * updates[j]
+        scaled = reading * lax.rsqrt(jnp.mean(reading * reading, -1, keepdims=True) + epsilon)
+        gate_vals = g_ref[0, t].astype(f32)
+        co_ref[0, t] = (scaled * gain * (gate_vals * jax.nn.sigmoid(gate_vals))).astype(co_ref.dtype)
+    for j in range(steps):
+        u_ref[pl.ds(j, heads, stride=span), :] = carried[j] * updates[j]
+    for h in range(heads):
+        kt = n_ref[pl.ds(h * span, span), :].T
+        w = u_ref[pl.ds(h * span, span), :]
+        k_hi, k_lo = split2(kt)
+        w_hi, w_lo = split2(w)
+        delta = (
+            jnp.dot(k_hi, w_hi, preferred_element_type=f32)
+            + jnp.dot(k_hi, w_lo, preferred_element_type=f32)
+            + jnp.dot(k_lo, w_hi, preferred_element_type=f32)
+        )
+        so_ref[0, h] = (total[h:h + 1, :] * s_ref[0, h].astype(f32) + delta).astype(so_ref.dtype)
+
+
+def recurrence(states, query_rows, key_rows, value_rows, gate_rows, beta_logit, decay_logit, core_gain):
+    batch, heads, width, _ = states.shape
+    steps = query_rows.shape[1]
+    key_heads = query_rows.shape[-1] // width
+    repeats = heads // key_heads
+    span = 2 * steps
+    kq = jnp.concatenate(
+        [key_rows.reshape(batch, steps, key_heads, width), query_rows.reshape(batch, steps, key_heads, width)], axis=1
+    )
+    kq = jnp.repeat(kq.transpose(0, 2, 1, 3), repeats, axis=1).reshape(batch, heads * span, width)
+    values = value_rows.reshape(batch, steps, heads, width)
+    gates = gate_rows.reshape(batch, steps, heads, width)
+    decay = decay_logit.astype(f32).transpose(0, 2, 1)
+    beta = beta_logit.astype(f32).transpose(0, 2, 1)
+    gain = core_gain.reshape(1, width)
+    state_spec = pl.BlockSpec((1, heads, width, width), lambda i: (i, 0, 0, 0))
+    row_spec = pl.BlockSpec((1, steps, heads, width), lambda i: (i, 0, 0, 0))
+    coef_spec = pl.BlockSpec((1, heads, steps), lambda i: (i, 0, 0))
+    fresh, core = pl.pallas_call(
+        recur_kernel,
+        grid=(batch,),
+        in_specs=[
+            state_spec,
+            pl.BlockSpec((1, heads * span, width), lambda i: (i, 0, 0)),
+            row_spec,
+            row_spec,
+            coef_spec,
+            coef_spec,
+            pl.BlockSpec((1, width), lambda i: (0, 0)),
+        ],
+        out_specs=[state_spec, row_spec],
+        out_shape=[
+            jax.ShapeDtypeStruct(states.shape, bf16),
+            jax.ShapeDtypeStruct((batch, steps, heads, width), bf16),
+        ],
+        scratch_shapes=[pltpu.VMEM((heads * span, width), f32)] * 3,
+    )(states, kq, values, gates, decay, beta, gain)
+    return fresh, core.reshape(batch, steps, heads * width)
 
 
 def unit_rows(values):
@@ -103,7 +219,7 @@
     lane_rank = jnp.sum(earlier.astype(jnp.int32), axis=1)
     lane_cap = req_count // ep_size
     buffer_index = target * lane_cap + lane_rank
-    fresh_states, core_out = delta_block(
+    fresh_states, core_out = recurrence(
         states, query_rows, key_rows, value_rows, gate_rows, beta_logit, decay_logit, core_gain
     )
     received = (

time: 577 us -> 470 us (0.81)
  matrix products: 112 us -> 7.4 us
  other arithmetic: 27.5 us -> 12.6 us
  Pallas kernels: 0 us -> 12.3 us
  waiting for transfers between devices: 180 us -> 190 us
    dot_general x8 -> x0, matrix products: 102 us -> none  [the longest x4 56.5 us: delta_block(): jnp.einsum('bhkv,bhk->bhv', memory_state, queries, precision=lax.Precisio...]
    convert_element_type x6 -> x0, other arithmetic: 17.4 us -> none  [the longest x1 13.3 us: delta_block(): return (memory_state.astype(jnp.bfloat16), jnp.stack(outputs, axis=1))]
    all_to_all x1, waiting for transfers between devices: 43.9 us -> 57.1 us  [shards(): lax.all_to_all(result, 'dp', split_axis=0, concat_axis=0, tiled=True)]
    pallas_call x0 -> x1, Pallas kernels: none -> 12.3 us  [recurrence(): pl.pallas_call(recur_kernel, grid=(batch,), in_specs=[state_spec, pl.Bloc...]
where the time goes in v1:
time: 470 us; the launch traced here: 467 us
  waiting for transfers between devices  190 us (40%)
  local copies, waits for them, and re-layouts  119 us (25%)
  blocking collectives  80.3 us (17%)
  starting transfers between devices  31.3 us (7%)
  between operations  14.3 us (3%)
  other arithmetic  12.6 us (3%)
  Pallas kernels  12.3 us (3%)
  matrix products  7.4 us (2%)
    all_to_all x1, blocking collectives, shards(): lax.all_to_all(outgoing.reshape(dp_size, ep_size, capacity, model_width),...  80.3 us
    all_to_all x1, waiting for transfers between devices, shards(): lax.all_to_all(result, 'dp', split_axis=0, concat_axis=0, tiled=True)  57.1 us
    all_to_all x1, waiting for transfers between devices, shards(): lax.all_to_all(pack(fresh_states, buffer_index, ep_size), 'ep', split_axi...  45.4 us
    all_to_all x1, waiting for transfers between devices, shards(): lax.all_to_all(lax.all_to_all(outgoing.reshape(dp_size, ep_size, capacity...  36.2 us
    all_gather x1, waiting for transfers between devices, shards(): lax.all_gather(core_flat, 'ep', axis=0, tiled=True)  29.2 us
    all_to_all x1, waiting for transfers between devices, shards(): lax.all_to_all(lax.all_to_all(result, 'dp', split_axis=0, concat_axis=0,...  16.9 us
    reshape x2, local copies, waits for them, and re-layouts, shards(): outgoing.reshape(dp_size, ep_size, capacity, model_width)  14.6 us
    pallas_call x1, Pallas kernels, recurrence(): pl.pallas_call(recur_kernel, grid=(batch,), in_specs=[state_spec, pl.Bloc...  12.3 us
  transfers between devices with their start and end apart: 7, of which 6 were waited for; matrix products, arithmetic and copies ran while one was open for 16% of the time, Pallas kernels for 0%

profile of v1, /device:TPU:1, one launch (start us, length us, event | category | flops | bytes accessed | tf_op | source)
XLA Modules:
  0.0 467.1 jit_solution(9632745394273123708)
XLA Ops:
  16.1 12.3 %shard_map.167 = (bf16[8,16,128,128]{3,2,1,0:T(8,128)(2,1)}, bf16[8,4,16,128]{3,2,1,0:T(8,128)(2,1)}) custom-call(bf16[8,16,128,128]{3,2,1,0:T(8,128)(2,1)} %s_ref.1, bf16[8,128,128]{2,1,0:T(8,128)(2,1)} %bitcast.50, bf16[8,4,16,128]{3,2,1,0:T(8,128)(2,1)} %reshape.185.v_ref, bf16[8,4,16,128]{3,2,1,0:T(8,128)(2,1)} %reshape.186.g_ref, f32[8,16,4]{2,1,0:T(8,128)} %bitcast.53, ...), custom_call_target="tpu_custom_call" | custom-call | tf_op jit(solution)/shard_map/pallas_call | solution.py:103
  31.0 29.2 %all-gather.2.cloned.1.call-done = bf16[256,2048]{1,0:T(8,128)(2,1)} async-done(((bf16[32,2048]{1,0:T(8,128)(2,1)}), bf16[256,2048]{1,0:T(8,128)(2,1)}) %all-gather.2.cloned.1.call-update) | async-done | bytes 1048592 | tf_op jit(solution)/shard_map/all_gather | solution.py:237
  62.9 3.5 all-to-all-start
  66.6 5.1 %all-to-all-done = bf16[8,32,256]{2,1,0:T(8,128)(2,1)S(1)} async-done(((bf16[8,32,256]{2,1,0:T(8,128)(2,1)}), bf16[8,32,256]{2,1,0:T(8,128)(2,1)S(1)}, u32[]{:S(2)}, u32[]{:S(2)}) %all-to-all-start) | async-done | bytes 131104 | tf_op jit(solution)/shard_map/all_to_all | solution.py:241
  74.1 3.6 reshape.215
  77.7 5.4 %scatter_custom_fusion = bf16[768,2048]{1,0:T(8,128)(2,1)} fusion(s32[320]{0:T(512)S(1)} %fusion.14, bf16[320,2048]{1,0:T(8,128)(2,1)} %reshape.215, bf16[]{:T(256)} %constant.48.clone.1), kind=kCustom, calls=%fused_computation.9 | custom fusion | bytes 3146240 | tf_op jit(solution)/shard_map/scatter | solution.py:257
  83.1 9.1 %reshape.191 = bf16[32,8,3,2048]{3,2,1,0:T(4,128)(2,1)} reshape(bf16[768,2048]{1,0:T(8,128)(2,1)} %scatter_custom_fusion) | data formatting | bytes 6291456 | tf_op jit(solution)/shard_map/reshape | solution.py:261
  92.2 5.5 %copy.81 = bf16[32,8,3,2048]{3,1,2,0:T(8,128)(2,1)S(1)} copy(bf16[32,8,3,2048]{3,2,1,0:T(4,128)(2,1)} %reshape.191) | data formatting | bytes 6291456 | tf_op jit(solution)/shard_map/reshape | solution.py:261
  97.7 80.3 %all_to_all.50 = bf16[32,8,3,2048]{3,1,2,0:T(8,128)(2,1)S(1)} all-to-all(bf16[32,8,3,2048]{3,1,2,0:T(8,128)(2,1)S(1)} %copy.81), channel_id=1, replica_groups=mesh['dp'=32,'ep'=8] {'dp'}, dimensions={0} | all-to-all | bytes 6291456 | tf_op jit(solution)/shard_map/all_to_all | solution.py:260
  178.1 3.4 copy.82
  181.4 7.4 %all-to-all-start.2 = ((bf16[32,8,3,2048]{3,0,2,1:T(8,128)(2,1)}), bf16[32,8,3,2048]{3,0,2,1:T(8,128)(2,1)}, u32[]{:S(2)}, u32[]{:S(2)}) async-start(bf16[32,8,3,2048]{3,0,2,1:T(8,128)(2,1)} %copy.82), calls=%async_computation.2 | async-start | bytes 6291456 | tf_op jit(solution)/shard_map/all_to_all | solution.py:259
  190.4 36.2 %all-to-all-done.2 = bf16[32,8,3,2048]{3,0,2,1:T(8,128)(2,1)} async-done(((bf16[32,8,3,2048]{3,0,2,1:T(8,128)(2,1)}), bf16[32,8,3,2048]{3,0,2,1:T(8,128)(2,1)}, u32[]{:S(2)}, u32[]{:S(2)}) %all-to-all-start.2) | async-done | bytes 3145760 | tf_op jit(solution)/shard_map/all_to_all | solution.py:259
  226.6 4.1 all-to-all-start.5
  230.7 6.5 %copy.83 = bf16[32,8,3,2048]{3,2,1,0:T(4,128)(2,1)} copy(bf16[32,8,3,2048]{3,0,2,1:T(8,128)(2,1)} %all-to-all-done.2) | data formatting | bytes 6291456 | tf_op jit(solution)/shard_map/all_to_all | solution.py:259
  237.2 8.8 %reshape.192 = bf16[768,2048]{1,0:T(8,128)(2,1)} reshape(bf16[32,8,3,2048]{3,2,1,0:T(4,128)(2,1)} %copy.83) | data formatting | bytes 6291456 | tf_op jit(solution)/shard_map/reshape | solution.py:272
  246.0 3.8 fusion
  250.8 4.4 reshape.193
  255.2 7.3 %copy.84 = bf16[32,8,3,2048]{3,1,2,0:T(8,128)(2,1)} copy(bf16[32,8,3,2048]{3,2,1,0:T(4,128)(2,1)} %reshape.193) | data formatting | bytes 6291456 | tf_op jit(solution)/shard_map/reshape | solution.py:272
  263.1 5.3 %all-to-all-start.3 = ((bf16[32,8,3,2048]{3,1,2,0:T(8,128)(2,1)}), bf16[32,8,3,2048]{3,1,2,0:T(8,128)(2,1)S(1)}, u32[]{:S(2)}, u32[]{:S(2)}) async-start(bf16[32,8,3,2048]{3,1,2,0:T(8,128)(2,1)} %copy.84), calls=%async_computation.3 | async-start | bytes 6291456 | tf_op jit(solution)/shard_map/all_to_all | solution.py:276
  271.4 11.0 %scatter_fusion = bf16[8,16,128,128]{3,2,1,0:T(8,128)(2,1)} fusion(bf16[8,16,128,128]{3,2,1,0:T(8,128)(2,1)} %broadcast.129.clone, s32[8]{0:T(128)S(1)} %compare_select_fusion.2, bf16[8,16,128,128]{3,2,1,0:T(8,128)(2,1)} %get-tuple-element.5), kind=kCustom, calls=%fused_computation.3 | custom fusion | bytes 12582944 | tf_op jit(solution)/shard_map/scatter | solution.py:184
  282.4 57.1 %all-to-all-done.3 = bf16[32,8,3,2048]{3,1,2,0:T(8,128)(2,1)S(1)} async-done(((bf16[32,8,3,2048]{3,1,2,0:T(8,128)(2,1)}), bf16[32,8,3,2048]{3,1,2,0:T(8,128)(2,1)S(1)}, u32[]{:S(2)}, u32[]{:S(2)}) %all-to-all-start.3) | async-done | bytes 3145760 | tf_op jit(solution)/shard_map/all_to_all | solution.py:276
  339.5 6.5 %all-to-all-start.6 = ((bf16[8,1,16,128,128]{4,3,2,1,0:T(8,128)(2,1)}), bf16[8,1,16,128,128]{4,3,2,1,0:T(8,128)(2,1)}, u32[]{:S(2)}, u32[]{:S(2)}) async-start(bf16[8,1,16,128,128]{4,3,2,1,0:T(8,128)(2,1)} %bitcast.47), calls=%async_computation.6 | async-start | bytes 8388608 | tf_op jit(solution)/shard_map/all_to_all | solution.py:226
  346.0 3.5 copy.85
  349.5 45.4 %all-to-all-done.6 = bf16[8,1,16,128,128]{4,3,2,1,0:T(8,128)(2,1)} async-done(((bf16[8,1,16,128,128]{4,3,2,1,0:T(8,128)(2,1)}), bf16[8,1,16,128,128]{4,3,2,1,0:T(8,128)(2,1)}, u32[]{:S(2)}, u32[]{:S(2)}) %all-to-all-start.6) | async-done | bytes 4194336 | tf_op jit(solution)/shard_map/all_to_all | solution.py:226
  394.9 4.4 all-to-all-start.4
  409.1 11.0 %scatter_fusion.1 = bf16[8,16,128,128]{3,2,1,0:T(8,128)(2,1)} fusion(bf16[8,16,128,128]{3,2,1,0:T(8,128)(2,1)} %broadcast.129, s32[8]{0:T(128)} %fusion.16, bf16[8,16,128,128]{3,2,1,0:T(8,128)(2,1)} %bitcast.18), kind=kCustom, calls=%fused_computation.4 | custom fusion | bytes 12582944 | tf_op jit(solution)/shard_map/scatter | solution.py:233
  420.0 16.9 %all-to-all-done.4 = bf16[32,8,3,2048]{3,0,2,1:T(8,128)(2,1)S(1)} async-done(((bf16[32,8,3,2048]{3,0,2,1:T(8,128)(2,1)}), bf16[32,8,3,2048]{3,0,2,1:T(8,128)(2,1)S(1)}, u32[]{:S(2)}, u32[]{:S(2)}) %all-to-all-start.4) | async-done | bytes 3145760 | tf_op jit(solution)/shard_map/all_to_all | solution.py:275
  437.0 4.6 copy.86
  441.6 7.5 %reshape.194 = bf16[768,2048]{1,0:T(8,128)(2,1)S(1)} reshape(bf16[32,8,3,2048]{3,2,1,0:T(4,128)(2,1)} %copy.86) | data formatting | bytes 6291456 | tf_op jit(solution)/shard_map/reshape | solution.py:282
  449.1 3.2 gather_fusion
  452.3 3.6 reshape.202
  455.9 3.6 multiply_reduce_fusion
  (75 shorter events, 33.2 us)
Async XLA Ops:
  7.2 238.8 %copy-start = (bf16[1,2048,512]{2,1,0:T(8,128)(2,1)S(1)}, bf16[1,2048,512]{2,1,0:T(8,128)(2,1)}, u32[]{:S(2)}) copy-start(bf16[1,2048,512]{2,1,0:T(8,128)(2,1)} %param.29) | copy-start | bytes 6291460
  7.2 53.1 %all-gather.2.cloned.1.call-start = ((), (), s32[]{:S(2)}) async-start(), calls=%async_computation.7 | async-start | bytes 1179648 | tf_op jit(solution)/shard_map/all_gather | solution.py:237
  12.1 17.9 %copy-start.3 = (s32[8,4,10]{2,1,0:T(4,128)S(1)}, s32[8,4,10]{2,1,0:T(4,128)}, u32[]{:S(2)}) copy-start(s32[8,4,10]{2,1,0:T(4,128)} %param.24) | copy-start | bytes 3844
  30.2 36.3 %copy-start.2 = (bf16[8,4,2048]{2,1,0:T(4,128)(2,1)S(1)}, bf16[8,4,2048]{2,1,0:T(4,128)(2,1)}, u32[]{:S(2)}) copy-start(bf16[8,4,2048]{2,1,0:T(4,128)(2,1)} %param.23) | copy-start | bytes 393220
  30.8 41.6 %copy-start.6 = (f32[2048]{0:T(1024)S(1)}, f32[2048]{0:T(1024)}, u32[]{:S(2)}) copy-start(f32[2048]{0:T(1024)} %param.28) | copy-start | bytes 24580
  62.9 8.8 %all-to-all-start = ((bf16[8,32,256]{2,1,0:T(8,128)(2,1)}), bf16[8,32,256]{2,1,0:T(8,128)(2,1)S(1)}, u32[]{:S(2)}, u32[]{:S(2)}) async-start(bf16[8,32,256]{2,1,0:T(8,128)(2,1)} %bitcast.5), calls=%async_computation | async-start | bytes 262144 | tf_op jit(solution)/shard_map/all_to_all | solution.py:241
  66.6 11.1 %copy-start.7 = (s32[320]{0:T(512)}, s32[320]{0:T(512)S(1)}, u32[]{:S(2)}) copy-start(s32[320]{0:T(512)S(1)} %fusion.14) | copy-start | bytes 3844
  181.4 7.4 %copy-start.9 = (s32[8]{0:T(128)S(1)}, s32[8]{0:T(128)}, u32[]{:S(2)}) copy-start(s32[8]{0:T(128)} %param.31) | copy-start | bytes 100
  181.4 45.1 %all-to-all-start.2 = ((bf16[32,8,3,2048]{3,0,2,1:T(8,128)(2,1)}), bf16[32,8,3,2048]{3,0,2,1:T(8,128)(2,1)}, u32[]{:S(2)}, u32[]{:S(2)}) async-start(bf16[32,8,3,2048]{3,0,2,1:T(8,128)(2,1)} %copy.82), calls=%async_computation.2 | async-start | bytes 6291456 | tf_op jit(solution)/shard_map/all_to_all | solution.py:259
  226.6 35.9 %all-to-all-start.5 = ((s32[8,1,1]{2,1,0:T(1,128)}), s32[8,1,1]{2,1,0:T(1,128)S(1)}, u32[]{:S(2)}, u32[]{:S(2)}) async-start(s32[8,1,1]{2,1,0:T(1,128)} %copy.87), calls=%async_computation.5 | async-start | bytes 8192 | tf_op jit(solution)/shard_map/all_to_all | solution.py:229
  246.0 3.8 copy-start.8
  262.5 0.6 copy-start.5
  263.1 76.5 %all-to-all-start.3 = ((bf16[32,8,3,2048]{3,1,2,0:T(8,128)(2,1)}), bf16[32,8,3,2048]{3,1,2,0:T(8,128)(2,1)S(1)}, u32[]{:S(2)}, u32[]{:S(2)}) async-start(bf16[32,8,3,2048]{3,1,2,0:T(8,128)(2,1)} %copy.84), calls=%async_computation.3 | async-start | bytes 6291456 | tf_op jit(solution)/shard_map/all_to_all | solution.py:276
  339.5 55.4 %all-to-all-start.6 = ((bf16[8,1,16,128,128]{4,3,2,1,0:T(8,128)(2,1)}), bf16[8,1,16,128,128]{4,3,2,1,0:T(8,128)(2,1)}, u32[]{:S(2)}, u32[]{:S(2)}) async-start(bf16[8,1,16,128,128]{4,3,2,1,0:T(8,128)(2,1)} %bitcast.47), calls=%async_computation.6 | async-start | bytes 8388608 | tf_op jit(solution)/shard_map/all_to_all | solution.py:226
  349.5 49.9 %copy-start.4 = (f32[8,4,10]{2,1,0:T(4,128)S(1)}, f32[8,4,10]{2,1,0:T(4,128)}, u32[]{:S(2)}) copy-start(f32[8,4,10]{2,1,0:T(4,128)} %param.25) | copy-start | bytes 3844
  394.9 42.0 %all-to-all-start.4 = ((bf16[32,8,3,2048]{3,0,2,1:T(8,128)(2,1)}), bf16[32,8,3,2048]{3,0,2,1:T(8,128)(2,1)S(1)}, u32[]{:S(2)}, u32[]{:S(2)}) async-start(bf16[32,8,3,2048]{3,0,2,1:T(8,128)(2,1)} %copy.85), calls=%async_computation.4 | async-start | bytes 6291456 | tf_op jit(solution)/shard_map/all_to_all | solution.py:275
  452.3 8.0 %copy-start.1 = (bf16[1,2048,512]{2,1,0:T(8,128)(2,1)S(1)}, bf16[1,2048,512]{2,1,0:T(8,128)(2,1)}, u32[]{:S(2)}) copy-start(bf16[1,2048,512]{2,1,0:T(8,128)(2,1)} %param.29) | copy-start | bytes 6291460
Sparse Core Ops, SparseCore 0:
  30.1 30.1 all-gather.1

commit v2 on v1

--- a/solution.py
+++ b/solution.py
@@ -256,29 +256,9 @@
         .at[slot_index]
         .set(jnp.repeat(normed, top_count, axis=0))
     )
-    arrived = lax.all_to_all(
-        lax.all_to_all(
-            outgoing.reshape(dp_size, ep_size, capacity, model_width),
-            "dp",
-            split_axis=0,
-            concat_axis=0,
-            tiled=True,
-        ),
-        "ep",
-        split_axis=1,
-        concat_axis=1,
-        tiled=True,
-    )
-    result = expert_apply(arrived.reshape(-1, model_width), gate_up[0], down_weight[0]).reshape(
-        dp_size, ep_size, capacity, model_width
-    )
-    returned = lax.all_to_all(
-        lax.all_to_all(result, "dp", split_axis=0, concat_axis=0, tiled=True),
-        "ep",
-        split_axis=1,
-        concat_axis=1,
-        tiled=True,
-    )
+    arrived = lax.all_to_all(outgoing, ("dp", "ep"), 0, 0, tiled=True)
+    result = expert_apply(arrived, gate_up[0], down_weight[0])
+    returned = lax.all_to_all(result, ("dp", "ep"), 0, 0, tiled=True)
     routed = returned.reshape(experts * capacity, model_width)[slot_index]
     weights = route_prob.reshape(token_count, top_count)
     weights = weights / jnp.sum(weights, -1, keepdims=True)

time: 470 us -> 394 us (0.84)
  blocking collectives: 80.3 us -> 0 us
  waiting for transfers between devices: 190 us -> 228 us
  local copies, waits for them, and re-layouts: 119 us -> 87 us
    all_to_all x1 -> x0, blocking collectives: 80.3 us -> none  [shards(): lax.all_to_all(outgoing.reshape(dp_size, ep_size, capacity, model_width),...]
    all_to_all x3 -> x2, waiting for transfers between devices: 110 us -> 164 us  [the longest x1 82.6 us: shards(): arrived = lax.all_to_all(outgoing, ('dp', 'ep'), 0, 0, tiled=True)]
    reshape x6 -> x0, local copies, waits for them, and re-layouts: 42.6 us -> none  [the longest x2 14.6 us: shards(): outgoing.reshape(dp_size, ep_size, capacity, model_width)]
    all_to_all x1, waiting for transfers between devices: 45.4 us -> 30.9 us  [shards(): lax.all_to_all(pack(fresh_states, buffer_index, ep_size), 'ep', split_axi...]
    all_to_all x4, local copies, waits for them, and re-layouts: 18 us -> 29.9 us  [the longest x2 17.9 us: shards(): arrived = lax.all_to_all(outgoing, ('dp', 'ep'), 0, 0, tiled=True)]
    all_to_all x3 -> x2, starting transfers between devices: 17.2 us -> 22.3 us  [the longest x1 14 us: shards(): arrived = lax.all_to_all(outgoing, ('dp', 'ep'), 0, 0, tiled=True)]
  transfers between devices with their start and end apart: 7 -> 6, of which waited for: 6 -> 5; matrix products, arithmetic and copies ran while one was open for 16% -> 12% of each run, Pallas kernels for 0% -> 0%
where the time goes in v2:
time: 394 us; the launch traced here: 393 us
  waiting for transfers between devices  228 us (58%)
  local copies, waits for them, and re-layouts  87 us (22%)
  starting transfers between devices  35.5 us (9%)
  between operations  14.3 us (4%)
  Pallas kernels  12.3 us (3%)
  other arithmetic  8.07 us (2%)
  matrix products  7.41 us (2%)
    all_to_all x1, waiting for transfers between devices, shards(): arrived = lax.all_to_all(outgoing, ('dp', 'ep'), 0, 0, tiled=True)  82.6 us
    all_to_all x1, waiting for transfers between devices, shards(): returned = lax.all_to_all(result, ('dp', 'ep'), 0, 0, tiled=True)  81.6 us
    all_to_all x1, waiting for transfers between devices, shards(): lax.all_to_all(pack(fresh_states, buffer_index, ep_size), 'ep', split_axi...  30.9 us
    all_gather x1, waiting for transfers between devices, shards(): lax.all_gather(core_flat, 'ep', axis=0, tiled=True)  29 us
    all_to_all x2, local copies, waits for them, and re-layouts, shards(): arrived = lax.all_to_all(outgoing, ('dp', 'ep'), 0, 0, tiled=True)  17.9 us
    all_to_all x1, starting transfers between devices, shards(): arrived = lax.all_to_all(outgoing, ('dp', 'ep'), 0, 0, tiled=True)  14 us
    pallas_call x1, Pallas kernels, recurrence(): pl.pallas_call(recur_kernel, grid=(batch,), in_specs=[state_spec, pl.Bloc...  12.3 us
    all_to_all x2, local copies, waits for them, and re-layouts, shards(): returned = lax.all_to_all(result, ('dp', 'ep'), 0, 0, tiled=True)  12 us
  transfers between devices with their start and end apart: 6, of which 5 were waited for; matrix products, arithmetic and copies ran while one was open for 12% of the time, Pallas kernels for 0%

profile of v2, /device:TPU:1, one launch (start us, length us, event | category | flops | bytes accessed | tf_op | source)
XLA Modules:
  0.0 392.5 jit_solution(5943366447360605381)
XLA Ops:
  7.2 1.0 reshape.175
  9.2 1.6 reshape.177.v_ref
  10.8 1.6 reshape.178.g_ref
  16.1 12.3 %shard_map.167 = (bf16[8,16,128,128]{3,2,1,0:T(8,128)(2,1)}, bf16[8,4,16,128]{3,2,1,0:T(8,128)(2,1)}) custom-call(bf16[8,16,128,128]{3,2,1,0:T(8,128)(2,1)} %s_ref.1, bf16[8,128,128]{2,1,0:T(8,128)(2,1)} %bitcast.46, bf16[8,4,16,128]{3,2,1,0:T(8,128)(2,1)} %reshape.177.v_ref, bf16[8,4,16,128]{3,2,1,0:T(8,128)(2,1)} %reshape.178.g_ref, f32[8,16,4]{2,1,0:T(8,128)} %bitcast.49, ...), custom_call_target="tpu_custom_call" | custom-call | tf_op jit(solution)/shard_map/pallas_call | solution.py:103
  28.4 1.6 copy.72
  31.3 29.0 %all-gather.2.cloned.1.call-done = bf16[256,2048]{1,0:T(8,128)(2,1)} async-done(((bf16[32,2048]{1,0:T(8,128)(2,1)}), bf16[256,2048]{1,0:T(8,128)(2,1)}) %all-gather.2.cloned.1.call-update) | async-done | bytes 1048592 | tf_op jit(solution)/shard_map/all_gather | solution.py:237
  60.3 2.6 convolution_convert_fusion.1
  62.9 3.5 all-to-all-start
  67.9 3.8 all-to-all-done
  71.7 4.1 %all-to-all-start.3 = ((s32[8,1,1]{2,1,0:T(1,128)}), s32[8,1,1]{2,1,0:T(1,128)S(1)}, u32[]{:S(2)}, u32[]{:S(2)}) async-start(s32[8,1,1]{2,1,0:T(1,128)} %copy.63), calls=%async_computation.3 | async-start | bytes 8192 | tf_op jit(solution)/shard_map/all_to_all | solution.py:229
  76.6 1.6 broadcast_in_dim.10
  78.2 3.6 reshape.203
  81.8 5.4 %scatter_custom_fusion = bf16[768,2048]{1,0:T(8,128)(2,1)} fusion(s32[320]{0:T(512)S(1)} %fusion.14, bf16[320,2048]{1,0:T(8,128)(2,1)} %reshape.203, bf16[]{:T(256)} %constant.48.clone.1), kind=kCustom, calls=%fused_computation.9 | custom fusion | bytes 3146240 | tf_op jit(solution)/shard_map/scatter | solution.py:257
  87.2 9.1 %all_to_all.39 = bf16[256,3,2048]{2,1,0:T(4,128)(2,1)} reshape(bf16[768,2048]{1,0:T(8,128)(2,1)} %scatter_custom_fusion) | data formatting | bytes 6291456 | tf_op jit(solution)/shard_map/all_to_all | solution.py:259
  96.9 14.0 %all-to-all-start.1 = ((bf16[256,3,2048]{2,1,0:T(4,128)(2,1)}), bf16[256,3,2048]{2,1,0:T(4,128)(2,1)}, u32[]{:S(2)}, u32[]{:S(2)}) async-start(bf16[256,3,2048]{2,1,0:T(4,128)(2,1)} %all_to_all.39), calls=%async_computation.1 | async-start | bytes 8388608 | tf_op jit(solution)/shard_map/all_to_all | solution.py:259
  111.0 3.0 broadcast.129.clone
  114.0 11.0 %scatter_fusion = bf16[8,16,128,128]{3,2,1,0:T(8,128)(2,1)} fusion(bf16[8,16,128,128]{3,2,1,0:T(8,128)(2,1)} %broadcast.129.clone, s32[8]{0:T(128)S(1)} %copy-done.9, bf16[8,16,128,128]{3,2,1,0:T(8,128)(2,1)} %get-tuple-element.5), kind=kCustom, calls=%fused_computation.3 | custom fusion | bytes 12582944 | tf_op jit(solution)/shard_map/scatter | solution.py:184
  125.0 82.6 %all-to-all-done.1 = bf16[256,3,2048]{2,1,0:T(4,128)(2,1)} async-done(((bf16[256,3,2048]{2,1,0:T(4,128)(2,1)}), bf16[256,3,2048]{2,1,0:T(4,128)(2,1)}, u32[]{:S(2)}, u32[]{:S(2)}) %all-to-all-start.1) | async-done | bytes 3145760 | tf_op jit(solution)/shard_map/all_to_all | solution.py:259
  207.6 5.5 %all-to-all-start.4 = ((bf16[8,1,16,128,128]{4,3,2,1,0:T(8,128)(2,1)}), bf16[8,1,16,128,128]{4,3,2,1,0:T(8,128)(2,1)}, u32[]{:S(2)}, u32[]{:S(2)}) async-start(bf16[8,1,16,128,128]{4,3,2,1,0:T(8,128)(2,1)} %bitcast.43), calls=%async_computation.4 | async-start | bytes 8388608 | tf_op jit(solution)/shard_map/all_to_all | solution.py:226
  213.1 8.8 %all_to_all.41 = bf16[768,2048]{1,0:T(8,128)(2,1)} reshape(bf16[256,3,2048]{2,1,0:T(4,128)(2,1)} %all-to-all-done.1) | data formatting | bytes 6291456 | tf_op jit(solution)/shard_map/all_to_all | solution.py:259
  221.9 3.8 fusion
  225.7 1.0 convolution_convert_fusion
  226.7 4.4 %all_to_all.42 = bf16[256,3,2048]{2,1,0:T(4,128)(2,1)} reshape(bf16[768,2048]{1,0:T(8,128)(2,1)S(1)} %convolution_convert_fusion) | data formatting | bytes 6291456 | tf_op jit(solution)/shard_map/all_to_all | solution.py:261
  231.2 30.9 %all-to-all-done.4 = bf16[8,1,16,128,128]{4,3,2,1,0:T(8,128)(2,1)} async-done(((bf16[8,1,16,128,128]{4,3,2,1,0:T(8,128)(2,1)}), bf16[8,1,16,128,128]{4,3,2,1,0:T(8,128)(2,1)}, u32[]{:S(2)}, u32[]{:S(2)}) %all-to-all-start.4) | async-done | bytes 4194336 | tf_op jit(solution)/shard_map/all_to_all | solution.py:226
  262.0 8.3 %all-to-all-start.2 = ((bf16[256,3,2048]{2,1,0:T(4,128)(2,1)}), bf16[256,3,2048]{2,1,0:T(4,128)(2,1)}, u32[]{:S(2)}, u32[]{:S(2)}) async-start(bf16[256,3,2048]{2,1,0:T(4,128)(2,1)} %all_to_all.42), calls=%async_computation.2 | async-start | bytes 8388608 | tf_op jit(solution)/shard_map/all_to_all | solution.py:261
  271.4 3.1 broadcast.129
  274.5 10.9 %scatter_fusion.1 = bf16[8,16,128,128]{3,2,1,0:T(8,128)(2,1)} fusion(bf16[8,16,128,128]{3,2,1,0:T(8,128)(2,1)} %broadcast.129, s32[8]{0:T(128)S(1)} %fusion.16, bf16[8,16,128,128]{3,2,1,0:T(8,128)(2,1)} %bitcast.18), kind=kCustom, calls=%fused_computation.4 | custom fusion | bytes 12582944 | tf_op jit(solution)/shard_map/scatter | solution.py:233
  285.3 81.6 %all-to-all-done.2 = bf16[256,3,2048]{2,1,0:T(4,128)(2,1)} async-done(((bf16[256,3,2048]{2,1,0:T(4,128)(2,1)}), bf16[256,3,2048]{2,1,0:T(4,128)(2,1)}, u32[]{:S(2)}, u32[]{:S(2)}) %all-to-all-start.2) | async-done | bytes 3145760 | tf_op jit(solution)/shard_map/all_to_all | solution.py:261
  366.9 7.5 %all_to_all.44 = bf16[768,2048]{1,0:T(8,128)(2,1)S(1)} reshape(bf16[256,3,2048]{2,1,0:T(4,128)(2,1)} %all-to-all-done.2) | data formatting | bytes 6291456 | tf_op jit(solution)/shard_map/all_to_all | solution.py:261
  374.5 3.2 gather_fusion
  377.6 3.6 reshape.190
  381.2 3.6 multiply_reduce_fusion
  (70 shorter events, 10.4 us)
Async XLA Ops:
  7.2 214.8 %copy-start = (bf16[1,2048,512]{2,1,0:T(8,128)(2,1)S(1)}, bf16[1,2048,512]{2,1,0:T(8,128)(2,1)}, u32[]{:S(2)}) copy-start(bf16[1,2048,512]{2,1,0:T(8,128)(2,1)} %param.29) | copy-start | bytes 6291460
  7.2 53.1 %all-gather.2.cloned.1.call-start = ((), (), s32[]{:S(2)}) async-start(), calls=%async_computation.5 | async-start | bytes 1179648 | tf_op jit(solution)/shard_map/all_gather | solution.py:237
  9.2 20.8 %copy-start.3 = (s32[8,4,10]{2,1,0:T(4,128)S(1)}, s32[8,4,10]{2,1,0:T(4,128)}, u32[]{:S(2)}) copy-start(s32[8,4,10]{2,1,0:T(4,128)} %param.24) | copy-start | bytes 3844
  28.4 2.4 copy-start.11
  30.3 36.3 %copy-start.2 = (bf16[8,4,2048]{2,1,0:T(4,128)(2,1)S(1)}, bf16[8,4,2048]{2,1,0:T(4,128)(2,1)}, u32[]{:S(2)}) copy-start(bf16[8,4,2048]{2,1,0:T(4,128)(2,1)} %param.23) | copy-start | bytes 393220
  30.8 45.6 %copy-start.7 = (f32[2048]{0:T(1024)S(1)}, f32[2048]{0:T(1024)}, u32[]{:S(2)}) copy-start(f32[2048]{0:T(1024)} %param.28) | copy-start | bytes 24580
  62.9 8.8 %all-to-all-start = ((bf16[8,32,256]{2,1,0:T(8,128)(2,1)}), bf16[8,32,256]{2,1,0:T(8,128)(2,1)S(1)}, u32[]{:S(2)}, u32[]{:S(2)}) async-start(bf16[8,32,256]{2,1,0:T(8,128)(2,1)} %bitcast.5), calls=%async_computation | async-start | bytes 262144 | tf_op jit(solution)/shard_map/all_to_all | solution.py:241
  66.4 5.3 %copy-start.8 = (s32[8]{0:T(128)}, s32[8]{0:T(128)S(1)}, u32[]{:S(2)}) copy-start(s32[8]{0:T(128)S(1)} %compare_select_fusion.2) | copy-start | bytes 100
  71.7 24.6 %all-to-all-start.3 = ((s32[8,1,1]{2,1,0:T(1,128)}), s32[8,1,1]{2,1,0:T(1,128)S(1)}, u32[]{:S(2)}, u32[]{:S(2)}) async-start(s32[8,1,1]{2,1,0:T(1,128)} %copy.63), calls=%async_computation.3 | async-start | bytes 8192 | tf_op jit(solution)/shard_map/all_to_all | solution.py:229
  96.3 0.6 copy-start.5
  96.9 110.7 %all-to-all-start.1 = ((bf16[256,3,2048]{2,1,0:T(4,128)(2,1)}), bf16[256,3,2048]{2,1,0:T(4,128)(2,1)}, u32[]{:S(2)}, u32[]{:S(2)}) async-start(bf16[256,3,2048]{2,1,0:T(4,128)(2,1)} %all_to_all.39), calls=%async_computation.1 | async-start | bytes 8388608 | tf_op jit(solution)/shard_map/all_to_all | solution.py:259
  111.0 3.0 copy-start.9
  207.6 54.5 %all-to-all-start.4 = ((bf16[8,1,16,128,128]{4,3,2,1,0:T(8,128)(2,1)}), bf16[8,1,16,128,128]{4,3,2,1,0:T(8,128)(2,1)}, u32[]{:S(2)}, u32[]{:S(2)}) async-start(bf16[8,1,16,128,128]{4,3,2,1,0:T(8,128)(2,1)} %bitcast.43), calls=%async_computation.4 | async-start | bytes 8388608 | tf_op jit(solution)/shard_map/all_to_all | solution.py:226
  221.9 3.8 copy-start.10
  231.2 39.1 %copy-start.4 = (f32[8,4,10]{2,1,0:T(4,128)S(1)}, f32[8,4,10]{2,1,0:T(4,128)}, u32[]{:S(2)}) copy-start(f32[8,4,10]{2,1,0:T(4,128)} %param.25) | copy-start | bytes 3844
  231.2 40.0 %copy-start.6 = (s32[8,1,1]{2,1,0:T(1,128)S(1)}, s32[8,1,1]{2,1,0:T(1,128)}, u32[]{:S(2)}) copy-start(s32[8,1,1]{2,1,0:T(1,128)} %copy-done.5) | copy-start | bytes 100
  262.0 104.9 %all-to-all-start.2 = ((bf16[256,3,2048]{2,1,0:T(4,128)(2,1)}), bf16[256,3,2048]{2,1,0:T(4,128)(2,1)}, u32[]{:S(2)}, u32[]{:S(2)}) async-start(bf16[256,3,2048]{2,1,0:T(4,128)(2,1)} %all_to_all.42), calls=%async_computation.2 | async-start | bytes 8388608 | tf_op jit(solution)/shard_map/all_to_all | solution.py:261
  377.6 8.0 %copy-start.1 = (bf16[1,2048,512]{2,1,0:T(8,128)(2,1)S(1)}, bf16[1,2048,512]{2,1,0:T(8,128)(2,1)}, u32[]{:S(2)}) copy-start(bf16[1,2048,512]{2,1,0:T(8,128)(2,1)} %param.29) | copy-start | bytes 6291460
Sparse Core Ops, SparseCore 0:
  30.1 30.0 all-gather.1

commit v3 on v2

--- a/solution.py
+++ b/solution.py
@@ -18,7 +18,7 @@
     return hi, lo
 
 
-def recur_kernel(s_ref, kq_ref, v_ref, g_ref, dec_ref, beta_ref, gain_ref, so_ref, co_ref, n_ref, r_ref, u_ref):
+def recur_kernel(slot_ref, s_ref, kq_ref, v_ref, g_ref, dec_ref, beta_ref, gain_ref, so_ref, co_ref, n_ref, r_ref, u_ref):
     heads = s_ref.shape[1]
     width = s_ref.shape[-1]
     steps = v_ref.shape[1]
@@ -82,7 +82,7 @@
         so_ref[0, h] = (total[h:h + 1, :] * s_ref[0, h].astype(f32) + delta).astype(so_ref.dtype)
 
 
-def recurrence(states, query_rows, key_rows, value_rows, gate_rows, beta_logit, decay_logit, core_gain):
+def recurrence(slots, states, query_rows, key_rows, value_rows, gate_rows, beta_logit, decay_logit, core_gain):
     batch, heads, width, _ = states.shape
     steps = query_rows.shape[1]
     key_heads = query_rows.shape[-1] // width
@@ -97,28 +97,32 @@
     decay = decay_logit.astype(f32).transpose(0, 2, 1)
     beta = beta_logit.astype(f32).transpose(0, 2, 1)
     gain = core_gain.reshape(1, width)
-    state_spec = pl.BlockSpec((1, heads, width, width), lambda i: (i, 0, 0, 0))
-    row_spec = pl.BlockSpec((1, steps, heads, width), lambda i: (i, 0, 0, 0))
-    coef_spec = pl.BlockSpec((1, heads, steps), lambda i: (i, 0, 0))
+    state_in = pl.BlockSpec((1, heads, width, width), lambda i, slot: (i, 0, 0, 0))
+    state_out = pl.BlockSpec((1, heads, width, width), lambda i, slot: (slot[i], 0, 0, 0))
+    row_spec = pl.BlockSpec((1, steps, heads, width), lambda i, slot: (i, 0, 0, 0))
+    coef_spec = pl.BlockSpec((1, heads, steps), lambda i, slot: (i, 0, 0))
     fresh, core = pl.pallas_call(
         recur_kernel,
-        grid=(batch,),
-        in_specs=[
-            state_spec,
-            pl.BlockSpec((1, heads * span, width), lambda i: (i, 0, 0)),
-            row_spec,
-            row_spec,
-            coef_spec,
-            coef_spec,
-            pl.BlockSpec((1, width), lambda i: (0, 0)),
-        ],
-        out_specs=[state_spec, row_spec],
+        grid_spec=pltpu.PrefetchScalarGridSpec(
+            num_scalar_prefetch=1,
+            grid=(batch,),
+            in_specs=[
+                state_in,
+                pl.BlockSpec((1, heads * span, width), lambda i, slot: (i, 0, 0)),
+                row_spec,
+                row_spec,
+                coef_spec,
+                coef_spec,
+                pl.BlockSpec((1, width), lambda i, slot: (0, 0)),
+            ],
+            out_specs=[state_out, row_spec],
+            scratch_shapes=[pltpu.VMEM((heads * span, width), f32)] * 3,
+        ),
         out_shape=[
             jax.ShapeDtypeStruct(states.shape, bf16),
             jax.ShapeDtypeStruct((batch, steps, heads, width), bf16),
         ],
-        scratch_shapes=[pltpu.VMEM((heads * span, width), f32)] * 3,
-    )(states, kq, values, gates, decay, beta, gain)
+    )(slots, states, kq, values, gates, decay, beta, gain)
     return fresh, core.reshape(batch, steps, heads * width)
 
 
@@ -166,6 +170,25 @@
         gated_out = scaled * core_gain * jax.nn.silu(gate_vals)
         outputs.append(gated_out.reshape(batch_size, head_count * head_width).astype(jnp.bfloat16))
     return (memory_state.astype(jnp.bfloat16), jnp.stack(outputs, axis=1))
+
+
+def place_kernel(place_ref, in_ref, out_ref):
+    out_ref[...] = in_ref[...]
+
+
+def place_rows(rows, places):
+    block = (1,) + rows.shape[1:]
+    tail = (0,) * (rows.ndim - 1)
+    return pl.pallas_call(
+        place_kernel,
+        grid_spec=pltpu.PrefetchScalarGridSpec(
+            num_scalar_prefetch=1,
+            grid=(rows.shape[0],),
+            in_specs=[pl.BlockSpec(block, lambda j, place: (j,) + tail)],
+            out_specs=pl.BlockSpec(block, lambda j, place: (place[j],) + tail),
+        ),
+        out_shape=jax.ShapeDtypeStruct(rows.shape, rows.dtype),
+    )(places, rows)
 
 
 def rms_scale(values, gain):
@@ -214,23 +237,15 @@
     dp_size = lax.axis_size("dp")
     target = new_home // req_count % ep_size
     new_place = new_home % req_count
-    order_ids = jnp.arange(req_count, dtype=jnp.int32)
-    earlier = (target[:, None] == target[None, :]) & (order_ids[None, :] < order_ids[:, None])
-    lane_rank = jnp.sum(earlier.astype(jnp.int32), axis=1)
-    lane_cap = req_count // ep_size
-    buffer_index = target * lane_cap + lane_rank
     fresh_states, core_out = recurrence(
-        states, query_rows, key_rows, value_rows, gate_rows, beta_logit, decay_logit, core_gain
-    )
+        target, states, query_rows, key_rows, value_rows, gate_rows, beta_logit, decay_logit, core_gain
+    )
+    packed_place = jnp.zeros_like(new_place).at[target].set(new_place)
     received = (
-        lax.all_to_all(
-            pack(fresh_states, buffer_index, ep_size), "ep", split_axis=0, concat_axis=0, tiled=True
-        ),
-        lax.all_to_all(
-            pack(new_place, buffer_index, ep_size), "ep", split_axis=0, concat_axis=0, tiled=True
-        ),
-    )
-    moved_out = jnp.zeros_like(states).at[unpack(received[1])].set(unpack(received[0]), mode="drop")
+        lax.all_to_all(fresh_states, "ep", split_axis=0, concat_axis=0, tiled=True),
+        lax.all_to_all(packed_place, "ep", split_axis=0, concat_axis=0, tiled=True),
+    )
+    moved_out = place_rows(received[0], received[1])
     token_count = req_count * step_count
     core_flat = core_out.reshape(token_count, core_out.shape[-1])
     columns = jnp.dot(
@@ -251,22 +266,25 @@
     onehot = (flat_ids[:, None] == jnp.arange(experts, dtype=jnp.int32)[None, :]).astype(jnp.int32)
     route_rank = jnp.sum(jnp.cumsum(onehot, axis=0) * onehot, axis=1) - 1
     slot_index = flat_ids * capacity + route_rank
-    outgoing = (
-        jnp.zeros((experts * capacity, model_width), jnp.bfloat16)
-        .at[slot_index]
-        .set(jnp.repeat(normed, top_count, axis=0))
-    )
+    slot_count = experts * capacity
+    match = slot_index[None, :] == jnp.arange(slot_count, dtype=jnp.int32)[:, None]
+    match = match.reshape(slot_count, token_count, top_count)
+    pick = jnp.any(match, axis=-1).astype(jnp.bfloat16)
+    outgoing = jnp.dot(pick, normed, preferred_element_type=jnp.float32).astype(jnp.bfloat16)
     arrived = lax.all_to_all(outgoing, ("dp", "ep"), 0, 0, tiled=True)
     result = expert_apply(arrived, gate_up[0], down_weight[0])
     returned = lax.all_to_all(result, ("dp", "ep"), 0, 0, tiled=True)
-    routed = returned.reshape(experts * capacity, model_width)[slot_index]
     weights = route_prob.reshape(token_count, top_count)
     weights = weights / jnp.sum(weights, -1, keepdims=True)
-    combined = jnp.sum(
-        routed.reshape(token_count, top_count, model_width).astype(jnp.float32)
-        * weights[:, :, None],
-        axis=1,
-    )
+    spread = jnp.sum(jnp.where(match, weights[None, :, :], 0.0), axis=-1).T
+    high = spread.astype(jnp.bfloat16)
+    rest = spread - high.astype(jnp.float32)
+    middle = rest.astype(jnp.bfloat16)
+    low = (rest - middle.astype(jnp.float32)).astype(jnp.bfloat16)
+    combined = (
+        jnp.dot(high, returned, preferred_element_type=jnp.float32)
+        + jnp.dot(middle, returned, preferred_element_type=jnp.float32)
+    ) + jnp.dot(low, returned, preferred_element_type=jnp.float32)
     mixed_out = (
         (hidden.astype(jnp.float32) + combined)
         .astype(jnp.bfloat16)

time: 394 us -> 383 us (0.972)
  blocking collectives: 0 us -> 111 us
  waiting for transfers between devices: 228 us -> 146 us
  local copies, waits for them, and re-layouts: 87 us -> 47.8 us
  starting transfers between devices: 35.5 us -> 21.4 us
  matrix products: 7.41 us -> 15.8 us
  Pallas kernels: 12.3 us -> 20.3 us
    all_to_all x0 -> x1, blocking collectives: none -> 111 us  [shards(): arrived = lax.all_to_all(outgoing, ('dp', 'ep'), 0, 0, tiled=True)]
    all_to_all x3 -> x2, waiting for transfers between devices: 114 us -> 24.5 us  [the longest x1 24.5 us: shards(): lax.all_to_all(fresh_states, 'ep', split_axis=0, concat_axis=0, tiled=True)]
    scatter x4 -> x1, local copies, waits for them, and re-layouts: 27.8 us -> 0.6 us  [shards(): packed_place = jnp.zeros_like(new_place).at[target].set(new_place)]
    all_to_all x3 -> x2, starting transfers between devices: 23.7 us -> 9.62 us  [the longest x1 5.52 us: shards(): lax.all_to_all(fresh_states, 'ep', split_axis=0, concat_axis=0, tiled=True)]
    pallas_call x1 -> x2, Pallas kernels: 12.3 us -> 20.3 us  [the longest x1 13 us: recurrence(): pl.pallas_call(recur_kernel, grid_spec=pltpu.PrefetchScalarGridSpec(num_s...]
    dot_general x0 -> x4, matrix products: none -> 6.7 us  [the longest x1 2.72 us: shards(): jnp.dot(pick, normed, preferred_element_type=jnp.float32)]
    all_to_all x1, waiting for transfers between devices: 81.6 us -> 88.2 us  [shards(): returned = lax.all_to_all(result, ('dp', 'ep'), 0, 0, tiled=True)]
    another operation x4 -> x2, local copies, waits for them, and re-layouts: 6.17 us -> 0.08 us
  transfers between devices with their start and end apart: 6 -> 5, of which waited for: 5 -> 4; matrix products, arithmetic and copies ran while one was open for 12% -> 4% of each run, Pallas kernels for 0% -> 2%
where the time goes in v3:
time: 383 us; the launch traced here: 381 us
  waiting for transfers between devices  146 us (38%)
  blocking collectives  111 us (29%)
  local copies, waits for them, and re-layouts  47.8 us (12%)
  starting transfers between devices  21.4 us (6%)
  Pallas kernels  20.3 us (5%)
  matrix products  15.8 us (4%)
  between operations  14.3 us (4%)
  other arithmetic  5.01 us (1%)
    all_to_all x1, blocking collectives, shards(): arrived = lax.all_to_all(outgoing, ('dp', 'ep'), 0, 0, tiled=True)  111 us
    all_to_all x1, waiting for transfers between devices, shards(): returned = lax.all_to_all(result, ('dp', 'ep'), 0, 0, tiled=True)  88.2 us
    all_gather x1, waiting for transfers between devices, shards(): lax.all_gather(core_flat, 'ep', axis=0, tiled=True)  27.7 us
    all_to_all x1, waiting for transfers between devices, shards(): lax.all_to_all(fresh_states, 'ep', split_axis=0, concat_axis=0, tiled=True)  24.5 us
    all_to_all x2, local copies, waits for them, and re-layouts, shards(): returned = lax.all_to_all(result, ('dp', 'ep'), 0, 0, tiled=True)  17.9 us
    all_to_all x2, local copies, waits for them, and re-layouts, shards(): arrived = lax.all_to_all(outgoing, ('dp', 'ep'), 0, 0, tiled=True)  17.9 us
    pallas_call x1, Pallas kernels, recurrence(): pl.pallas_call(recur_kernel, grid_spec=pltpu.PrefetchScalarGridSpec(num_s...  13 us
    all_to_all x1, starting transfers between devices, shards(): returned = lax.all_to_all(result, ('dp', 'ep'), 0, 0, tiled=True)  8.25 us
  transfers between devices with their start and end apart: 5, of which 4 were waited for; matrix products, arithmetic and copies ran while one was open for 4% of the time, Pallas kernels for 2%

profile of v3, /device:TPU:1, one launch (start us, length us, event | category | flops | bytes accessed | tf_op | source)
XLA Modules:
  0.0 380.8 jit_solution(3384768142478804578)
XLA Ops:
  7.2 1.3 compare_select_fusion
  8.6 0.9 reshape.117
  9.4 0.9 reshape.118
  10.4 1.6 reshape.119.v_ref
  12.0 1.6 reshape.120.g_ref
  14.4 0.7 copy.58
  15.1 0.7 copy_convert_fusion
  15.8 0.7 copy.60
  16.6 0.7 broadcast_in_dim.12
  17.3 13.0 %shard_map.167 = (bf16[8,16,128,128]{3,2,1,0:T(8,128)(2,1)}, bf16[8,4,16,128]{3,2,1,0:T(8,128)(2,1)}) custom-call(s32[8]{0:T(128)} %get-tuple-element.7.slot_ref, bf16[8,16,128,128]{3,2,1,0:T(8,128)(2,1)} %s_ref.1, bf16[8,128,128]{2,1,0:T(8,128)(2,1)} %bitcast.68, bf16[8,4,16,128]{3,2,1,0:T(8,128)(2,1)} %reshape.119.v_ref, ...), custom_call_target="tpu_custom_call" | custom-call | tf_op jit(solution)/shard_map/pallas_call | solution.py:104
  30.3 1.6 copy.75
  34.5 27.7 %all-gather.2.cloned.1.call-done = bf16[256,2048]{1,0:T(8,128)(2,1)} async-done(((bf16[32,2048]{1,0:T(8,128)(2,1)}), bf16[256,2048]{1,0:T(8,128)(2,1)}) %all-gather.2.cloned.1.call-update) | async-done | bytes 1048592 | tf_op jit(solution)/shard_map/all_gather | solution.py:252
  62.2 2.6 convolution_convert_fusion.2
  64.8 3.5 all-to-all-start
  68.6 5.1 %all-to-all-done = bf16[8,32,256]{2,1,0:T(8,128)(2,1)S(1)} async-done(((bf16[8,32,256]{2,1,0:T(8,128)(2,1)}), bf16[8,32,256]{2,1,0:T(8,128)(2,1)S(1)}, u32[]{:S(2)}, u32[]{:S(2)}) %all-to-all-start) | async-done | bytes 131104 | tf_op jit(solution)/shard_map/all_to_all | solution.py:256
  73.7 4.1 %all-to-all-start.3 = ((s32[8,1,1]{2,1,0:T(1,128)}), s32[8,1,1]{2,1,0:T(1,128)S(1)}, u32[]{:S(2)}, u32[]{:S(2)}) async-start(s32[8,1,1]{2,1,0:T(1,128)} %copy.67), calls=%async_computation.3 | async-start | bytes 8192 | tf_op jit(solution)/shard_map/all_to_all | solution.py:246
  78.4 2.7 convolution_convert_fusion.1
  81.2 9.1 %all_to_all.38 = bf16[256,3,2048]{2,1,0:T(4,128)(2,1)} reshape(bf16[768,2048]{1,0:T(8,128)(2,1)} %convolution_convert_fusion.1) | data formatting | bytes 6291456 | tf_op jit(solution)/shard_map/all_to_all | solution.py:274
  90.3 110.7 %all_to_all.53 = bf16[256,3,2048]{2,1,0:T(4,128)(2,1)} all-to-all(bf16[256,3,2048]{2,1,0:T(4,128)(2,1)} %all_to_all.38), channel_id=1, replica_groups=mesh['dp'=32,'ep'=8] {'dp','ep'}, dimensions={0} | all-to-all | bytes 6291456 | tf_op jit(solution)/shard_map/all_to_all | solution.py:274
  201.0 5.5 %all-to-all-start.4 = ((bf16[8,16,128,128]{3,2,1,0:T(8,128)(2,1)}), bf16[8,16,128,128]{3,2,1,0:T(8,128)(2,1)}, u32[]{:S(2)}, u32[]{:S(2)}) async-start(bf16[8,16,128,128]{3,2,1,0:T(8,128)(2,1)} %get-tuple-element.5), calls=%async_computation.4 | async-start | bytes 8388608 | tf_op jit(solution)/shard_map/all_to_all | solution.py:245
  206.5 8.8 %all_to_all.40 = bf16[768,2048]{1,0:T(8,128)(2,1)} reshape(bf16[256,3,2048]{2,1,0:T(4,128)(2,1)} %all_to_all.53) | data formatting | bytes 6291456 | tf_op jit(solution)/shard_map/all_to_all | solution.py:274
  215.3 3.8 fusion.2
  219.1 2.7 convolution_convert_fusion
  221.8 9.1 %all_to_all.41 = bf16[256,3,2048]{2,1,0:T(4,128)(2,1)} reshape(bf16[768,2048]{1,0:T(8,128)(2,1)} %convolution_convert_fusion) | data formatting | bytes 6291456 | tf_op jit(solution)/shard_map/all_to_all | solution.py:276
  230.9 24.5 %all-to-all-done.4.in_ref = bf16[8,16,128,128]{3,2,1,0:T(8,128)(2,1)} async-done(((bf16[8,16,128,128]{3,2,1,0:T(8,128)(2,1)}), bf16[8,16,128,128]{3,2,1,0:T(8,128)(2,1)}, u32[]{:S(2)}, u32[]{:S(2)}) %all-to-all-start.4) | async-done | bytes 4194336 | tf_op jit(solution)/shard_map/all_to_all | solution.py:245
  255.4 8.3 %all-to-all-start.2 = ((bf16[256,3,2048]{2,1,0:T(4,128)(2,1)}), bf16[256,3,2048]{2,1,0:T(4,128)(2,1)}, u32[]{:S(2)}, u32[]{:S(2)}) async-start(bf16[256,3,2048]{2,1,0:T(4,128)(2,1)} %all_to_all.41), calls=%async_computation.2 | async-start | bytes 8388608 | tf_op jit(solution)/shard_map/all_to_all | solution.py:276
  264.1 0.8 reduce.2.place_ref
  264.9 7.3 %shard_map.168 = bf16[8,16,128,128]{3,2,1,0:T(8,128)(2,1)} custom-call(s32[8]{0:T(128)} %reduce.2.place_ref, bf16[8,16,128,128]{3,2,1,0:T(8,128)(2,1)} %all-to-all-done.4.in_ref), custom_call_target="tpu_custom_call" | custom-call | tf_op jit(solution)/shard_map/pallas_call | solution.py:182
  272.1 88.2 %all-to-all-done.2 = bf16[256,3,2048]{2,1,0:T(4,128)(2,1)} async-done(((bf16[256,3,2048]{2,1,0:T(4,128)(2,1)}), bf16[256,3,2048]{2,1,0:T(4,128)(2,1)}, u32[]{:S(2)}, u32[]{:S(2)}) %all-to-all-start.2) | async-done | bytes 3145760 | tf_op jit(solution)/shard_map/all_to_all | solution.py:276
  360.3 8.8 %all_to_all.43 = bf16[768,2048]{1,0:T(8,128)(2,1)} reshape(bf16[256,3,2048]{2,1,0:T(4,128)(2,1)} %all-to-all-done.2) | data formatting | bytes 6291456 | tf_op jit(solution)/shard_map/all_to_all | solution.py:276
  369.1 2.7 fusion.25
  373.3 0.7 reshape.125
  (53 shorter events, 6.0 us)
Async XLA Ops:
  7.2 208.1 %copy-start = (bf16[1,2048,512]{2,1,0:T(8,128)(2,1)S(1)}, bf16[1,2048,512]{2,1,0:T(8,128)(2,1)}, u32[]{:S(2)}) copy-start(bf16[1,2048,512]{2,1,0:T(8,128)(2,1)} %param.29) | copy-start | bytes 6291460
  7.2 55.0 %all-gather.2.cloned.1.call-start = ((), (), s32[]{:S(2)}) async-start(), calls=%async_computation.5 | async-start | bytes 1179648 | tf_op jit(solution)/shard_map/all_gather | solution.py:252
  10.4 21.6 %copy-start.3 = (s32[8,4,10]{2,1,0:T(4,128)S(1)}, s32[8,4,10]{2,1,0:T(4,128)}, u32[]{:S(2)}) copy-start(s32[8,4,10]{2,1,0:T(4,128)} %param.24) | copy-start | bytes 3844
  30.3 2.9 copy-start.2
  33.1 45.3 %copy-start.5 = (f32[2048]{0:T(1024)S(1)}, f32[2048]{0:T(1024)}, u32[]{:S(2)}) copy-start(f32[2048]{0:T(1024)} %param.28) | copy-start | bytes 24580
  64.8 8.8 %all-to-all-start = ((bf16[8,32,256]{2,1,0:T(8,128)(2,1)}), bf16[8,32,256]{2,1,0:T(8,128)(2,1)S(1)}, u32[]{:S(2)}, u32[]{:S(2)}) async-start(bf16[8,32,256]{2,1,0:T(8,128)(2,1)} %bitcast.5), calls=%async_computation | async-start | bytes 262144 | tf_op jit(solution)/shard_map/all_to_all | solution.py:256
  73.7 16.6 %all-to-all-start.3 = ((s32[8,1,1]{2,1,0:T(1,128)}), s32[8,1,1]{2,1,0:T(1,128)S(1)}, u32[]{:S(2)}, u32[]{:S(2)}) async-start(s32[8,1,1]{2,1,0:T(1,128)} %copy.67), calls=%async_computation.3 | async-start | bytes 8192 | tf_op jit(solution)/shard_map/all_to_all | solution.py:246
  201.0 54.5 %all-to-all-start.4 = ((bf16[8,16,128,128]{3,2,1,0:T(8,128)(2,1)}), bf16[8,16,128,128]{3,2,1,0:T(8,128)(2,1)}, u32[]{:S(2)}, u32[]{:S(2)}) async-start(bf16[8,16,128,128]{3,2,1,0:T(8,128)(2,1)} %get-tuple-element.5), calls=%async_computation.4 | async-start | bytes 8388608 | tf_op jit(solution)/shard_map/all_to_all | solution.py:245
  215.3 3.8 copy-start.6
  230.9 32.8 %copy-start.4 = (f32[8,4,10]{2,1,0:T(4,128)S(1)}, f32[8,4,10]{2,1,0:T(4,128)}, u32[]{:S(2)}) copy-start(f32[8,4,10]{2,1,0:T(4,128)} %param.25) | copy-start | bytes 3844
  255.4 104.9 %all-to-all-start.2 = ((bf16[256,3,2048]{2,1,0:T(4,128)(2,1)}), bf16[256,3,2048]{2,1,0:T(4,128)(2,1)}, u32[]{:S(2)}, u32[]{:S(2)}) async-start(bf16[256,3,2048]{2,1,0:T(4,128)(2,1)} %all_to_all.41), calls=%async_computation.2 | async-start | bytes 8388608 | tf_op jit(solution)/shard_map/all_to_all | solution.py:276
  369.1 2.8 copy-start.1
Sparse Core Ops, SparseCore 0:
  32.1 30.0 all-gather.1

commit v4 on v3

--- a/solution.py
+++ b/solution.py
@@ -261,30 +261,38 @@
     normed = rms_scale(hidden.astype(jnp.float32), moe_gain).astype(jnp.bfloat16)
     top_count = route_ids.shape[-1]
     experts = dp_size * ep_size
-    capacity = (token_count * top_count + experts - 1) // experts + 1
+    capacity = 4
     flat_ids = route_ids.reshape(-1)
     onehot = (flat_ids[:, None] == jnp.arange(experts, dtype=jnp.int32)[None, :]).astype(jnp.int32)
     route_rank = jnp.sum(jnp.cumsum(onehot, axis=0) * onehot, axis=1) - 1
     slot_index = flat_ids * capacity + route_rank
     slot_count = experts * capacity
     match = slot_index[None, :] == jnp.arange(slot_count, dtype=jnp.int32)[:, None]
-    match = match.reshape(slot_count, token_count, top_count)
+    match = match.reshape(experts, capacity, token_count, top_count)
     pick = jnp.any(match, axis=-1).astype(jnp.bfloat16)
-    outgoing = jnp.dot(pick, normed, preferred_element_type=jnp.float32).astype(jnp.bfloat16)
+    outgoing = jnp.einsum(
+        "esk,kd->esd", pick, normed, preferred_element_type=jnp.float32
+    ).astype(jnp.bfloat16)
     arrived = lax.all_to_all(outgoing, ("dp", "ep"), 0, 0, tiled=True)
-    result = expert_apply(arrived, gate_up[0], down_weight[0])
+    hidden_units = down_weight.shape[1]
+    joined = jnp.einsum("esd,df->esf", arrived, gate_up[0], preferred_element_type=jnp.float32)
+    active = (jax.nn.silu(joined[..., :hidden_units]) * joined[..., hidden_units:]).astype(jnp.bfloat16)
+    result = jnp.einsum(
+        "esf,fd->esd", active, down_weight[0], preferred_element_type=jnp.float32
+    ).astype(jnp.bfloat16)
     returned = lax.all_to_all(result, ("dp", "ep"), 0, 0, tiled=True)
     weights = route_prob.reshape(token_count, top_count)
     weights = weights / jnp.sum(weights, -1, keepdims=True)
-    spread = jnp.sum(jnp.where(match, weights[None, :, :], 0.0), axis=-1).T
+    spread = jnp.sum(jnp.where(match, weights[None, None, :, :], 0.0), axis=-1)
     high = spread.astype(jnp.bfloat16)
     rest = spread - high.astype(jnp.float32)
     middle = rest.astype(jnp.bfloat16)
     low = (rest - middle.astype(jnp.float32)).astype(jnp.bfloat16)
+    combine = "esk,esd->kd"
     combined = (
-        jnp.dot(high, returned, preferred_element_type=jnp.float32)
-        + jnp.dot(middle, returned, preferred_element_type=jnp.float32)
-    ) + jnp.dot(low, returned, preferred_element_type=jnp.float32)
+        jnp.einsum(combine, high, returned, preferred_element_type=jnp.float32)
+        + jnp.einsum(combine, middle, returned, preferred_element_type=jnp.float32)
+    ) + jnp.einsum(combine, low, returned, preferred_element_type=jnp.float32)
     mixed_out = (
         (hidden.astype(jnp.float32) + combined)
         .astype(jnp.bfloat16)

time: 383 us -> 384 us (level)
  local copies, waits for them, and re-layouts: 47.8 us -> 22.2 us
  matrix products: 15.8 us -> 32.4 us
  waiting for transfers between devices: 146 us -> 156 us
    all_to_all x4 -> x0, local copies, waits for them, and re-layouts: 35.8 us -> none  [the longest x2 17.9 us: shards(): returned = lax.all_to_all(result, ('dp', 'ep'), 0, 0, tiled=True)]
    dot_general x6, matrix products: 13.2 us -> 29.7 us  [the longest x1 6.88 us: shards(): jnp.einsum('esd,df->esf', arrived, gate_up[0], preferred_element_type=jnp...]
    all_to_all x1, waiting for transfers between devices: 24.5 us -> 35.5 us  [shards(): lax.all_to_all(fresh_states, 'ep', split_axis=0, concat_axis=0, tiled=True)]
    convert_element_type x0 -> x2, local copies, waits for them, and re-layouts: none -> 10.4 us  [the longest x1 5.21 us: shards(): result = jnp.einsum('esf,fd->esd', active, down_weight[0], preferred_elem...]
  transfers between devices with their start and end apart: 5 -> 5, of which waited for: 4 -> 4; matrix products, arithmetic and copies ran while one was open for 4% -> 6% of each run, Pallas kernels for 2% -> 2%
where the time goes in v4:
time: 384 us; the launch traced here: 383 us
  waiting for transfers between devices  156 us (41%)
  blocking collectives  111 us (29%)
  matrix products  32.4 us (8%)
  local copies, waits for them, and re-layouts  22.2 us (6%)
  starting transfers between devices  21.4 us (6%)
  Pallas kernels  20.4 us (5%)
  between operations  14.3 us (4%)
  other arithmetic  5.07 us (1%)
    all_to_all x1, blocking collectives, shards(): arrived = lax.all_to_all(outgoing, ('dp', 'ep'), 0, 0, tiled=True)  111 us
    all_to_all x1, waiting for transfers between devices, shards(): returned = lax.all_to_all(result, ('dp', 'ep'), 0, 0, tiled=True)  88.1 us
    all_to_all x1, waiting for transfers between devices, shards(): lax.all_to_all(fresh_states, 'ep', split_axis=0, concat_axis=0, tiled=True)  35.5 us
    all_gather x1, waiting for transfers between devices, shards(): lax.all_gather(core_flat, 'ep', axis=0, tiled=True)  27.7 us
    pallas_call x1, Pallas kernels, recurrence(): pl.pallas_call(recur_kernel, grid_spec=pltpu.PrefetchScalarGridSpec(num_s...  13.1 us
    all_to_all x1, starting transfers between devices, shards(): returned = lax.all_to_all(result, ('dp', 'ep'), 0, 0, tiled=True)  8.25 us
  transfers between devices with their start and end apart: 5, of which 4 were waited for; matrix products, arithmetic and copies ran while one was open for 6% of the time, Pallas kernels for 2%

profile of v4, /device:TPU:1, one launch (start us, length us, event | category | flops | bytes accessed | tf_op | source)
XLA Modules:
  0.0 382.8 jit_solution(10065815982335671021)
XLA Ops:
  7.2 1.3 compare_select_fusion.1
  8.6 0.9 reshape.119
  9.4 0.9 reshape.120
  10.4 1.6 reshape.121.v_ref
  12.0 1.6 reshape.122.g_ref
  13.7 0.7 copy_convert_fusion.1
  14.4 0.7 copy.76
  15.8 0.7 copy.78
  16.5 0.7 broadcast_in_dim.12
  17.3 13.1 %shard_map.167 = (bf16[8,16,128,128]{3,2,1,0:T(8,128)(2,1)}, bf16[8,4,16,128]{3,2,1,0:T(8,128)(2,1)}) custom-call(s32[8]{0:T(128)} %get-tuple-element.7.slot_ref, bf16[8,16,128,128]{3,2,1,0:T(8,128)(2,1)} %s_ref.1, bf16[8,128,128]{2,1,0:T(8,128)(2,1)} %bitcast.58, bf16[8,4,16,128]{3,2,1,0:T(8,128)(2,1)} %reshape.121.v_ref, ...), custom_call_target="tpu_custom_call" | custom-call | tf_op jit(solution)/shard_map/pallas_call | solution.py:104
  30.4 1.6 copy.121
  34.6 27.7 %all-gather.2.cloned.1.call-done = bf16[256,2048]{1,0:T(8,128)(2,1)} async-done(((bf16[32,2048]{1,0:T(8,128)(2,1)}), bf16[256,2048]{1,0:T(8,128)(2,1)}) %all-gather.2.cloned.1.call-update) | async-done | bytes 1048592 | tf_op jit(solution)/shard_map/all_gather | solution.py:252
  62.3 2.6 convolution_convert_fusion.2
  64.9 3.5 all-to-all-start
  68.7 5.0 %all-to-all-done = bf16[8,32,256]{2,1,0:T(8,128)(2,1)S(1)} async-done(((bf16[8,32,256]{2,1,0:T(8,128)(2,1)}), bf16[8,32,256]{2,1,0:T(8,128)(2,1)S(1)}, u32[]{:S(2)}, u32[]{:S(2)}) %all-to-all-start) | async-done | bytes 131104 | tf_op jit(solution)/shard_map/all_to_all | solution.py:256
  73.7 4.0 %all-to-all-start.3 = ((s32[8,1,1]{2,1,0:T(1,128)}), s32[8,1,1]{2,1,0:T(1,128)S(1)}, u32[]{:S(2)}, u32[]{:S(2)}) async-start(s32[8,1,1]{2,1,0:T(1,128)} %copy.91), calls=%async_computation.3 | async-start | bytes 8192 | tf_op jit(solution)/shard_map/all_to_all | solution.py:246
  78.4 1.3 convolution_convert_fusion.1
  79.8 5.2 %copy.85 = bf16[256,4,2048]{2,1,0:T(4,128)(2,1)} copy(bf16[256,4,2048]{2,0,1:T(8,128)(2,1)S(1)} %convolution_convert_fusion.1) | data formatting | bytes 8388608 | tf_op jit(solution)/shard_map/convert_element_type | solution.py:275
  84.9 110.7 %all_to_all.39 = bf16[256,4,2048]{2,1,0:T(4,128)(2,1)} all-to-all(bf16[256,4,2048]{2,1,0:T(4,128)(2,1)} %copy.85), channel_id=1, replica_groups=mesh['dp'=32,'ep'=8] {'dp','ep'}, dimensions={0} | all-to-all | bytes 8388608 | tf_op jit(solution)/shard_map/all_to_all | solution.py:276
  195.6 5.5 %all-to-all-start.4 = ((bf16[8,16,128,128]{3,2,1,0:T(8,128)(2,1)}), bf16[8,16,128,128]{3,2,1,0:T(8,128)(2,1)}, u32[]{:S(2)}, u32[]{:S(2)}) async-start(bf16[8,16,128,128]{3,2,1,0:T(8,128)(2,1)} %get-tuple-element.5), calls=%async_computation.4 | async-start | bytes 8388608 | tf_op jit(solution)/shard_map/all_to_all | solution.py:245
  201.2 6.9 %fusion = f32[256,4,512]{2,0,1:T(8,128)S(1)} fusion(bf16[256,4,2048]{2,1,0:T(4,128)(2,1)} %all_to_all.39, bf16[1,2048,512]{2,1,0:T(8,128)(2,1)S(1)} %copy-done), kind=kOutput, calls=%fused_computation.1 | convolution fusion | flops 2147483648 | bytes 8388608 | tf_op jit(solution)/shard_map/esd,df->esf/dot_general | solution.py:278
  208.0 1.3 convolution_convert_fusion
  209.3 5.2 %copy.87 = bf16[256,4,2048]{2,1,0:T(4,128)(2,1)} copy(bf16[256,4,2048]{2,0,1:T(8,128)(2,1)S(1)} %convolution_convert_fusion) | data formatting | bytes 8388608 | tf_op jit(solution)/shard_map/convert_element_type | solution.py:282
  214.5 35.5 %all-to-all-done.4.in_ref = bf16[8,16,128,128]{3,2,1,0:T(8,128)(2,1)} async-done(((bf16[8,16,128,128]{3,2,1,0:T(8,128)(2,1)}), bf16[8,16,128,128]{3,2,1,0:T(8,128)(2,1)}, u32[]{:S(2)}, u32[]{:S(2)}) %all-to-all-start.4) | async-done | bytes 4194336 | tf_op jit(solution)/shard_map/all_to_all | solution.py:245
  250.1 8.3 %all-to-all-start.2 = ((bf16[256,4,2048]{2,1,0:T(4,128)(2,1)}), bf16[256,4,2048]{2,1,0:T(4,128)(2,1)}, u32[]{:S(2)}, u32[]{:S(2)}) async-start(bf16[256,4,2048]{2,1,0:T(4,128)(2,1)} %copy.87), calls=%async_computation.2 | async-start | bytes 8388608 | tf_op jit(solution)/shard_map/all_to_all | solution.py:283
  258.8 0.8 reduce.2.place_ref
  259.6 7.3 %shard_map.168 = bf16[8,16,128,128]{3,2,1,0:T(8,128)(2,1)} custom-call(s32[8]{0:T(128)} %reduce.2.place_ref, bf16[8,16,128,128]{3,2,1,0:T(8,128)(2,1)} %all-to-all-done.4.in_ref), custom_call_target="tpu_custom_call" | custom-call | tf_op jit(solution)/shard_map/pallas_call | solution.py:182
  266.8 88.1 %all-to-all-done.2 = bf16[256,4,2048]{2,1,0:T(4,128)(2,1)} async-done(((bf16[256,4,2048]{2,1,0:T(4,128)(2,1)}), bf16[256,4,2048]{2,1,0:T(4,128)(2,1)}, u32[]{:S(2)}, u32[]{:S(2)}) %all-to-all-start.2) | async-done | bytes 4194336 | tf_op jit(solution)/shard_map/all_to_all | solution.py:283
  355.0 6.7 %fusion.8 = f32[32,2048]{1,0:T(8,128)S(1)} fusion(bf16[256,4,2048]{2,1,0:T(4,128)(2,1)} %all-to-all-done.2, f32[256,4,32]{0,2,1:T(8,128)S(1)} %fusion.30), kind=kOutput, calls=%fused_computation.11 | convolution fusion | flops 134250496 | bytes 4587520 | tf_op jit(solution)/shard_map/esk,esd->kd/dot_general | solution.py:293
  361.7 6.8 %fusion.23 = f32[32,2048]{1,0:T(8,128)S(1)} fusion(f32[32,2048]{1,0:T(8,128)S(1)} %fusion.8, bf16[256,4,2048]{2,1,0:T(4,128)(2,1)} %all-to-all-done.2, f32[256,4,32]{0,2,1:T(8,128)S(1)} %fusion.30), kind=kOutput, calls=%fused_computation.16 | convolution fusion | flops 134414336 | bytes 4849664 | tf_op jit(solution)/shard_map/esk,esd->kd/dot_general | solution.py:294
  368.5 6.8 %fusion.26 = bf16[32,2048]{1,0:T(8,128)(2,1)S(1)} fusion(f32[32,2048]{1,0:T(8,128)S(1)} %fusion.23, bf16[256,4,2048]{2,1,0:T(4,128)(2,1)} %all-to-all-done.2, bf16[32,2048]{1,0:T(8,128)(2,1)S(1)} %add_convert_fusion.1, f32[256,4,32]{0,2,1:T(8,128)S(1)} %fusion.30), kind=kOutput, calls=%fused_computation.17 | convolution fusion | flops 134709248 | bytes 4849664 | tf_op jit(solution)/shard_map/esk,esd->kd/dot_general | solution.py:295
  375.2 0.7 reshape.127
  (50 shorter events, 4.6 us)
Async XLA Ops:
  7.2 194.0 %copy-start = (bf16[1,2048,512]{2,1,0:T(8,128)(2,1)S(1)}, bf16[1,2048,512]{2,1,0:T(8,128)(2,1)}, u32[]{:S(2)}) copy-start(bf16[1,2048,512]{2,1,0:T(8,128)(2,1)} %param.29) | copy-start | bytes 6291460
  7.2 24.8 %copy-start.2 = (s32[8,4,10]{2,1,0:T(4,128)S(1)}, s32[8,4,10]{2,1,0:T(4,128)}, u32[]{:S(2)}) copy-start(s32[8,4,10]{2,1,0:T(4,128)} %param.24) | copy-start | bytes 3844
  7.2 55.1 %all-gather.2.cloned.1.call-start = ((), (), s32[]{:S(2)}) async-start(), calls=%async_computation.5 | async-start | bytes 1179648 | tf_op jit(solution)/shard_map/all_gather | solution.py:252
  17.3 16.0 %copy-start.1 = (bf16[8,4,2048]{2,1,0:T(4,128)(2,1)S(1)}, bf16[8,4,2048]{2,1,0:T(4,128)(2,1)}, u32[]{:S(2)}) copy-start(bf16[8,4,2048]{2,1,0:T(4,128)(2,1)} %param.23) | copy-start | bytes 393220
  32.6 45.8 %copy-start.4 = (f32[2048]{0:T(1024)S(1)}, f32[2048]{0:T(1024)}, u32[]{:S(2)}) copy-start(f32[2048]{0:T(1024)} %param.28) | copy-start | bytes 24580
  64.9 8.8 %all-to-all-start = ((bf16[8,32,256]{2,1,0:T(8,128)(2,1)}), bf16[8,32,256]{2,1,0:T(8,128)(2,1)S(1)}, u32[]{:S(2)}, u32[]{:S(2)}) async-start(bf16[8,32,256]{2,1,0:T(8,128)(2,1)} %bitcast.5), calls=%async_computation | async-start | bytes 262144 | tf_op jit(solution)/shard_map/all_to_all | solution.py:256
  73.7 11.2 %all-to-all-start.3 = ((s32[8,1,1]{2,1,0:T(1,128)}), s32[8,1,1]{2,1,0:T(1,128)S(1)}, u32[]{:S(2)}, u32[]{:S(2)}) async-start(s32[8,1,1]{2,1,0:T(1,128)} %copy.91), calls=%async_computation.3 | async-start | bytes 8192 | tf_op jit(solution)/shard_map/all_to_all | solution.py:246
  195.6 54.5 %all-to-all-start.4 = ((bf16[8,16,128,128]{3,2,1,0:T(8,128)(2,1)}), bf16[8,16,128,128]{3,2,1,0:T(8,128)(2,1)}, u32[]{:S(2)}, u32[]{:S(2)}) async-start(bf16[8,16,128,128]{3,2,1,0:T(8,128)(2,1)} %get-tuple-element.5), calls=%async_computation.4 | async-start | bytes 8388608 | tf_op jit(solution)/shard_map/all_to_all | solution.py:245
  201.1 6.9 %copy-start.5 = (bf16[1,256,2048]{2,1,0:T(8,128)(2,1)S(1)}, bf16[1,256,2048]{2,1,0:T(8,128)(2,1)}, u32[]{:S(2)}) copy-start(bf16[1,256,2048]{2,1,0:T(8,128)(2,1)} %param.30) | copy-start | bytes 3145732
  214.5 43.8 %copy-start.3 = (f32[8,4,10]{2,1,0:T(4,128)S(1)}, f32[8,4,10]{2,1,0:T(4,128)}, u32[]{:S(2)}) copy-start(f32[8,4,10]{2,1,0:T(4,128)} %param.25) | copy-start | bytes 3844
  250.1 104.9 %all-to-all-start.2 = ((bf16[256,4,2048]{2,1,0:T(4,128)(2,1)}), bf16[256,4,2048]{2,1,0:T(4,128)(2,1)}, u32[]{:S(2)}, u32[]{:S(2)}) async-start(bf16[256,4,2048]{2,1,0:T(4,128)(2,1)} %copy.87), calls=%async_computation.2 | async-start | bytes 8388608 | tf_op jit(solution)/shard_map/all_to_all | solution.py:283
Sparse Core Ops, SparseCore 0:
  32.1 30.0 all-gather.1

commit v5 on v4

--- a/solution.py
+++ b/solution.py
@@ -261,7 +261,7 @@
     normed = rms_scale(hidden.astype(jnp.float32), moe_gain).astype(jnp.bfloat16)
     top_count = route_ids.shape[-1]
     experts = dp_size * ep_size
-    capacity = 4
+    capacity = (token_count * top_count + experts - 1) // experts + 1
     flat_ids = route_ids.reshape(-1)
     onehot = (flat_ids[:, None] == jnp.arange(experts, dtype=jnp.int32)[None, :]).astype(jnp.int32)
     route_rank = jnp.sum(jnp.cumsum(onehot, axis=0) * onehot, axis=1) - 1
@@ -270,17 +270,26 @@
     match = slot_index[None, :] == jnp.arange(slot_count, dtype=jnp.int32)[:, None]
     match = match.reshape(experts, capacity, token_count, top_count)
     pick = jnp.any(match, axis=-1).astype(jnp.bfloat16)
+    lane_count = 128
+    chunks = model_width // lane_count
+    normed_tiles = normed.reshape(token_count, chunks, lane_count)
     outgoing = jnp.einsum(
-        "esk,kd->esd", pick, normed, preferred_element_type=jnp.float32
+        "esk,kcl->escl", pick, normed_tiles, preferred_element_type=jnp.float32
     ).astype(jnp.bfloat16)
+    outgoing = outgoing.reshape(experts, capacity * chunks, lane_count)
     arrived = lax.all_to_all(outgoing, ("dp", "ep"), 0, 0, tiled=True)
+    arrived = arrived.reshape(experts, capacity, chunks, lane_count)
     hidden_units = down_weight.shape[1]
-    joined = jnp.einsum("esd,df->esf", arrived, gate_up[0], preferred_element_type=jnp.float32)
+    gate_tiles = gate_up[0].reshape(chunks, lane_count, gate_up.shape[-1])
+    joined = jnp.einsum("escl,clf->esf", arrived, gate_tiles, preferred_element_type=jnp.float32)
     active = (jax.nn.silu(joined[..., :hidden_units]) * joined[..., hidden_units:]).astype(jnp.bfloat16)
+    down_tiles = down_weight[0].reshape(hidden_units, chunks, lane_count)
     result = jnp.einsum(
-        "esf,fd->esd", active, down_weight[0], preferred_element_type=jnp.float32
+        "esf,fcl->escl", active, down_tiles, preferred_element_type=jnp.float32
     ).astype(jnp.bfloat16)
+    result = result.reshape(experts, capacity * chunks, lane_count)
     returned = lax.all_to_all(result, ("dp", "ep"), 0, 0, tiled=True)
+    returned = returned.reshape(experts, capacity, chunks, lane_count)
     weights = route_prob.reshape(token_count, top_count)
     weights = weights / jnp.sum(weights, -1, keepdims=True)
     spread = jnp.sum(jnp.where(match, weights[None, None, :, :], 0.0), axis=-1)
@@ -288,11 +297,12 @@
     rest = spread - high.astype(jnp.float32)
     middle = rest.astype(jnp.bfloat16)
     low = (rest - middle.astype(jnp.float32)).astype(jnp.bfloat16)
-    combine = "esk,esd->kd"
+    combine = "esk,escl->kcl"
     combined = (
         jnp.einsum(combine, high, returned, preferred_element_type=jnp.float32)
         + jnp.einsum(combine, middle, returned, preferred_element_type=jnp.float32)
     ) + jnp.einsum(combine, low, returned, preferred_element_type=jnp.float32)
+    combined = combined.reshape(token_count, model_width)
     mixed_out = (
         (hidden.astype(jnp.float32) + combined)
         .astype(jnp.bfloat16)

time: 384 us -> 325 us (0.85)
  blocking collectives: 111 us -> 88.8 us
  waiting for transfers between devices: 156 us -> 137 us
  matrix products: 32.4 us -> 14.1 us
    all_to_all x1, blocking collectives: 111 us -> 88.8 us  [shards(): arrived = lax.all_to_all(outgoing, ('dp', 'ep'), 0, 0, tiled=True)]
    all_to_all x1, waiting for transfers between devices: 88.1 us -> 66.4 us  [shards(): returned = lax.all_to_all(result, ('dp', 'ep'), 0, 0, tiled=True)]
    convert_element_type x2 -> x0, local copies, waits for them, and re-layouts: 10.4 us -> none  [the longest x1 5.21 us: shards(): result = jnp.einsum('esf,fd->esd', active, down_weight[0], preferred_elem...]
    reshape x1 -> x3, local copies, waits for them, and re-layouts: 0.71 us -> 7.53 us  [the longest x1 3.75 us: shards(): result = result.reshape(experts, capacity * chunks, lane_count)]
    dot_general x3, matrix products: 9.49 us -> 3.87 us  [the longest x1 1.78 us: shards(): jnp.einsum('escl,clf->esf', arrived, gate_tiles, preferred_element_type=j...]
    dot_general x1, matrix products: 6.75 us -> 2.53 us  [shards(): jnp.einsum(combine, low, returned, preferred_element_type=jnp.float32)]
    dot_general x1, matrix products: 6.73 us -> 2.52 us  [shards(): jnp.einsum(combine, high, returned, preferred_element_type=jnp.float32)]
    dot_general x1, matrix products: 6.76 us -> 2.55 us  [shards(): jnp.einsum(combine, middle, returned, preferred_element_type=jnp.float32)]
where the time goes in v5:
time: 325 us; the launch traced here: 324 us
  waiting for transfers between devices  137 us (42%)
  blocking collectives  88.8 us (27%)
  local copies, waits for them, and re-layouts  23 us (7%)
  starting transfers between devices  20.7 us (6%)
  Pallas kernels  20.3 us (6%)
  between operations  14.3 us (4%)
  matrix products  14.1 us (4%)
  other arithmetic  5.84 us (2%)
    all_to_all x1, blocking collectives, shards(): arrived = lax.all_to_all(outgoing, ('dp', 'ep'), 0, 0, tiled=True)  88.8 us
    all_to_all x1, waiting for transfers between devices, shards(): returned = lax.all_to_all(result, ('dp', 'ep'), 0, 0, tiled=True)  66.4 us
    all_to_all x1, waiting for transfers between devices, shards(): lax.all_to_all(fresh_states, 'ep', split_axis=0, concat_axis=0, tiled=True)  38.1 us
    all_gather x1, waiting for transfers between devices, shards(): lax.all_gather(core_flat, 'ep', axis=0, tiled=True)  27.6 us
    pallas_call x1, Pallas kernels, recurrence(): pl.pallas_call(recur_kernel, grid_spec=pltpu.PrefetchScalarGridSpec(num_s...  13 us
    all_to_all x1, starting transfers between devices, shards(): returned = lax.all_to_all(result, ('dp', 'ep'), 0, 0, tiled=True)  7.84 us
    pallas_call x1, Pallas kernels, place_rows(): pl.pallas_call(place_kernel, grid_spec=pltpu.PrefetchScalarGridSpec(num_s...  7.26 us
  transfers between devices with their start and end apart: 5, of which 4 were waited for; matrix products, arithmetic and copies ran while one was open for 6% of the time, Pallas kernels for 2%

profile of v5, /device:TPU:1, one launch (start us, length us, event | category | flops | bytes accessed | tf_op | source)
XLA Modules:
  0.0 324.2 jit_solution(7757992553663519584)
XLA Ops:
  7.2 1.3 compare_select_fusion.1
  8.6 0.9 reshape.147
  9.4 0.9 reshape.148
  10.4 1.7 reshape.149.v_ref
  12.0 1.6 reshape.150.g_ref
  14.4 0.7 copy.92
  15.9 0.7 copy.94
  17.3 13.0 %shard_map.167 = (bf16[8,16,128,128]{3,2,1,0:T(8,128)(2,1)}, bf16[8,4,16,128]{3,2,1,0:T(8,128)(2,1)}) custom-call(s32[8]{0:T(128)} %get-tuple-element.7.slot_ref, bf16[8,16,128,128]{3,2,1,0:T(8,128)(2,1)} %s_ref.1, bf16[8,128,128]{2,1,0:T(8,128)(2,1)} %bitcast.88, bf16[8,4,16,128]{3,2,1,0:T(8,128)(2,1)} %reshape.149.v_ref, ...), custom_call_target="tpu_custom_call" | custom-call | tf_op jit(solution)/shard_map/pallas_call | solution.py:104
  30.3 1.6 copy.148
  34.6 27.6 %all-gather.2.cloned.1.call-done = bf16[256,2048]{1,0:T(8,128)(2,1)} async-done(((bf16[32,2048]{1,0:T(8,128)(2,1)}), bf16[256,2048]{1,0:T(8,128)(2,1)}) %all-gather.2.cloned.1.call-update) | async-done | bytes 1048592 | tf_op jit(solution)/shard_map/all_gather | solution.py:252
  62.2 2.6 convolution_convert_fusion.2
  64.8 3.5 %all-to-all-start = ((bf16[8,32,256]{2,1,0:T(8,128)(2,1)}), bf16[8,32,256]{2,1,0:T(8,128)(2,1)S(1)}, u32[]{:S(2)}, u32[]{:S(2)}) async-start(bf16[8,32,256]{2,1,0:T(8,128)(2,1)} %bitcast.5), calls=%async_computation | async-start | bytes 262144 | tf_op jit(solution)/shard_map/all_to_all | solution.py:256
  68.6 5.1 %all-to-all-done = bf16[8,32,256]{2,1,0:T(8,128)(2,1)S(1)} async-done(((bf16[8,32,256]{2,1,0:T(8,128)(2,1)}), bf16[8,32,256]{2,1,0:T(8,128)(2,1)S(1)}, u32[]{:S(2)}, u32[]{:S(2)}) %all-to-all-start) | async-done | bytes 131104 | tf_op jit(solution)/shard_map/all_to_all | solution.py:256
  73.7 4.0 %all-to-all-start.3 = ((s32[8,1,1]{2,1,0:T(1,128)}), s32[8,1,1]{2,1,0:T(1,128)S(1)}, u32[]{:S(2)}, u32[]{:S(2)}) async-start(s32[8,1,1]{2,1,0:T(1,128)} %copy.110), calls=%async_computation.3 | async-start | bytes 8192 | tf_op jit(solution)/shard_map/all_to_all | solution.py:246
  78.4 1.0 convolution_convert_fusion
  79.4 3.7 %copy.102 = bf16[256,48,128]{2,1,0:T(8,128)(2,1)} copy(bf16[256,48,128]{2,0,1:T(8,128)(2,1)S(1)} %bitcast.81) | data formatting | bytes 6291456 | tf_op jit(solution)/shard_map/reshape | solution.py:279
  83.1 88.8 %all_to_all.39 = bf16[256,48,128]{2,1,0:T(8,128)(2,1)} all-to-all(bf16[256,48,128]{2,1,0:T(8,128)(2,1)} %copy.102), channel_id=1, replica_groups=mesh['dp'=32,'ep'=8] {'dp','ep'}, dimensions={0} | all-to-all | bytes 6291456 | tf_op jit(solution)/shard_map/all_to_all | solution.py:280
  171.9 5.3 %all-to-all-start.4 = ((bf16[8,16,128,128]{3,2,1,0:T(8,128)(2,1)}), bf16[8,16,128,128]{3,2,1,0:T(8,128)(2,1)}, u32[]{:S(2)}, u32[]{:S(2)}) async-start(bf16[8,16,128,128]{3,2,1,0:T(8,128)(2,1)} %get-tuple-element.5), calls=%async_computation.4 | async-start | bytes 8388608 | tf_op jit(solution)/shard_map/all_to_all | solution.py:245
  177.1 1.4 copy.118
  178.6 2.7 copy.103
  181.3 1.8 convolution_bitcast_fusion
  183.1 1.1 convolution_convert_fusion.1
  184.2 3.7 %copy.105 = bf16[256,48,128]{2,1,0:T(8,128)(2,1)} copy(bf16[256,48,128]{2,0,1:T(8,128)(2,1)S(1)} %bitcast.82) | data formatting | bytes 6291456 | tf_op jit(solution)/shard_map/reshape | solution.py:290
  187.9 38.1 %all-to-all-done.4.in_ref = bf16[8,16,128,128]{3,2,1,0:T(8,128)(2,1)} async-done(((bf16[8,16,128,128]{3,2,1,0:T(8,128)(2,1)}), bf16[8,16,128,128]{3,2,1,0:T(8,128)(2,1)}, u32[]{:S(2)}, u32[]{:S(2)}) %all-to-all-start.4) | async-done | bytes 4194336 | tf_op jit(solution)/shard_map/all_to_all | solution.py:245
  226.1 7.8 %all-to-all-start.2 = ((bf16[256,48,128]{2,1,0:T(8,128)(2,1)}), bf16[256,48,128]{2,1,0:T(8,128)(2,1)}, u32[]{:S(2)}, u32[]{:S(2)}) async-start(bf16[256,48,128]{2,1,0:T(8,128)(2,1)} %copy.105), calls=%async_computation.2 | async-start | bytes 6291456 | tf_op jit(solution)/shard_map/all_to_all | solution.py:291
  234.4 0.8 reduce.2.place_ref
  235.1 7.3 %shard_map.168 = bf16[8,16,128,128]{3,2,1,0:T(8,128)(2,1)} custom-call(s32[8]{0:T(128)} %reduce.2.place_ref, bf16[8,16,128,128]{3,2,1,0:T(8,128)(2,1)} %all-to-all-done.4.in_ref), custom_call_target="tpu_custom_call" | custom-call | tf_op jit(solution)/shard_map/pallas_call | solution.py:182
  242.4 66.4 %all-to-all-done.2 = bf16[256,48,128]{2,1,0:T(8,128)(2,1)} async-done(((bf16[256,48,128]{2,1,0:T(8,128)(2,1)}), bf16[256,48,128]{2,1,0:T(8,128)(2,1)}, u32[]{:S(2)}, u32[]{:S(2)}) %all-to-all-start.2) | async-done | bytes 3145760 | tf_op jit(solution)/shard_map/all_to_all | solution.py:291
  308.8 2.5 fusion.6
  311.3 2.5 fusion.18
  313.8 2.5 fusion.15
  316.6 0.8 fusion.31
  (52 shorter events, 6.3 us)
Async XLA Ops:
  7.2 174.1 %copy-start = (bf16[1,2048,512]{2,1,0:T(8,128)(2,1)S(1)}, bf16[1,2048,512]{2,1,0:T(8,128)(2,1)}, u32[]{:S(2)}) copy-start(bf16[1,2048,512]{2,1,0:T(8,128)(2,1)} %param.29) | copy-start | bytes 6291460
  7.2 55.0 %all-gather.2.cloned.1.call-start = ((), (), s32[]{:S(2)}) async-start(), calls=%async_computation.5 | async-start | bytes 1179648 | tf_op jit(solution)/shard_map/all_gather | solution.py:252
  10.4 21.6 %copy-start.1 = (bf16[8,4,2048]{2,1,0:T(4,128)(2,1)S(1)}, bf16[8,4,2048]{2,1,0:T(4,128)(2,1)}, u32[]{:S(2)}) copy-start(bf16[8,4,2048]{2,1,0:T(4,128)(2,1)} %param.23) | copy-start | bytes 393220
  13.7 18.3 %copy-start.2 = (s32[8,4,10]{2,1,0:T(4,128)S(1)}, s32[8,4,10]{2,1,0:T(4,128)}, u32[]{:S(2)}) copy-start(s32[8,4,10]{2,1,0:T(4,128)} %param.24) | copy-start | bytes 3844
  32.7 45.5 %copy-start.4 = (f32[2048]{0:T(1024)S(1)}, f32[2048]{0:T(1024)}, u32[]{:S(2)}) copy-start(f32[2048]{0:T(1024)} %param.28) | copy-start | bytes 24580
  64.8 8.8 %all-to-all-start = ((bf16[8,32,256]{2,1,0:T(8,128)(2,1)}), bf16[8,32,256]{2,1,0:T(8,128)(2,1)S(1)}, u32[]{:S(2)}, u32[]{:S(2)}) async-start(bf16[8,32,256]{2,1,0:T(8,128)(2,1)} %bitcast.5), calls=%async_computation | async-start | bytes 262144 | tf_op jit(solution)/shard_map/all_to_all | solution.py:256
  73.7 9.4 %all-to-all-start.3 = ((s32[8,1,1]{2,1,0:T(1,128)}), s32[8,1,1]{2,1,0:T(1,128)S(1)}, u32[]{:S(2)}, u32[]{:S(2)}) async-start(s32[8,1,1]{2,1,0:T(1,128)} %copy.110), calls=%async_computation.3 | async-start | bytes 8192 | tf_op jit(solution)/shard_map/all_to_all | solution.py:246
  171.9 54.2 %all-to-all-start.4 = ((bf16[8,16,128,128]{3,2,1,0:T(8,128)(2,1)}), bf16[8,16,128,128]{3,2,1,0:T(8,128)(2,1)}, u32[]{:S(2)}, u32[]{:S(2)}) async-start(bf16[8,16,128,128]{3,2,1,0:T(8,128)(2,1)} %get-tuple-element.5), calls=%async_computation.4 | async-start | bytes 8388608 | tf_op jit(solution)/shard_map/all_to_all | solution.py:245
  187.9 46.0 %copy-start.3 = (f32[8,4,10]{2,1,0:T(4,128)S(1)}, f32[8,4,10]{2,1,0:T(4,128)}, u32[]{:S(2)}) copy-start(f32[8,4,10]{2,1,0:T(4,128)} %param.25) | copy-start | bytes 3844
  226.1 82.7 %all-to-all-start.2 = ((bf16[256,48,128]{2,1,0:T(8,128)(2,1)}), bf16[256,48,128]{2,1,0:T(8,128)(2,1)}, u32[]{:S(2)}, u32[]{:S(2)}) async-start(bf16[256,48,128]{2,1,0:T(8,128)(2,1)} %copy.105), calls=%async_computation.2 | async-start | bytes 6291456 | tf_op jit(solution)/shard_map/all_to_all | solution.py:291
Sparse Core Ops, SparseCore 0:
  32.1 30.0 all-gather.1

commit v6 on v5

--- a/solution.py
+++ b/solution.py
@@ -172,6 +172,53 @@
     return (memory_state.astype(jnp.bfloat16), jnp.stack(outputs, axis=1))
 
 
+def migrate_kernel(src_hbm, dst_hbm, send_sem, recv_sem, local_sem):
+    lanes = src_hbm.shape[0]
+    group = lax.axis_index("dp")
+    me = lax.axis_index("ep")
+    mesh_ids = pl.DeviceIdType.MESH
+    barrier = pltpu.get_barrier_semaphore()
+    for i in range(1, lanes):
+        pl.semaphore_signal(barrier, 1, device_id=(group, lax.rem(me + i, lanes)), device_id_type=mesh_ids)
+    pl.semaphore_wait(barrier, lanes - 1)
+    own = pltpu.make_async_copy(src_hbm.at[me], dst_hbm.at[me], local_sem)
+    own.start()
+    copies = []
+    for i in range(1, lanes):
+        peer = lax.rem(me + i, lanes)
+        copy = pltpu.make_async_remote_copy(
+            src_hbm.at[peer],
+            dst_hbm.at[me],
+            send_sem.at[i - 1],
+            recv_sem.at[i - 1],
+            device_id=(group, peer),
+            device_id_type=mesh_ids,
+        )
+        copy.start()
+        copies.append(copy)
+    own.wait()
+    for copy in copies:
+        copy.wait()
+
+
+def migrate(rows):
+    lanes = rows.shape[0]
+    any_spec = pl.BlockSpec(memory_space=pl.ANY)
+    return pl.pallas_call(
+        migrate_kernel,
+        in_specs=[any_spec],
+        out_specs=any_spec,
+        out_shape=jax.ShapeDtypeStruct(rows.shape, rows.dtype),
+        scratch_shapes=[
+            pltpu.SemaphoreType.DMA((lanes - 1,)),
+            pltpu.SemaphoreType.DMA((lanes - 1,)),
+            pltpu.SemaphoreType.DMA,
+        ],
+        compiler_params=pltpu.CompilerParams(collective_id=0, has_side_effects=True),
+        cost_estimate=pl.CostEstimate(flops=0, transcendentals=0, bytes_accessed=2 * rows.size * rows.dtype.itemsize),
+    )(rows)
+
+
 def place_kernel(place_ref, in_ref, out_ref):
     out_ref[...] = in_ref[...]
 
@@ -242,7 +289,7 @@
     )
     packed_place = jnp.zeros_like(new_place).at[target].set(new_place)
     received = (
-        lax.all_to_all(fresh_states, "ep", split_axis=0, concat_axis=0, tiled=True),
+        migrate(fresh_states),
         lax.all_to_all(packed_place, "ep", split_axis=0, concat_axis=0, tiled=True),
     )
     moved_out = place_rows(received[0], received[1])

time: 325 us -> 295 us (0.908)
  blocking collectives: 88.8 us -> 0 us
  Pallas kernels: 20.3 us -> 101 us
  waiting for transfers between devices: 137 us -> 106 us
  starting transfers between devices: 20.7 us -> 29.4 us
    all_to_all x1 -> x0, blocking collectives: 88.8 us -> none  [shards(): arrived = lax.all_to_all(outgoing, ('dp', 'ep'), 0, 0, tiled=True)]
    pallas_call x0 -> x1, Pallas kernels: none -> 80.4 us  [migrate(): pl.pallas_call(migrate_kernel, in_specs=[any_spec], out_specs=any_spec, o...]
    all_to_all x1, waiting for transfers between devices: 66.4 us -> 0.01 us  [shards(): returned = lax.all_to_all(result, ('dp', 'ep'), 0, 0, tiled=True)]
    all_to_all x1, waiting for transfers between devices: 38.1 us -> 72.2 us  [shards(): arrived = lax.all_to_all(outgoing, ('dp', 'ep'), 0, 0, tiled=True)]
    all_to_all x1, starting transfers between devices: 5.28 us -> 12.4 us  [shards(): arrived = lax.all_to_all(outgoing, ('dp', 'ep'), 0, 0, tiled=True)]
  transfers between devices with their start and end apart: 5 -> 5, of which waited for: 4 -> 3; matrix products, arithmetic and copies ran while one was open for 6% -> 5% of each run, Pallas kernels for 2% -> 30%
where the time goes in v6:
time: 295 us; the launch traced here: 294 us
  waiting for transfers between devices  106 us (36%)
  Pallas kernels  101 us (34%)
  starting transfers between devices  29.4 us (10%)
  local copies, waits for them, and re-layouts  23 us (8%)
  between operations  14.4 us (5%)
  matrix products  14.1 us (5%)
  other arithmetic  5.88 us (2%)
    pallas_call x1, Pallas kernels, migrate(): pl.pallas_call(migrate_kernel, in_specs=[any_spec], out_specs=any_spec, o...  80.4 us
    all_to_all x1, waiting for transfers between devices, shards(): arrived = lax.all_to_all(outgoing, ('dp', 'ep'), 0, 0, tiled=True)  72.2 us
    all_gather x1, waiting for transfers between devices, shards(): lax.all_gather(core_flat, 'ep', axis=0, tiled=True)  28.9 us
    pallas_call x1, Pallas kernels, recurrence(): pl.pallas_call(recur_kernel, grid_spec=pltpu.PrefetchScalarGridSpec(num_s...  13 us
    all_to_all x1, starting transfers between devices, shards(): arrived = lax.all_to_all(outgoing, ('dp', 'ep'), 0, 0, tiled=True)  12.4 us
    all_to_all x1, starting transfers between devices, shards(): returned = lax.all_to_all(result, ('dp', 'ep'), 0, 0, tiled=True)  8.48 us
    pallas_call x1, Pallas kernels, place_rows(): pl.pallas_call(place_kernel, grid_spec=pltpu.PrefetchScalarGridSpec(num_s...  7.26 us
  transfers between devices with their start and end apart: 5, of which 3 were waited for; matrix products, arithmetic and copies ran while one was open for 5% of the time, Pallas kernels for 30%

profile of v6, /device:TPU:1, one launch (start us, length us, event | category | flops | bytes accessed | tf_op | source)
XLA Modules:
  0.0 293.6 jit_solution(9466952563594424692)
XLA Ops:
  7.2 1.4 compare_select_fusion.1
  8.6 0.9 reshape.147
  9.5 0.9 reshape.148
  10.4 1.7 reshape.149.v_ref
  12.1 1.6 reshape.150.g_ref
  14.5 0.7 copy.92
  15.9 0.7 copy.94
  16.7 0.7 broadcast_in_dim.12
  17.4 13.0 %shard_map.167 = (bf16[8,16,128,128]{3,2,1,0:T(8,128)(2,1)}, bf16[8,4,16,128]{3,2,1,0:T(8,128)(2,1)}) custom-call(s32[8]{0:T(128)} %get-tuple-element.7.slot_ref, bf16[8,16,128,128]{3,2,1,0:T(8,128)(2,1)} %s_ref.1, bf16[8,128,128]{2,1,0:T(8,128)(2,1)} %bitcast.88, bf16[8,4,16,128]{3,2,1,0:T(8,128)(2,1)} %reshape.149.v_ref, ...), custom_call_target="tpu_custom_call" | custom-call | tf_op jit(solution)/shard_map/pallas_call | solution.py:104
  30.4 1.6 copy.148
  33.3 28.9 %all-gather.2.cloned.1.call-done = bf16[256,2048]{1,0:T(8,128)(2,1)} async-done(((bf16[32,2048]{1,0:T(8,128)(2,1)}), bf16[256,2048]{1,0:T(8,128)(2,1)}) %all-gather.2.cloned.1.call-update) | async-done | bytes 1048592 | tf_op jit(solution)/shard_map/all_gather | solution.py:299
  62.3 2.6 convolution_convert_fusion.2
  64.9 3.5 %all-to-all-start = ((bf16[8,32,256]{2,1,0:T(8,128)(2,1)}), bf16[8,32,256]{2,1,0:T(8,128)(2,1)S(1)}, u32[]{:S(2)}, u32[]{:S(2)}) async-start(bf16[8,32,256]{2,1,0:T(8,128)(2,1)} %bitcast.5), calls=%async_computation | async-start | bytes 262144 | tf_op jit(solution)/shard_map/all_to_all | solution.py:303
  68.6 5.1 %all-to-all-done = bf16[8,32,256]{2,1,0:T(8,128)(2,1)S(1)} async-done(((bf16[8,32,256]{2,1,0:T(8,128)(2,1)}), bf16[8,32,256]{2,1,0:T(8,128)(2,1)S(1)}, u32[]{:S(2)}, u32[]{:S(2)}) %all-to-all-start) | async-done | bytes 131104 | tf_op jit(solution)/shard_map/all_to_all | solution.py:303
  74.4 1.0 convolution_convert_fusion
  75.5 3.7 %copy.102 = bf16[256,48,128]{2,1,0:T(8,128)(2,1)} copy(bf16[256,48,128]{2,0,1:T(8,128)(2,1)S(1)} %bitcast.81) | data formatting | bytes 6291456 | tf_op jit(solution)/shard_map/reshape | solution.py:326
  79.2 12.4 %all-to-all-start.1 = ((bf16[256,48,128]{2,1,0:T(8,128)(2,1)}), bf16[256,48,128]{2,1,0:T(8,128)(2,1)}, u32[]{:S(2)}, u32[]{:S(2)}) async-start(bf16[256,48,128]{2,1,0:T(8,128)(2,1)} %copy.102), calls=%async_computation.1 | async-start | bytes 6291456 | tf_op jit(solution)/shard_map/all_to_all | solution.py:327
  91.6 1.2 copy.118
  94.3 72.2 %all-to-all-done.1 = bf16[256,48,128]{2,1,0:T(8,128)(2,1)} async-done(((bf16[256,48,128]{2,1,0:T(8,128)(2,1)}), bf16[256,48,128]{2,1,0:T(8,128)(2,1)}, u32[]{:S(2)}, u32[]{:S(2)}) %all-to-all-start.1) | async-done | bytes 3145760 | tf_op jit(solution)/shard_map/all_to_all | solution.py:327
  166.4 4.9 %all-to-all-start.3 = ((s32[8,1,1]{2,1,0:T(1,128)}), s32[8,1,1]{2,1,0:T(1,128)S(1)}, u32[]{:S(2)}, u32[]{:S(2)}) async-start(s32[8,1,1]{2,1,0:T(1,128)} %copy.110), calls=%async_computation.3 | async-start | bytes 8192 | tf_op jit(solution)/shard_map/all_to_all | solution.py:293
  171.4 2.7 copy.103
  174.1 1.8 convolution_bitcast_fusion
  175.9 1.1 convolution_convert_fusion.1
  177.0 3.7 %copy.105 = bf16[256,48,128]{2,1,0:T(8,128)(2,1)} copy(bf16[256,48,128]{2,0,1:T(8,128)(2,1)S(1)} %bitcast.82) | data formatting | bytes 6291456 | tf_op jit(solution)/shard_map/reshape | solution.py:337
  180.7 8.5 %all-to-all-start.2 = ((bf16[256,48,128]{2,1,0:T(8,128)(2,1)}), bf16[256,48,128]{2,1,0:T(8,128)(2,1)}, u32[]{:S(2)}, u32[]{:S(2)}) async-start(bf16[256,48,128]{2,1,0:T(8,128)(2,1)} %copy.105), calls=%async_computation.2 | async-start | bytes 6291456 | tf_op jit(solution)/shard_map/all_to_all | solution.py:338
  189.5 80.4 %shard_map.168.in_ref = bf16[8,16,128,128]{3,2,1,0:T(8,128)(2,1)} custom-call(bf16[8,16,128,128]{3,2,1,0:T(8,128)(2,1)} %get-tuple-element.5.src_hbm), custom_call_target="tpu_custom_call" | custom-call | bytes 8388608 | tf_op jit(solution)/shard_map/pallas_call | solution.py:207
  270.1 0.8 reduce.2.place_ref
  270.8 7.3 %shard_map.169 = bf16[8,16,128,128]{3,2,1,0:T(8,128)(2,1)} custom-call(s32[8]{0:T(128)} %reduce.2.place_ref, bf16[8,16,128,128]{3,2,1,0:T(8,128)(2,1)} %shard_map.168.in_ref), custom_call_target="tpu_custom_call" | custom-call | tf_op jit(solution)/shard_map/pallas_call | solution.py:229
  278.1 2.5 fusion.6
  280.6 2.5 fusion.18
  283.2 2.5 fusion.15
  286.0 0.8 fusion.31
  (56 shorter events, 5.7 us)
Async XLA Ops:
  7.2 166.9 %copy-start = (bf16[1,2048,512]{2,1,0:T(8,128)(2,1)S(1)}, bf16[1,2048,512]{2,1,0:T(8,128)(2,1)}, u32[]{:S(2)}) copy-start(bf16[1,2048,512]{2,1,0:T(8,128)(2,1)} %param.29) | copy-start | bytes 6291460
  7.2 55.1 %all-gather.2.cloned.1.call-start = ((), (), s32[]{:S(2)}) async-start(), calls=%async_computation.4 | async-start | bytes 1179648 | tf_op jit(solution)/shard_map/all_gather | solution.py:299
  10.4 21.6 %copy-start.1 = (bf16[8,4,2048]{2,1,0:T(4,128)(2,1)S(1)}, bf16[8,4,2048]{2,1,0:T(4,128)(2,1)}, u32[]{:S(2)}) copy-start(bf16[8,4,2048]{2,1,0:T(4,128)(2,1)} %param.23) | copy-start | bytes 393220
  13.8 18.3 %copy-start.4 = (s32[8,4,10]{2,1,0:T(4,128)S(1)}, s32[8,4,10]{2,1,0:T(4,128)}, u32[]{:S(2)}) copy-start(s32[8,4,10]{2,1,0:T(4,128)} %param.24) | copy-start | bytes 3844
  32.8 41.5 %copy-start.6 = (f32[2048]{0:T(1024)S(1)}, f32[2048]{0:T(1024)}, u32[]{:S(2)}) copy-start(f32[2048]{0:T(1024)} %param.28) | copy-start | bytes 24580
  64.9 8.8 %all-to-all-start = ((bf16[8,32,256]{2,1,0:T(8,128)(2,1)}), bf16[8,32,256]{2,1,0:T(8,128)(2,1)S(1)}, u32[]{:S(2)}, u32[]{:S(2)}) async-start(bf16[8,32,256]{2,1,0:T(8,128)(2,1)} %bitcast.5), calls=%async_computation | async-start | bytes 262144 | tf_op jit(solution)/shard_map/all_to_all | solution.py:303
  79.2 12.4 %copy-start.2 = (bf16[1,256,2048]{2,1,0:T(8,128)(2,1)S(1)}, bf16[1,256,2048]{2,1,0:T(8,128)(2,1)}, u32[]{:S(2)}) copy-start(bf16[1,256,2048]{2,1,0:T(8,128)(2,1)} %param.30) | copy-start | bytes 3145732
  79.2 87.2 %all-to-all-start.1 = ((bf16[256,48,128]{2,1,0:T(8,128)(2,1)}), bf16[256,48,128]{2,1,0:T(8,128)(2,1)}, u32[]{:S(2)}, u32[]{:S(2)}) async-start(bf16[256,48,128]{2,1,0:T(8,128)(2,1)} %copy.102), calls=%async_computation.1 | async-start | bytes 6291456 | tf_op jit(solution)/shard_map/all_to_all | solution.py:327
  166.4 14.3 %all-to-all-start.3 = ((s32[8,1,1]{2,1,0:T(1,128)}), s32[8,1,1]{2,1,0:T(1,128)S(1)}, u32[]{:S(2)}, u32[]{:S(2)}) async-start(s32[8,1,1]{2,1,0:T(1,128)} %copy.110), calls=%async_computation.3 | async-start | bytes 8192 | tf_op jit(solution)/shard_map/all_to_all | solution.py:293
  174.1 1.8 copy-start.3
  180.7 8.5 %copy-start.5 = (f32[8,4,10]{2,1,0:T(4,128)S(1)}, f32[8,4,10]{2,1,0:T(4,128)}, u32[]{:S(2)}) copy-start(f32[8,4,10]{2,1,0:T(4,128)} %param.25) | copy-start | bytes 3844
  180.7 97.4 %all-to-all-start.2 = ((bf16[256,48,128]{2,1,0:T(8,128)(2,1)}), bf16[256,48,128]{2,1,0:T(8,128)(2,1)}, u32[]{:S(2)}, u32[]{:S(2)}) async-start(bf16[256,48,128]{2,1,0:T(8,128)(2,1)} %copy.105), calls=%async_computation.2 | async-start | bytes 6291456 | tf_op jit(solution)/shard_map/all_to_all | solution.py:338
Sparse Core Ops, SparseCore 0:
  32.1 30.1 all-gather.1

commit v7 on v6

--- a/solution.py
+++ b/solution.py
@@ -219,6 +219,72 @@
     )(rows)
 
 
+def project_kernel(rows_ref, weight_ref, out_ref, gathered, product, send_a, recv_a, send_b, recv_b, local_sem):
+    lanes = gathered.shape[0]
+    count = rows_ref.shape[0]
+    block = weight_ref.shape[1]
+    group = lax.axis_index("dp")
+    me = lax.axis_index("ep")
+    mesh_ids = pl.DeviceIdType.MESH
+    barrier = pltpu.get_barrier_semaphore()
+    for i in range(1, lanes):
+        pl.semaphore_signal(barrier, 1, device_id=(group, lax.rem(me + i, lanes)), device_id_type=mesh_ids)
+    pl.semaphore_wait(barrier, lanes - 1)
+    own = pltpu.make_async_copy(rows_ref, gathered.at[me], local_sem)
+    own.start()
+    sends = []
+    for i in range(1, lanes):
+        copy = pltpu.make_async_remote_copy(
+            rows_ref, gathered.at[me], send_a.at[i - 1], recv_a.at[i - 1],
+            device_id=(group, lax.rem(me + i, lanes)), device_id_type=mesh_ids,
+        )
+        copy.start()
+        sends.append(copy)
+    own.wait()
+    for copy in sends:
+        copy.wait()
+    for j in range(lanes):
+        product[j] = jnp.dot(gathered[j], weight_ref[...], preferred_element_type=jnp.float32).astype(product.dtype)
+    columns = pl.ds(pl.multiple_of(me * block, block), block)
+    back = pltpu.make_async_copy(product.at[me], out_ref.at[:, columns], local_sem)
+    back.start()
+    replies = []
+    for i in range(1, lanes):
+        peer = lax.rem(me + i, lanes)
+        copy = pltpu.make_async_remote_copy(
+            product.at[peer], out_ref.at[:, columns], send_b.at[i - 1], recv_b.at[i - 1],
+            device_id=(group, peer), device_id_type=mesh_ids,
+        )
+        copy.start()
+        replies.append(copy)
+    back.wait()
+    for copy in replies:
+        copy.wait()
+
+
+def project(rows, weight):
+    lanes = lax.axis_size("ep")
+    count, width = rows.shape
+    block = weight.shape[1]
+    vmem = pl.BlockSpec(memory_space=pltpu.VMEM)
+    return pl.pallas_call(
+        project_kernel,
+        in_specs=[vmem, vmem],
+        out_specs=vmem,
+        out_shape=jax.ShapeDtypeStruct((count, lanes * block), rows.dtype),
+        scratch_shapes=[
+            pltpu.VMEM((lanes, count, width), rows.dtype),
+            pltpu.VMEM((lanes, count, block), rows.dtype),
+            pltpu.SemaphoreType.DMA((lanes - 1,)),
+            pltpu.SemaphoreType.DMA((lanes - 1,)),
+            pltpu.SemaphoreType.DMA((lanes - 1,)),
+            pltpu.SemaphoreType.DMA((lanes - 1,)),
+            pltpu.SemaphoreType.DMA,
+        ],
+        compiler_params=pltpu.CompilerParams(collective_id=1, has_side_effects=True),
+    )(rows, weight)
+
+
 def place_kernel(place_ref, in_ref, out_ref):
     out_ref[...] = in_ref[...]
 
@@ -295,12 +361,7 @@
     moved_out = place_rows(received[0], received[1])
     token_count = req_count * step_count
     core_flat = core_out.reshape(token_count, core_out.shape[-1])
-    columns = jnp.dot(
-        lax.all_gather(core_flat, "ep", axis=0, tiled=True),
-        out_weight,
-        preferred_element_type=jnp.float32,
-    ).astype(jnp.bfloat16)
-    attention = lax.all_to_all(columns, "ep", split_axis=0, concat_axis=1, tiled=True)
+    attention = project(core_flat, out_weight)
     hidden = (
         residual.reshape(token_count, model_width).astype(jnp.float32)
         + attention.astype(jnp.float32)

time: 295 us -> 263 us (0.89)
  waiting for transfers between devices: 106 us -> 72.3 us
  Pallas kernels: 101 us -> 126 us
  between operations: 14.4 us -> 0.98 us
    all_gather x1 -> x0, waiting for transfers between devices: 28.9 us -> none  [shards(): lax.all_gather(core_flat, 'ep', axis=0, tiled=True)]
    pallas_call x0 -> x1, Pallas kernels: none -> 25 us  [project(): pl.pallas_call(project_kernel, in_specs=[vmem, vmem], out_specs=vmem, out...]
    all_to_all x1 -> x0, waiting for transfers between devices: 5.08 us -> none  [shards(): lax.all_to_all(columns, 'ep', split_axis=0, concat_axis=1, tiled=True)]
    all_to_all x1 -> x0, starting transfers between devices: 3.52 us -> none  [shards(): lax.all_to_all(columns, 'ep', split_axis=0, concat_axis=1, tiled=True)]
  transfers between devices with their start and end apart: 5 -> 3, of which waited for: 3 -> 1; matrix products, arithmetic and copies ran while one was open for 5% -> 5% of each run, Pallas kernels for 30% -> 33%
where the time goes in v7:
time: 263 us; the launch traced here: 262 us
  Pallas kernels  126 us (48%)
  waiting for transfers between devices  72.3 us (27%)
  starting transfers between devices  27 us (10%)
  local copies, waits for them, and re-layouts  20.3 us (8%)
  matrix products  11.5 us (4%)
  other arithmetic  4.39 us (2%)
    pallas_call x1, Pallas kernels, migrate(): pl.pallas_call(migrate_kernel, in_specs=[any_spec], out_specs=any_spec, o...  80.4 us
    all_to_all x1, waiting for transfers between devices, shards(): arrived = lax.all_to_all(outgoing, ('dp', 'ep'), 0, 0, tiled=True)  72.3 us
    pallas_call x1, Pallas kernels, project(): pl.pallas_call(project_kernel, in_specs=[vmem, vmem], out_specs=vmem, out...  25 us
    all_to_all x1, starting transfers between devices, shards(): arrived = lax.all_to_all(outgoing, ('dp', 'ep'), 0, 0, tiled=True)  13.6 us
    pallas_call x1, Pallas kernels, recurrence(): pl.pallas_call(recur_kernel, grid_spec=pltpu.PrefetchScalarGridSpec(num_s...  13.1 us
    all_to_all x1, starting transfers between devices, shards(): returned = lax.all_to_all(result, ('dp', 'ep'), 0, 0, tiled=True)  8.48 us
    pallas_call x1, Pallas kernels, place_rows(): pl.pallas_call(place_kernel, grid_spec=pltpu.PrefetchScalarGridSpec(num_s...  7.26 us
  transfers between devices with their start and end apart: 3, of which 1 were waited for; matrix products, arithmetic and copies ran while one was open for 5% of the time, Pallas kernels for 33%

profile of v7, /device:TPU:1, one launch (start us, length us, event | category | flops | bytes accessed | tf_op | source)
XLA Modules:
  0.0 262.2 jit_solution(7715241241358768959)
XLA Ops:
  0.7 1.0 eq.45
  1.7 0.7 broadcast_multiply_fusion
  3.5 0.5 compare_select_fusion.1
  4.2 0.7 reshape.122.v_ref
  5.0 0.7 reshape.123.g_ref
  5.7 0.7 copy.85
  6.5 0.7 copy.87
  7.2 0.7 broadcast_in_dim.12
  8.0 13.1 %shard_map.167 = (bf16[8,16,128,128]{3,2,1,0:T(8,128)(2,1)}, bf16[8,4,16,128]{3,2,1,0:T(8,128)(2,1)}) custom-call(s32[8]{0:T(128)} %get-tuple-element.7.slot_ref, bf16[8,16,128,128]{3,2,1,0:T(8,128)(2,1)} %s_ref.1, bf16[8,128,128]{2,1,0:T(8,128)(2,1)} %bitcast.95, bf16[8,4,16,128]{3,2,1,0:T(8,128)(2,1)} %reshape.122.v_ref, ...), custom_call_target="tpu_custom_call" | custom-call | tf_op jit(solution)/shard_map/pallas_call | solution.py:104
  21.1 1.6 copy.144
  22.7 25.0 %shard_map.168 = bf16[32,2048]{1,0:T(8,128)(2,1)} custom-call(bf16[32,2048]{1,0:T(8,128)(2,1)} %bitcast.96, bf16[2048,256]{1,0:T(8,128)(2,1)} %weight_ref.1), custom_call_target="tpu_custom_call" | custom-call | tf_op jit(solution)/shard_map/pallas_call | solution.py:270
  47.7 1.1 fusion.33
  49.0 1.0 convolution_convert_fusion
  50.0 3.7 %copy.93 = bf16[256,48,128]{2,1,0:T(8,128)(2,1)} copy(bf16[256,48,128]{2,0,1:T(8,128)(2,1)S(1)} %bitcast.88) | data formatting | bytes 6291456 | tf_op jit(solution)/shard_map/reshape | solution.py:387
  53.8 13.6 %all-to-all-start = ((bf16[256,48,128]{2,1,0:T(8,128)(2,1)}), bf16[256,48,128]{2,1,0:T(8,128)(2,1)}, u32[]{:S(2)}, u32[]{:S(2)}) async-start(bf16[256,48,128]{2,1,0:T(8,128)(2,1)} %copy.93), calls=%async_computation | async-start | bytes 6291456 | tf_op jit(solution)/shard_map/all_to_all | solution.py:388
  67.4 1.2 copy.111
  68.6 0.6 scatter_custom_fusion
  69.2 0.7 copy.101
  69.9 72.3 %all-to-all-done = bf16[256,48,128]{2,1,0:T(8,128)(2,1)} async-done(((bf16[256,48,128]{2,1,0:T(8,128)(2,1)}), bf16[256,48,128]{2,1,0:T(8,128)(2,1)}, u32[]{:S(2)}, u32[]{:S(2)}) %all-to-all-start) | async-done | bytes 3145760 | tf_op jit(solution)/shard_map/all_to_all | solution.py:388
  142.2 4.9 %all-to-all-start.2 = ((s32[8,1,1]{2,1,0:T(1,128)}), s32[8,1,1]{2,1,0:T(1,128)S(1)}, u32[]{:S(2)}, u32[]{:S(2)}) async-start(s32[8,1,1]{2,1,0:T(1,128)} %copy.101), calls=%async_computation.2 | async-start | bytes 8192 | tf_op jit(solution)/shard_map/all_to_all | solution.py:359
  147.2 2.7 %copy.94 = bf16[256,48,128]{2,0,1:T(8,128)(2,1)S(1)} copy(bf16[256,48,128]{2,1,0:T(8,128)(2,1)} %all-to-all-done) | data formatting | bytes 6291456 | tf_op jit(solution)/shard_map/all_to_all | solution.py:388
  149.9 1.8 convolution_bitcast_fusion
  151.7 1.1 convolution_convert_fusion.1
  152.7 3.7 %copy.96 = bf16[256,48,128]{2,1,0:T(8,128)(2,1)} copy(bf16[256,48,128]{2,0,1:T(8,128)(2,1)S(1)} %bitcast.89) | data formatting | bytes 6291456 | tf_op jit(solution)/shard_map/reshape | solution.py:398
  156.5 8.5 %all-to-all-start.1 = ((bf16[256,48,128]{2,1,0:T(8,128)(2,1)}), bf16[256,48,128]{2,1,0:T(8,128)(2,1)}, u32[]{:S(2)}, u32[]{:S(2)}) async-start(bf16[256,48,128]{2,1,0:T(8,128)(2,1)} %copy.96), calls=%async_computation.1 | async-start | bytes 6291456 | tf_op jit(solution)/shard_map/all_to_all | solution.py:399
  165.2 80.4 %shard_map.169.in_ref = bf16[8,16,128,128]{3,2,1,0:T(8,128)(2,1)} custom-call(bf16[8,16,128,128]{3,2,1,0:T(8,128)(2,1)} %get-tuple-element.5.src_hbm), custom_call_target="tpu_custom_call" | custom-call | bytes 8388608 | tf_op jit(solution)/shard_map/pallas_call | solution.py:207
  245.8 0.8 reduce.1.place_ref
  246.6 7.3 %shard_map.170 = bf16[8,16,128,128]{3,2,1,0:T(8,128)(2,1)} custom-call(s32[8]{0:T(128)} %reduce.1.place_ref, bf16[8,16,128,128]{3,2,1,0:T(8,128)(2,1)} %shard_map.169.in_ref), custom_call_target="tpu_custom_call" | custom-call | tf_op jit(solution)/shard_map/pallas_call | solution.py:295
  253.9 2.5 fusion.6
  256.4 2.5 fusion.21
  258.9 2.5 fusion.18
  261.5 0.7 reshape.134
  (56 shorter events, 1.9 us)
Async XLA Ops:
  0.6 149.2 %copy-start = (bf16[1,2048,512]{2,1,0:T(8,128)(2,1)S(1)}, bf16[1,2048,512]{2,1,0:T(8,128)(2,1)}, u32[]{:S(2)}) copy-start(bf16[1,2048,512]{2,1,0:T(8,128)(2,1)} %param.29) | copy-start | bytes 6291460
  0.6 2.9 %copy-start.12 = (s32[8]{0:T(128)S(1)}, s32[8]{0:T(128)}, u32[]{:S(2)}) copy-start(s32[8]{0:T(128)} %param.31) | copy-start | bytes 100
  0.7 3.4 %copy-start.6 = (bf16[8,4,1024]{2,1,0:T(4,128)(2,1)S(1)}, bf16[8,4,1024]{2,1,0:T(4,128)(2,1)}, u32[]{:S(2)}) copy-start(bf16[8,4,1024]{2,1,0:T(4,128)(2,1)} %param.18) | copy-start | bytes 196612
  0.7 3.4 %copy-start.7 = (bf16[8,4,1024]{2,1,0:T(4,128)(2,1)S(1)}, bf16[8,4,1024]{2,1,0:T(4,128)(2,1)}, u32[]{:S(2)}) copy-start(bf16[8,4,1024]{2,1,0:T(4,128)(2,1)} %param.17) | copy-start | bytes 196612
  0.7 3.5 %copy-start.4 = (bf16[8,4,2048]{2,1,0:T(4,128)(2,1)S(1)}, bf16[8,4,2048]{2,1,0:T(4,128)(2,1)}, u32[]{:S(2)}) copy-start(bf16[8,4,2048]{2,1,0:T(4,128)(2,1)} %param.19) | copy-start | bytes 393220
  0.7 4.3 %copy-start.5 = (bf16[8,4,2048]{2,1,0:T(4,128)(2,1)S(1)}, bf16[8,4,2048]{2,1,0:T(4,128)(2,1)}, u32[]{:S(2)}) copy-start(bf16[8,4,2048]{2,1,0:T(4,128)(2,1)} %param.20) | copy-start | bytes 393220
  0.7 5.0 %copy-start.10 = (bf16[8,4,16]{2,1,0:T(4,128)(2,1)S(1)}, bf16[8,4,16]{2,1,0:T(4,128)(2,1)}, u32[]{:S(2)}) copy-start(bf16[8,4,16]{2,1,0:T(4,128)(2,1)} %param.22) | copy-start | bytes 3076
  0.7 5.8 %copy-start.11 = (bf16[8,4,16]{2,1,0:T(4,128)(2,1)S(1)}, bf16[8,4,16]{2,1,0:T(4,128)(2,1)}, u32[]{:S(2)}) copy-start(bf16[8,4,16]{2,1,0:T(4,128)(2,1)} %param.21) | copy-start | bytes 3076
  4.2 18.5 %copy-start.3 = (bf16[8,4,2048]{2,1,0:T(4,128)(2,1)S(1)}, bf16[8,4,2048]{2,1,0:T(4,128)(2,1)}, u32[]{:S(2)}) copy-start(bf16[8,4,2048]{2,1,0:T(4,128)(2,1)} %param.23) | copy-start | bytes 393220
  8.0 41.0 %copy-start.9 = (f32[2048]{0:T(1024)S(1)}, f32[2048]{0:T(1024)}, u32[]{:S(2)}) copy-start(f32[2048]{0:T(1024)} %param.28) | copy-start | bytes 24580
  53.8 13.6 %copy-start.1 = (bf16[1,256,2048]{2,1,0:T(8,128)(2,1)S(1)}, bf16[1,256,2048]{2,1,0:T(8,128)(2,1)}, u32[]{:S(2)}) copy-start(bf16[1,256,2048]{2,1,0:T(8,128)(2,1)} %param.30) | copy-start | bytes 3145732
  53.8 88.4 %all-to-all-start = ((bf16[256,48,128]{2,1,0:T(8,128)(2,1)}), bf16[256,48,128]{2,1,0:T(8,128)(2,1)}, u32[]{:S(2)}, u32[]{:S(2)}) async-start(bf16[256,48,128]{2,1,0:T(8,128)(2,1)} %copy.93), calls=%async_computation | async-start | bytes 6291456 | tf_op jit(solution)/shard_map/all_to_all | solution.py:388
  142.2 14.3 %all-to-all-start.2 = ((s32[8,1,1]{2,1,0:T(1,128)}), s32[8,1,1]{2,1,0:T(1,128)S(1)}, u32[]{:S(2)}, u32[]{:S(2)}) async-start(s32[8,1,1]{2,1,0:T(1,128)} %copy.101), calls=%async_computation.2 | async-start | bytes 8192 | tf_op jit(solution)/shard_map/all_to_all | solution.py:359
  149.9 1.8 copy-start.2
  156.5 8.5 %copy-start.8 = (f32[8,4,10]{2,1,0:T(4,128)S(1)}, f32[8,4,10]{2,1,0:T(4,128)}, u32[]{:S(2)}) copy-start(f32[8,4,10]{2,1,0:T(4,128)} %param.25) | copy-start | bytes 3844
  156.5 97.4 %all-to-all-start.1 = ((bf16[256,48,128]{2,1,0:T(8,128)(2,1)}), bf16[256,48,128]{2,1,0:T(8,128)(2,1)}, u32[]{:S(2)}, u32[]{:S(2)}) async-start(bf16[256,48,128]{2,1,0:T(8,128)(2,1)} %copy.96), calls=%async_computation.1 | async-start | bytes 6291456 | tf_op jit(solution)/shard_map/all_to_all | solution.py:399

commit v8 on v7

--- a/solution.py
+++ b/solution.py
@@ -243,8 +243,13 @@
     own.wait()
     for copy in sends:
         copy.wait()
-    for j in range(lanes):
-        product[j] = jnp.dot(gathered[j], weight_ref[...], preferred_element_type=jnp.float32).astype(product.dtype)
+    width = gathered.shape[-1]
+    stacked = gathered[...].reshape(lanes * count, width)
+    product[...] = (
+        jnp.dot(stacked, weight_ref[...], preferred_element_type=jnp.float32)
+        .astype(product.dtype)
+        .reshape(lanes, count, block)
+    )
     columns = pl.ds(pl.multiple_of(me * block, block), block)
     back = pltpu.make_async_copy(product.at[me], out_ref.at[:, columns], local_sem)
     back.start()
@@ -405,11 +410,9 @@
     rest = spread - high.astype(jnp.float32)
     middle = rest.astype(jnp.bfloat16)
     low = (rest - middle.astype(jnp.float32)).astype(jnp.bfloat16)
-    combine = "esk,escl->kcl"
-    combined = (
-        jnp.einsum(combine, high, returned, preferred_element_type=jnp.float32)
-        + jnp.einsum(combine, middle, returned, preferred_element_type=jnp.float32)
-    ) + jnp.einsum(combine, low, returned, preferred_element_type=jnp.float32)
+    parts = jnp.concatenate([high, middle, low], axis=-1)
+    combined = jnp.einsum("esk,escl->kcl", parts, returned, preferred_element_type=jnp.float32)
+    combined = combined.reshape(3, token_count, chunks, lane_count).sum(axis=0)
     combined = combined.reshape(token_count, model_width)
     mixed_out = (
         (hidden.astype(jnp.float32) + combined)

time: 263 us -> 257 us (0.977)
  matrix products: 11.5 us -> 6.45 us
    dot_general x3 -> x1, matrix products: 7.6 us -> 2.56 us  [shards(): jnp.einsum('esk,escl->kcl', parts, returned, preferred_element_type=jnp.f...]
  transfers between devices with their start and end apart: 3 -> 3, of which waited for: 1 -> 1; matrix products, arithmetic and copies ran while one was open for 5% -> 5% of each run, Pallas kernels for 33% -> 34%
where the time goes in v8:
time: 257 us; the launch traced here: 256 us
  Pallas kernels  125 us (49%)
  waiting for transfers between devices  72.3 us (28%)
  starting transfers between devices  27 us (11%)
  local copies, waits for them, and re-layouts  20.3 us (8%)
  matrix products  6.45 us (3%)
  other arithmetic  4.42 us (2%)
    pallas_call x1, Pallas kernels, migrate(): pl.pallas_call(migrate_kernel, in_specs=[any_spec], out_specs=any_spec, o...  80.4 us
    all_to_all x1, waiting for transfers between devices, shards(): arrived = lax.all_to_all(outgoing, ('dp', 'ep'), 0, 0, tiled=True)  72.3 us
    pallas_call x1, Pallas kernels, project(): pl.pallas_call(project_kernel, in_specs=[vmem, vmem], out_specs=vmem, out...  23.9 us
    all_to_all x1, starting transfers between devices, shards(): arrived = lax.all_to_all(outgoing, ('dp', 'ep'), 0, 0, tiled=True)  13.6 us
    pallas_call x1, Pallas kernels, recurrence(): pl.pallas_call(recur_kernel, grid_spec=pltpu.PrefetchScalarGridSpec(num_s...  13.1 us
    all_to_all x1, starting transfers between devices, shards(): returned = lax.all_to_all(result, ('dp', 'ep'), 0, 0, tiled=True)  8.48 us
    pallas_call x1, Pallas kernels, place_rows(): pl.pallas_call(place_kernel, grid_spec=pltpu.PrefetchScalarGridSpec(num_s...  7.26 us
  transfers between devices with their start and end apart: 3, of which 1 were waited for; matrix products, arithmetic and copies ran while one was open for 5% of the time, Pallas kernels for 34%

profile of v8, /device:TPU:1, one launch (start us, length us, event | category | flops | bytes accessed | tf_op | source)
XLA Modules:
  0.0 256.1 jit_solution(15361334341459217017)
XLA Ops:
  0.7 1.0 eq.45
  1.7 0.7 broadcast_multiply_fusion
  2.6 0.3 fusion.13
  3.1 0.2 fusion.17
  3.5 0.5 compare_select_fusion.1
  4.2 0.7 reshape.124.v_ref
  5.0 0.7 reshape.125.g_ref
  5.7 0.7 copy.79
  6.5 0.7 copy.81
  7.2 0.7 broadcast_in_dim.12
  8.0 13.1 %shard_map.167 = (bf16[8,16,128,128]{3,2,1,0:T(8,128)(2,1)}, bf16[8,4,16,128]{3,2,1,0:T(8,128)(2,1)}) custom-call(s32[8]{0:T(128)} %get-tuple-element.7.slot_ref, bf16[8,16,128,128]{3,2,1,0:T(8,128)(2,1)} %s_ref.1, bf16[8,128,128]{2,1,0:T(8,128)(2,1)} %bitcast.89, bf16[8,4,16,128]{3,2,1,0:T(8,128)(2,1)} %reshape.124.v_ref, ...), custom_call_target="tpu_custom_call" | custom-call | tf_op jit(solution)/shard_map/pallas_call | solution.py:104
  21.1 1.6 copy.130
  22.7 23.9 %shard_map.168 = bf16[32,2048]{1,0:T(8,128)(2,1)} custom-call(bf16[32,2048]{1,0:T(8,128)(2,1)} %bitcast.90, bf16[2048,256]{1,0:T(8,128)(2,1)} %weight_ref.1), custom_call_target="tpu_custom_call" | custom-call | tf_op jit(solution)/shard_map/pallas_call | solution.py:275
  46.6 1.1 fusion.18
  47.9 1.0 convolution_convert_fusion
  48.9 3.7 %copy.87 = bf16[256,48,128]{2,1,0:T(8,128)(2,1)} copy(bf16[256,48,128]{2,0,1:T(8,128)(2,1)S(1)} %bitcast.82) | data formatting | bytes 6291456 | tf_op jit(solution)/shard_map/reshape | solution.py:392
  52.7 13.6 %all-to-all-start = ((bf16[256,48,128]{2,1,0:T(8,128)(2,1)}), bf16[256,48,128]{2,1,0:T(8,128)(2,1)}, u32[]{:S(2)}, u32[]{:S(2)}) async-start(bf16[256,48,128]{2,1,0:T(8,128)(2,1)} %copy.87), calls=%async_computation | async-start | bytes 6291456 | tf_op jit(solution)/shard_map/all_to_all | solution.py:393
  66.3 1.2 copy.105
  67.5 0.6 scatter_custom_fusion
  68.1 0.7 copy.94
  68.8 72.3 %all-to-all-done = bf16[256,48,128]{2,1,0:T(8,128)(2,1)} async-done(((bf16[256,48,128]{2,1,0:T(8,128)(2,1)}), bf16[256,48,128]{2,1,0:T(8,128)(2,1)}, u32[]{:S(2)}, u32[]{:S(2)}) %all-to-all-start) | async-done | bytes 3145760 | tf_op jit(solution)/shard_map/all_to_all | solution.py:393
  141.1 4.9 %all-to-all-start.2 = ((s32[8,1,1]{2,1,0:T(1,128)}), s32[8,1,1]{2,1,0:T(1,128)S(1)}, u32[]{:S(2)}, u32[]{:S(2)}) async-start(s32[8,1,1]{2,1,0:T(1,128)} %copy.94), calls=%async_computation.2 | async-start | bytes 8192 | tf_op jit(solution)/shard_map/all_to_all | solution.py:364
  146.1 2.7 %copy.88 = bf16[256,48,128]{2,0,1:T(8,128)(2,1)S(1)} copy(bf16[256,48,128]{2,1,0:T(8,128)(2,1)} %all-to-all-done) | data formatting | bytes 6291456 | tf_op jit(solution)/shard_map/all_to_all | solution.py:393
  148.8 1.8 convolution_bitcast_fusion
  150.6 1.1 convolution_convert_fusion.1
  151.6 3.7 %copy.90 = bf16[256,48,128]{2,1,0:T(8,128)(2,1)} copy(bf16[256,48,128]{2,0,1:T(8,128)(2,1)S(1)} %bitcast.83) | data formatting | bytes 6291456 | tf_op jit(solution)/shard_map/reshape | solution.py:403
  155.4 8.5 %all-to-all-start.1 = ((bf16[256,48,128]{2,1,0:T(8,128)(2,1)}), bf16[256,48,128]{2,1,0:T(8,128)(2,1)}, u32[]{:S(2)}, u32[]{:S(2)}) async-start(bf16[256,48,128]{2,1,0:T(8,128)(2,1)} %copy.90), calls=%async_computation.1 | async-start | bytes 6291456 | tf_op jit(solution)/shard_map/all_to_all | solution.py:404
  164.1 80.4 %shard_map.169.in_ref = bf16[8,16,128,128]{3,2,1,0:T(8,128)(2,1)} custom-call(bf16[8,16,128,128]{3,2,1,0:T(8,128)(2,1)} %get-tuple-element.5.src_hbm), custom_call_target="tpu_custom_call" | custom-call | bytes 8388608 | tf_op jit(solution)/shard_map/pallas_call | solution.py:207
  244.8 0.8 reduce.1.place_ref
  245.5 7.3 %shard_map.170 = bf16[8,16,128,128]{3,2,1,0:T(8,128)(2,1)} custom-call(s32[8]{0:T(128)} %reduce.1.place_ref, bf16[8,16,128,128]{3,2,1,0:T(8,128)(2,1)} %shard_map.169.in_ref), custom_call_target="tpu_custom_call" | custom-call | tf_op jit(solution)/shard_map/pallas_call | solution.py:300
  252.8 2.6 %fusion.6 = f32[32,16,128]{2,0,1:T(8,128)S(1)} fusion(bf16[256,3,16,128]{3,2,1,0:T(8,128)(2,1)} %bitcast.27, bf16[3,32,256,3,1]{2,1,0,3,4:T(8,128)(2,1)S(1)} %bitcast.93), kind=kOutput, calls=%fused_computation.10 | convolution fusion | flops 302120960 | bytes 3555328 | tf_op jit(solution)/shard_map/esk,escl->kcl/dot_general | solution.py:414
  255.4 0.7 reshape.136
  (56 shorter events, 1.4 us)
Async XLA Ops:
  0.6 148.1 %copy-start = (bf16[1,2048,512]{2,1,0:T(8,128)(2,1)S(1)}, bf16[1,2048,512]{2,1,0:T(8,128)(2,1)}, u32[]{:S(2)}) copy-start(bf16[1,2048,512]{2,1,0:T(8,128)(2,1)} %param.29) | copy-start | bytes 6291460
  0.6 2.9 %copy-start.12 = (s32[8]{0:T(128)S(1)}, s32[8]{0:T(128)}, u32[]{:S(2)}) copy-start(s32[8]{0:T(128)} %param.31) | copy-start | bytes 100
  0.7 3.4 %copy-start.6 = (bf16[8,4,1024]{2,1,0:T(4,128)(2,1)S(1)}, bf16[8,4,1024]{2,1,0:T(4,128)(2,1)}, u32[]{:S(2)}) copy-start(bf16[8,4,1024]{2,1,0:T(4,128)(2,1)} %param.18) | copy-start | bytes 196612
  0.7 3.4 %copy-start.7 = (bf16[8,4,1024]{2,1,0:T(4,128)(2,1)S(1)}, bf16[8,4,1024]{2,1,0:T(4,128)(2,1)}, u32[]{:S(2)}) copy-start(bf16[8,4,1024]{2,1,0:T(4,128)(2,1)} %param.17) | copy-start | bytes 196612
  0.7 3.5 %copy-start.4 = (bf16[8,4,2048]{2,1,0:T(4,128)(2,1)S(1)}, bf16[8,4,2048]{2,1,0:T(4,128)(2,1)}, u32[]{:S(2)}) copy-start(bf16[8,4,2048]{2,1,0:T(4,128)(2,1)} %param.19) | copy-start | bytes 393220
  0.7 4.3 %copy-start.5 = (bf16[8,4,2048]{2,1,0:T(4,128)(2,1)S(1)}, bf16[8,4,2048]{2,1,0:T(4,128)(2,1)}, u32[]{:S(2)}) copy-start(bf16[8,4,2048]{2,1,0:T(4,128)(2,1)} %param.20) | copy-start | bytes 393220
  0.7 5.0 %copy-start.10 = (bf16[8,4,16]{2,1,0:T(4,128)(2,1)S(1)}, bf16[8,4,16]{2,1,0:T(4,128)(2,1)}, u32[]{:S(2)}) copy-start(bf16[8,4,16]{2,1,0:T(4,128)(2,1)} %param.22) | copy-start | bytes 3076
  0.7 5.8 %copy-start.11 = (bf16[8,4,16]{2,1,0:T(4,128)(2,1)S(1)}, bf16[8,4,16]{2,1,0:T(4,128)(2,1)}, u32[]{:S(2)}) copy-start(bf16[8,4,16]{2,1,0:T(4,128)(2,1)} %param.21) | copy-start | bytes 3076
  4.2 18.5 %copy-start.3 = (bf16[8,4,2048]{2,1,0:T(4,128)(2,1)S(1)}, bf16[8,4,2048]{2,1,0:T(4,128)(2,1)}, u32[]{:S(2)}) copy-start(bf16[8,4,2048]{2,1,0:T(4,128)(2,1)} %param.23) | copy-start | bytes 393220
  8.0 39.9 %copy-start.9 = (f32[2048]{0:T(1024)S(1)}, f32[2048]{0:T(1024)}, u32[]{:S(2)}) copy-start(f32[2048]{0:T(1024)} %param.28) | copy-start | bytes 24580
  52.7 13.6 %copy-start.1 = (bf16[1,256,2048]{2,1,0:T(8,128)(2,1)S(1)}, bf16[1,256,2048]{2,1,0:T(8,128)(2,1)}, u32[]{:S(2)}) copy-start(bf16[1,256,2048]{2,1,0:T(8,128)(2,1)} %param.30) | copy-start | bytes 3145732
  52.7 88.4 %all-to-all-start = ((bf16[256,48,128]{2,1,0:T(8,128)(2,1)}), bf16[256,48,128]{2,1,0:T(8,128)(2,1)}, u32[]{:S(2)}, u32[]{:S(2)}) async-start(bf16[256,48,128]{2,1,0:T(8,128)(2,1)} %copy.87), calls=%async_computation | async-start | bytes 6291456 | tf_op jit(solution)/shard_map/all_to_all | solution.py:393
  141.1 14.3 %all-to-all-start.2 = ((s32[8,1,1]{2,1,0:T(1,128)}), s32[8,1,1]{2,1,0:T(1,128)S(1)}, u32[]{:S(2)}, u32[]{:S(2)}) async-start(s32[8,1,1]{2,1,0:T(1,128)} %copy.94), calls=%async_computation.2 | async-start | bytes 8192 | tf_op jit(solution)/shard_map/all_to_all | solution.py:364
  148.8 1.8 copy-start.2
  155.4 8.5 %copy-start.8 = (f32[8,4,10]{2,1,0:T(4,128)S(1)}, f32[8,4,10]{2,1,0:T(4,128)}, u32[]{:S(2)}) copy-start(f32[8,4,10]{2,1,0:T(4,128)} %param.25) | copy-start | bytes 3844
  155.4 97.4 %all-to-all-start.1 = ((bf16[256,48,128]{2,1,0:T(8,128)(2,1)}), bf16[256,48,128]{2,1,0:T(8,128)(2,1)}, u32[]{:S(2)}, u32[]{:S(2)}) async-start(bf16[256,48,128]{2,1,0:T(8,128)(2,1)} %copy.90), calls=%async_computation.1 | async-start | bytes 6291456 | tf_op jit(solution)/shard_map/all_to_all | solution.py:404

commit v9 on v8

--- a/solution.py
+++ b/solution.py
@@ -172,7 +172,7 @@
     return (memory_state.astype(jnp.bfloat16), jnp.stack(outputs, axis=1))
 
 
-def migrate_kernel(src_hbm, dst_hbm, send_sem, recv_sem, local_sem):
+def migrate_kernel(src_hbm, tag_hbm, dst_hbm, tag_out, send_sem, recv_sem, tag_send, tag_recv, local_sem):
     lanes = src_hbm.shape[0]
     group = lax.axis_index("dp")
     me = lax.axis_index("ep")
@@ -181,43 +181,51 @@
     for i in range(1, lanes):
         pl.semaphore_signal(barrier, 1, device_id=(group, lax.rem(me + i, lanes)), device_id_type=mesh_ids)
     pl.semaphore_wait(barrier, lanes - 1)
-    own = pltpu.make_async_copy(src_hbm.at[me], dst_hbm.at[me], local_sem)
+    own = pltpu.make_async_copy(src_hbm.at[me], dst_hbm.at[me], local_sem.at[0])
     own.start()
+    own_tag = pltpu.make_async_copy(tag_hbm.at[me], tag_out.at[me], local_sem.at[1])
+    own_tag.start()
     copies = []
     for i in range(1, lanes):
         peer = lax.rem(me + i, lanes)
-        copy = pltpu.make_async_remote_copy(
-            src_hbm.at[peer],
-            dst_hbm.at[me],
-            send_sem.at[i - 1],
-            recv_sem.at[i - 1],
-            device_id=(group, peer),
-            device_id_type=mesh_ids,
-        )
-        copy.start()
-        copies.append(copy)
+        for source, target, sent, landed in ((tag_hbm, tag_out, tag_send, tag_recv), (src_hbm, dst_hbm, send_sem, recv_sem)):
+            copy = pltpu.make_async_remote_copy(
+                source.at[peer],
+                target.at[me],
+                sent.at[i - 1],
+                landed.at[i - 1],
+                device_id=(group, peer),
+                device_id_type=mesh_ids,
+            )
+            copy.start()
+            copies.append(copy)
     own.wait()
+    own_tag.wait()
     for copy in copies:
         copy.wait()
 
 
-def migrate(rows):
+def migrate(rows, tags):
     lanes = rows.shape[0]
     any_spec = pl.BlockSpec(memory_space=pl.ANY)
     return pl.pallas_call(
         migrate_kernel,
-        in_specs=[any_spec],
-        out_specs=any_spec,
-        out_shape=jax.ShapeDtypeStruct(rows.shape, rows.dtype),
+        in_specs=[any_spec, any_spec],
+        out_specs=[any_spec, any_spec],
+        out_shape=[
+            jax.ShapeDtypeStruct(rows.shape, rows.dtype),
+            jax.ShapeDtypeStruct(tags.shape, tags.dtype),
+        ],
         scratch_shapes=[
             pltpu.SemaphoreType.DMA((lanes - 1,)),
             pltpu.SemaphoreType.DMA((lanes - 1,)),
-            pltpu.SemaphoreType.DMA,
+            pltpu.SemaphoreType.DMA((lanes - 1,)),
+            pltpu.SemaphoreType.DMA((lanes - 1,)),
+            pltpu.SemaphoreType.DMA((2,)),
         ],
         compiler_params=pltpu.CompilerParams(collective_id=0, has_side_effects=True),
         cost_estimate=pl.CostEstimate(flops=0, transcendentals=0, bytes_accessed=2 * rows.size * rows.dtype.itemsize),
-    )(rows)
-
+    )(rows, tags)
 
 def project_kernel(rows_ref, weight_ref, out_ref, gathered, product, send_a, recv_a, send_b, recv_b, local_sem):
     lanes = gathered.shape[0]
@@ -359,11 +367,9 @@
         target, states, query_rows, key_rows, value_rows, gate_rows, beta_logit, decay_logit, core_gain
     )
     packed_place = jnp.zeros_like(new_place).at[target].set(new_place)
-    received = (
-        migrate(fresh_states),
-        lax.all_to_all(packed_place, "ep", split_axis=0, concat_axis=0, tiled=True),
-    )
-    moved_out = place_rows(received[0], received[1])
+    tags = jnp.broadcast_to(packed_place[:, None, None], (ep_size, 8, 128))
+    moved_rows, moved_tags = migrate(fresh_states, tags)
+    moved_out = place_rows(moved_rows, moved_tags[:, 0, 0])
     token_count = req_count * step_count
     core_flat = core_out.reshape(token_count, core_out.shape[-1])
     attention = project(core_flat, out_weight)

time: 257 us -> 253 us (0.984)
  starting transfers between devices: 27 us -> 21.1 us
    all_to_all x1 -> x0, starting transfers between devices: 4.95 us -> none  [shards(): lax.all_to_all(packed_place, 'ep', split_axis=0, concat_axis=0, tiled=True)]
  transfers between devices with their start and end apart: 3 -> 2, of which waited for: 1 -> 1; matrix products, arithmetic and copies ran while one was open for 5% -> 2% of each run, Pallas kernels for 34% -> 35%
where the time goes in v9:
time: 253 us; the launch traced here: 252 us
  Pallas kernels  125 us (49%)
  waiting for transfers between devices  73.6 us (29%)
  local copies, waits for them, and re-layouts  21.8 us (9%)
  starting transfers between devices  21.1 us (8%)
  matrix products  6.45 us (3%)
  other arithmetic  3.67 us (1%)
    pallas_call x1, Pallas kernels, migrate(): pl.pallas_call(migrate_kernel, in_specs=[any_spec, any_spec], out_specs=[...  80.3 us
    all_to_all x1, waiting for transfers between devices, shards(): arrived = lax.all_to_all(outgoing, ('dp', 'ep'), 0, 0, tiled=True)  73.6 us
    pallas_call x1, Pallas kernels, project(): pl.pallas_call(project_kernel, in_specs=[vmem, vmem], out_specs=vmem, out...  23.9 us
    all_to_all x1, starting transfers between devices, shards(): arrived = lax.all_to_all(outgoing, ('dp', 'ep'), 0, 0, tiled=True)  13.6 us
    pallas_call x1, Pallas kernels, recurrence(): pl.pallas_call(recur_kernel, grid_spec=pltpu.PrefetchScalarGridSpec(num_s...  13.1 us
    all_to_all x1, starting transfers between devices, shards(): returned = lax.all_to_all(result, ('dp', 'ep'), 0, 0, tiled=True)  7.51 us
    pallas_call x1, Pallas kernels, place_rows(): pl.pallas_call(place_kernel, grid_spec=pltpu.PrefetchScalarGridSpec(num_s...  7.26 us
  transfers between devices with their start and end apart: 2, of which 1 were waited for; matrix products, arithmetic and copies ran while one was open for 2% of the time, Pallas kernels for 35%

profile of v9, /device:TPU:1, one launch (start us, length us, event | category | flops | bytes accessed | tf_op | source)
XLA Modules:
  0.0 252.2 jit_solution(15110187011757215991)
XLA Ops:
  0.7 1.0 eq.45
  1.7 0.7 broadcast_multiply_fusion
  2.6 0.3 fusion.13
  3.1 0.2 fusion.17
  3.5 0.5 compare_select_fusion.1
  4.2 0.7 reshape.123.v_ref
  5.0 0.7 reshape.124.g_ref
  5.7 0.7 copy.63
  6.5 0.7 copy.65
  7.2 0.7 broadcast_in_dim.14
  8.0 13.1 %shard_map.167 = (bf16[8,16,128,128]{3,2,1,0:T(8,128)(2,1)}, bf16[8,4,16,128]{3,2,1,0:T(8,128)(2,1)}) custom-call(s32[8]{0:T(128)} %get-tuple-element.11.slot_ref, bf16[8,16,128,128]{3,2,1,0:T(8,128)(2,1)} %s_ref.1, bf16[8,128,128]{2,1,0:T(8,128)(2,1)} %bitcast.88, bf16[8,4,16,128]{3,2,1,0:T(8,128)(2,1)} %reshape.123.v_ref, ...), custom_call_target="tpu_custom_call" | custom-call | tf_op jit(solution)/shard_map/pallas_call | solution.py:104
  21.1 1.6 copy.113
  22.7 23.9 %shard_map.168 = bf16[32,2048]{1,0:T(8,128)(2,1)} custom-call(bf16[32,2048]{1,0:T(8,128)(2,1)} %bitcast.89, bf16[2048,256]{1,0:T(8,128)(2,1)} %weight_ref.1), custom_call_target="tpu_custom_call" | custom-call | tf_op jit(solution)/shard_map/pallas_call | solution.py:283
  46.6 1.1 fusion.18
  47.6 0.2 compare_reduce_fusion
  47.9 1.0 convolution_convert_fusion
  48.9 3.7 %copy.71 = bf16[256,48,128]{2,1,0:T(8,128)(2,1)} copy(bf16[256,48,128]{2,0,1:T(8,128)(2,1)S(1)} %bitcast.81) | data formatting | bytes 6291456 | tf_op jit(solution)/shard_map/reshape | solution.py:398
  52.7 13.6 %all-to-all-start = ((bf16[256,48,128]{2,1,0:T(8,128)(2,1)}), bf16[256,48,128]{2,1,0:T(8,128)(2,1)}, u32[]{:S(2)}, u32[]{:S(2)}) async-start(bf16[256,48,128]{2,1,0:T(8,128)(2,1)} %copy.71), calls=%async_computation | async-start | bytes 6291456 | tf_op jit(solution)/shard_map/all_to_all | solution.py:399
  66.3 1.2 copy.88
  67.5 73.6 %all-to-all-done = bf16[256,48,128]{2,1,0:T(8,128)(2,1)} async-done(((bf16[256,48,128]{2,1,0:T(8,128)(2,1)}), bf16[256,48,128]{2,1,0:T(8,128)(2,1)}, u32[]{:S(2)}, u32[]{:S(2)}) %all-to-all-start) | async-done | bytes 3145760 | tf_op jit(solution)/shard_map/all_to_all | solution.py:399
  141.1 2.7 %copy.72 = bf16[256,48,128]{2,0,1:T(8,128)(2,1)S(1)} copy(bf16[256,48,128]{2,1,0:T(8,128)(2,1)} %all-to-all-done) | data formatting | bytes 6291456 | tf_op jit(solution)/shard_map/all_to_all | solution.py:399
  143.8 1.8 convolution_bitcast_fusion
  145.6 1.1 convolution_convert_fusion.1
  146.7 3.7 %copy.74 = bf16[256,48,128]{2,1,0:T(8,128)(2,1)} copy(bf16[256,48,128]{2,0,1:T(8,128)(2,1)S(1)} %bitcast.82) | data formatting | bytes 6291456 | tf_op jit(solution)/shard_map/reshape | solution.py:409
  150.4 7.5 %all-to-all-start.1 = ((bf16[256,48,128]{2,1,0:T(8,128)(2,1)}), bf16[256,48,128]{2,1,0:T(8,128)(2,1)}, u32[]{:S(2)}, u32[]{:S(2)}) async-start(bf16[256,48,128]{2,1,0:T(8,128)(2,1)} %copy.74), calls=%async_computation.1 | async-start | bytes 6291456 | tf_op jit(solution)/shard_map/all_to_all | solution.py:410
  158.2 0.6 scatter_custom_fusion
  158.8 0.7 broadcast_in_dim.35.tag_hbm
  159.5 80.3 %shard_map.169 = (bf16[8,16,128,128]{3,2,1,0:T(8,128)(2,1)}, s32[8,8,128]{2,1,0:T(8,128)}) custom-call(bf16[8,16,128,128]{3,2,1,0:T(8,128)(2,1)} %get-tuple-element.7.src_hbm, s32[8,8,128]{2,1,0:T(8,128)} %broadcast_in_dim.35.tag_hbm), custom_call_target="tpu_custom_call" | custom-call | bytes 8388608 | tf_op jit(solution)/shard_map/pallas_call | solution.py:211
  239.9 1.5 slice_reduce_fusion.place_ref
  241.4 7.3 %shard_map.170 = bf16[8,16,128,128]{3,2,1,0:T(8,128)(2,1)} custom-call(s32[8]{0:T(128)} %slice_reduce_fusion.place_ref, bf16[8,16,128,128]{3,2,1,0:T(8,128)(2,1)} %get-tuple-element.9.in_ref), custom_call_target="tpu_custom_call" | custom-call | tf_op jit(solution)/shard_map/pallas_call | solution.py:308
  248.9 2.6 %fusion.6 = f32[32,16,128]{2,0,1:T(8,128)S(1)} fusion(bf16[256,3,16,128]{3,2,1,0:T(8,128)(2,1)} %bitcast.27, bf16[3,32,256,3,1]{2,1,0,3,4:T(8,128)(2,1)S(1)} %bitcast.92), kind=kOutput, calls=%fused_computation.10 | convolution fusion | flops 302120960 | bytes 3555328 | tf_op jit(solution)/shard_map/esk,escl->kcl/dot_general | solution.py:420
  251.5 0.7 reshape.135
  (54 shorter events, 1.2 us)
Async XLA Ops:
  0.6 143.2 %copy-start = (bf16[1,2048,512]{2,1,0:T(8,128)(2,1)S(1)}, bf16[1,2048,512]{2,1,0:T(8,128)(2,1)}, u32[]{:S(2)}) copy-start(bf16[1,2048,512]{2,1,0:T(8,128)(2,1)} %param.29) | copy-start | bytes 6291460
  0.6 2.9 %copy-start.12 = (s32[8]{0:T(128)S(1)}, s32[8]{0:T(128)}, u32[]{:S(2)}) copy-start(s32[8]{0:T(128)} %param.31) | copy-start | bytes 100
  0.7 3.4 %copy-start.6 = (bf16[8,4,1024]{2,1,0:T(4,128)(2,1)S(1)}, bf16[8,4,1024]{2,1,0:T(4,128)(2,1)}, u32[]{:S(2)}) copy-start(bf16[8,4,1024]{2,1,0:T(4,128)(2,1)} %param.18) | copy-start | bytes 196612
  0.7 3.4 %copy-start.7 = (bf16[8,4,1024]{2,1,0:T(4,128)(2,1)S(1)}, bf16[8,4,1024]{2,1,0:T(4,128)(2,1)}, u32[]{:S(2)}) copy-start(bf16[8,4,1024]{2,1,0:T(4,128)(2,1)} %param.17) | copy-start | bytes 196612
  0.7 3.5 %copy-start.4 = (bf16[8,4,2048]{2,1,0:T(4,128)(2,1)S(1)}, bf16[8,4,2048]{2,1,0:T(4,128)(2,1)}, u32[]{:S(2)}) copy-start(bf16[8,4,2048]{2,1,0:T(4,128)(2,1)} %param.19) | copy-start | bytes 393220
  0.7 4.3 %copy-start.5 = (bf16[8,4,2048]{2,1,0:T(4,128)(2,1)S(1)}, bf16[8,4,2048]{2,1,0:T(4,128)(2,1)}, u32[]{:S(2)}) copy-start(bf16[8,4,2048]{2,1,0:T(4,128)(2,1)} %param.20) | copy-start | bytes 393220
  0.7 5.0 %copy-start.10 = (bf16[8,4,16]{2,1,0:T(4,128)(2,1)S(1)}, bf16[8,4,16]{2,1,0:T(4,128)(2,1)}, u32[]{:S(2)}) copy-start(bf16[8,4,16]{2,1,0:T(4,128)(2,1)} %param.22) | copy-start | bytes 3076
  0.7 5.8 %copy-start.11 = (bf16[8,4,16]{2,1,0:T(4,128)(2,1)S(1)}, bf16[8,4,16]{2,1,0:T(4,128)(2,1)}, u32[]{:S(2)}) copy-start(bf16[8,4,16]{2,1,0:T(4,128)(2,1)} %param.21) | copy-start | bytes 3076
  4.2 18.5 %copy-start.3 = (bf16[8,4,2048]{2,1,0:T(4,128)(2,1)S(1)}, bf16[8,4,2048]{2,1,0:T(4,128)(2,1)}, u32[]{:S(2)}) copy-start(bf16[8,4,2048]{2,1,0:T(4,128)(2,1)} %param.23) | copy-start | bytes 393220
  8.0 39.9 %copy-start.9 = (f32[2048]{0:T(1024)S(1)}, f32[2048]{0:T(1024)}, u32[]{:S(2)}) copy-start(f32[2048]{0:T(1024)} %param.28) | copy-start | bytes 24580
  52.7 13.6 %copy-start.1 = (bf16[1,256,2048]{2,1,0:T(8,128)(2,1)S(1)}, bf16[1,256,2048]{2,1,0:T(8,128)(2,1)}, u32[]{:S(2)}) copy-start(bf16[1,256,2048]{2,1,0:T(8,128)(2,1)} %param.30) | copy-start | bytes 3145732
  52.7 88.4 %all-to-all-start = ((bf16[256,48,128]{2,1,0:T(8,128)(2,1)}), bf16[256,48,128]{2,1,0:T(8,128)(2,1)}, u32[]{:S(2)}, u32[]{:S(2)}) async-start(bf16[256,48,128]{2,1,0:T(8,128)(2,1)} %copy.71), calls=%async_computation | async-start | bytes 6291456 | tf_op jit(solution)/shard_map/all_to_all | solution.py:399
  143.8 1.8 copy-start.2
  150.4 7.5 %copy-start.8 = (f32[8,4,10]{2,1,0:T(4,128)S(1)}, f32[8,4,10]{2,1,0:T(4,128)}, u32[]{:S(2)}) copy-start(f32[8,4,10]{2,1,0:T(4,128)} %param.25) | copy-start | bytes 3844
  150.4 98.4 %all-to-all-start.1 = ((bf16[256,48,128]{2,1,0:T(8,128)(2,1)}), bf16[256,48,128]{2,1,0:T(8,128)(2,1)}, u32[]{:S(2)}, u32[]{:S(2)}) async-start(bf16[256,48,128]{2,1,0:T(8,128)(2,1)} %copy.74), calls=%async_computation.1 | async-start | bytes 6291456 | tf_op jit(solution)/shard_map/all_to_all | solution.py:410

commit v10 on v9

--- a/solution.py
+++ b/solution.py
@@ -298,24 +298,38 @@
     )(rows, weight)
 
 
-def place_kernel(place_ref, in_ref, out_ref):
-    out_ref[...] = in_ref[...]
+def place_kernel(place_ref, in_hbm, out_hbm, held, in_sem, out_sem):
+    count = in_hbm.shape[0]
+    loads = []
+    for j in range(count):
+        load = pltpu.make_async_copy(in_hbm.at[j], held.at[j], in_sem.at[j])
+        load.start()
+        loads.append(load)
+    stores = []
+    for j in range(count):
+        loads[j].wait()
+        store = pltpu.make_async_copy(held.at[j], out_hbm.at[place_ref[j]], out_sem.at[j])
+        store.start()
+        stores.append(store)
+    for store in stores:
+        store.wait()
 
 
 def place_rows(rows, places):
-    block = (1,) + rows.shape[1:]
-    tail = (0,) * (rows.ndim - 1)
+    count = rows.shape[0]
+    any_spec = pl.BlockSpec(memory_space=pl.ANY)
     return pl.pallas_call(
         place_kernel,
-        grid_spec=pltpu.PrefetchScalarGridSpec(
-            num_scalar_prefetch=1,
-            grid=(rows.shape[0],),
-            in_specs=[pl.BlockSpec(block, lambda j, place: (j,) + tail)],
-            out_specs=pl.BlockSpec(block, lambda j, place: (place[j],) + tail),
-        ),
+        in_specs=[pl.BlockSpec(memory_space=pltpu.SMEM), any_spec],
+        out_specs=any_spec,
         out_shape=jax.ShapeDtypeStruct(rows.shape, rows.dtype),
+        scratch_shapes=[
+            pltpu.VMEM(rows.shape, rows.dtype),
+            pltpu.SemaphoreType.DMA((count,)),
+            pltpu.SemaphoreType.DMA((count,)),
+        ],
+        compiler_params=pltpu.CompilerParams(vmem_limit_bytes=48 * 1024 * 1024),
     )(places, rows)
-
 
 def rms_scale(values, gain):
     return values * lax.rsqrt(jnp.mean(values * values, -1, keepdims=True) + epsilon) * gain

time: 253 us -> 250 us (0.988)
  Pallas kernels: 125 us -> 120 us
    pallas_call x1, Pallas kernels: 7.26 us -> 2.97 us  [place_rows(): pl.pallas_call(place_kernel, in_specs=[pl.BlockSpec(memory_space=pltpu.SM...]
    unnamed x28 -> x30, local copies, waits for them, and re-layouts: 2.89 us -> 5.08 us
  transfers between devices with their start and end apart: 2 -> 2, of which waited for: 1 -> 1; matrix products, arithmetic and copies ran while one was open for 2% -> 2% of each run, Pallas kernels for 35% -> 33%
where the time goes in v10:
time: 250 us
  Pallas kernels  120 us (48%)
  waiting for transfers between devices  73.6 us (29%)
  local copies, waits for them, and re-layouts  23.5 us (9%)
  starting transfers between devices  21.1 us (8%)
  matrix products  6.46 us (3%)
  other arithmetic  3.66 us (1%)
    pallas_call x1, Pallas kernels, migrate(): pl.pallas_call(migrate_kernel, in_specs=[any_spec, any_spec], out_specs=[...  80.3 us
    all_to_all x1, waiting for transfers between devices, shards(): arrived = lax.all_to_all(outgoing, ('dp', 'ep'), 0, 0, tiled=True)  73.6 us
    pallas_call x1, Pallas kernels, project(): pl.pallas_call(project_kernel, in_specs=[vmem, vmem], out_specs=vmem, out...  23.9 us
    all_to_all x1, starting transfers between devices, shards(): arrived = lax.all_to_all(outgoing, ('dp', 'ep'), 0, 0, tiled=True)  13.6 us
    pallas_call x1, Pallas kernels, recurrence(): pl.pallas_call(recur_kernel, grid_spec=pltpu.PrefetchScalarGridSpec(num_s...  13.1 us
    all_to_all x1, starting transfers between devices, shards(): returned = lax.all_to_all(result, ('dp', 'ep'), 0, 0, tiled=True)  7.51 us
    unnamed x30, local copies, waits for them, and re-layouts  5.08 us
  transfers between devices with their start and end apart: 2, of which 1 were waited for; matrix products, arithmetic and copies ran while one was open for 2% of the time, Pallas kernels for 33%

profile of v10, /device:TPU:1, one launch (start us, length us, event | category | flops | bytes accessed | tf_op | source)
XLA Modules:
  0.0 249.6 jit_solution(10296954742000177770)
XLA Ops:
  0.7 1.0 eq.45
  1.7 0.7 broadcast_multiply_fusion
  2.6 0.3 fusion.13
  3.1 0.2 fusion.17
  3.5 0.5 compare_select_fusion.1
  4.2 0.7 reshape.123.v_ref
  5.0 0.7 reshape.124.g_ref
  5.7 0.7 copy.63
  6.5 0.7 copy.65
  7.2 0.7 broadcast_in_dim.14
  8.0 13.1 %shard_map.167 = (bf16[8,16,128,128]{3,2,1,0:T(8,128)(2,1)}, bf16[8,4,16,128]{3,2,1,0:T(8,128)(2,1)}) custom-call(s32[8]{0:T(128)} %get-tuple-element.11.slot_ref, bf16[8,16,128,128]{3,2,1,0:T(8,128)(2,1)} %s_ref.1, bf16[8,128,128]{2,1,0:T(8,128)(2,1)} %bitcast.88, bf16[8,4,16,128]{3,2,1,0:T(8,128)(2,1)} %reshape.123.v_ref, ...), custom_call_target="tpu_custom_call" | custom-call | tf_op jit(solution)/shard_map/pallas_call | solution.py:104
  21.1 1.6 copy.113
  22.7 23.9 %shard_map.168 = bf16[32,2048]{1,0:T(8,128)(2,1)} custom-call(bf16[32,2048]{1,0:T(8,128)(2,1)} %bitcast.89, bf16[2048,256]{1,0:T(8,128)(2,1)} %weight_ref.1), custom_call_target="tpu_custom_call" | custom-call | tf_op jit(solution)/shard_map/pallas_call | solution.py:283
  46.6 1.1 fusion.18
  47.9 1.0 convolution_convert_fusion
  48.9 3.7 %copy.71 = bf16[256,48,128]{2,1,0:T(8,128)(2,1)} copy(bf16[256,48,128]{2,0,1:T(8,128)(2,1)S(1)} %bitcast.81) | data formatting | bytes 6291456 | tf_op jit(solution)/shard_map/reshape | solution.py:412
  52.7 13.6 %all-to-all-start = ((bf16[256,48,128]{2,1,0:T(8,128)(2,1)}), bf16[256,48,128]{2,1,0:T(8,128)(2,1)}, u32[]{:S(2)}, u32[]{:S(2)}) async-start(bf16[256,48,128]{2,1,0:T(8,128)(2,1)} %copy.71), calls=%async_computation | async-start | bytes 6291456 | tf_op jit(solution)/shard_map/all_to_all | solution.py:413
  66.3 1.2 copy.88
  67.5 73.6 %all-to-all-done = bf16[256,48,128]{2,1,0:T(8,128)(2,1)} async-done(((bf16[256,48,128]{2,1,0:T(8,128)(2,1)}), bf16[256,48,128]{2,1,0:T(8,128)(2,1)}, u32[]{:S(2)}, u32[]{:S(2)}) %all-to-all-start) | async-done | bytes 3145760 | tf_op jit(solution)/shard_map/all_to_all | solution.py:413
  141.1 2.7 %copy.72 = bf16[256,48,128]{2,0,1:T(8,128)(2,1)S(1)} copy(bf16[256,48,128]{2,1,0:T(8,128)(2,1)} %all-to-all-done) | data formatting | bytes 6291456 | tf_op jit(solution)/shard_map/all_to_all | solution.py:413
  143.8 1.8 convolution_bitcast_fusion
  145.6 1.1 convolution_convert_fusion.1
  146.7 3.7 %copy.74 = bf16[256,48,128]{2,1,0:T(8,128)(2,1)} copy(bf16[256,48,128]{2,0,1:T(8,128)(2,1)S(1)} %bitcast.82) | data formatting | bytes 6291456 | tf_op jit(solution)/shard_map/reshape | solution.py:423
  150.4 7.5 %all-to-all-start.1 = ((bf16[256,48,128]{2,1,0:T(8,128)(2,1)}), bf16[256,48,128]{2,1,0:T(8,128)(2,1)}, u32[]{:S(2)}, u32[]{:S(2)}) async-start(bf16[256,48,128]{2,1,0:T(8,128)(2,1)} %copy.74), calls=%async_computation.1 | async-start | bytes 6291456 | tf_op jit(solution)/shard_map/all_to_all | solution.py:424
  158.2 0.6 scatter_custom_fusion
  158.8 0.7 broadcast_in_dim.35.tag_hbm
  159.5 80.3 %shard_map.169 = (bf16[8,16,128,128]{3,2,1,0:T(8,128)(2,1)}, s32[8,8,128]{2,1,0:T(8,128)}) custom-call(bf16[8,16,128,128]{3,2,1,0:T(8,128)(2,1)} %get-tuple-element.7.src_hbm, s32[8,8,128]{2,1,0:T(8,128)} %broadcast_in_dim.35.tag_hbm), custom_call_target="tpu_custom_call" | custom-call | bytes 8388608 | tf_op jit(solution)/shard_map/pallas_call | solution.py:211
  239.9 1.0 slice_reduce_fusion.place_ref
  240.9 2.2 copy-done.1
  243.0 3.0 %shard_map.170 = bf16[8,16,128,128]{3,2,1,0:T(8,128)(2,1)} custom-call(s32[8]{0:T(128)S(1)} %slice_reduce_fusion.place_ref, bf16[8,16,128,128]{3,2,1,0:T(8,128)(2,1)S(1)} %copy-done.1), custom_call_target="tpu_custom_call" | custom-call | tf_op jit(solution)/shard_map/pallas_call | solution.py:321
  246.3 2.6 %fusion.6 = f32[32,16,128]{2,0,1:T(8,128)S(1)} fusion(bf16[256,3,16,128]{3,2,1,0:T(8,128)(2,1)} %bitcast.27, bf16[3,32,256,3,1]{2,1,0,3,4:T(8,128)(2,1)S(1)} %bitcast.92), kind=kOutput, calls=%fused_computation.10 | convolution fusion | flops 302120960 | bytes 3555328 | tf_op jit(solution)/shard_map/esk,escl->kcl/dot_general | solution.py:434
  248.9 0.7 reshape.135
  (56 shorter events, 1.4 us)
Async XLA Ops:
  0.6 143.2 %copy-start = (bf16[1,2048,512]{2,1,0:T(8,128)(2,1)S(1)}, bf16[1,2048,512]{2,1,0:T(8,128)(2,1)}, u32[]{:S(2)}) copy-start(bf16[1,2048,512]{2,1,0:T(8,128)(2,1)} %param.29) | copy-start | bytes 6291460
  0.6 2.9 %copy-start.13 = (s32[8]{0:T(128)S(1)}, s32[8]{0:T(128)}, u32[]{:S(2)}) copy-start(s32[8]{0:T(128)} %param.31) | copy-start | bytes 100
  0.7 3.4 %copy-start.7 = (bf16[8,4,1024]{2,1,0:T(4,128)(2,1)S(1)}, bf16[8,4,1024]{2,1,0:T(4,128)(2,1)}, u32[]{:S(2)}) copy-start(bf16[8,4,1024]{2,1,0:T(4,128)(2,1)} %param.18) | copy-start | bytes 196612
  0.7 3.4 %copy-start.8 = (bf16[8,4,1024]{2,1,0:T(4,128)(2,1)S(1)}, bf16[8,4,1024]{2,1,0:T(4,128)(2,1)}, u32[]{:S(2)}) copy-start(bf16[8,4,1024]{2,1,0:T(4,128)(2,1)} %param.17) | copy-start | bytes 196612
  0.7 3.5 %copy-start.5 = (bf16[8,4,2048]{2,1,0:T(4,128)(2,1)S(1)}, bf16[8,4,2048]{2,1,0:T(4,128)(2,1)}, u32[]{:S(2)}) copy-start(bf16[8,4,2048]{2,1,0:T(4,128)(2,1)} %param.19) | copy-start | bytes 393220
  0.7 4.3 %copy-start.6 = (bf16[8,4,2048]{2,1,0:T(4,128)(2,1)S(1)}, bf16[8,4,2048]{2,1,0:T(4,128)(2,1)}, u32[]{:S(2)}) copy-start(bf16[8,4,2048]{2,1,0:T(4,128)(2,1)} %param.20) | copy-start | bytes 393220
  0.7 5.0 %copy-start.11 = (bf16[8,4,16]{2,1,0:T(4,128)(2,1)S(1)}, bf16[8,4,16]{2,1,0:T(4,128)(2,1)}, u32[]{:S(2)}) copy-start(bf16[8,4,16]{2,1,0:T(4,128)(2,1)} %param.22) | copy-start | bytes 3076
  0.7 5.8 %copy-start.12 = (bf16[8,4,16]{2,1,0:T(4,128)(2,1)S(1)}, bf16[8,4,16]{2,1,0:T(4,128)(2,1)}, u32[]{:S(2)}) copy-start(bf16[8,4,16]{2,1,0:T(4,128)(2,1)} %param.21) | copy-start | bytes 3076
  4.2 18.5 %copy-start.4 = (bf16[8,4,2048]{2,1,0:T(4,128)(2,1)S(1)}, bf16[8,4,2048]{2,1,0:T(4,128)(2,1)}, u32[]{:S(2)}) copy-start(bf16[8,4,2048]{2,1,0:T(4,128)(2,1)} %param.23) | copy-start | bytes 393220
  8.0 39.9 %copy-start.10 = (f32[2048]{0:T(1024)S(1)}, f32[2048]{0:T(1024)}, u32[]{:S(2)}) copy-start(f32[2048]{0:T(1024)} %param.28) | copy-start | bytes 24580
  52.7 13.6 %copy-start.2 = (bf16[1,256,2048]{2,1,0:T(8,128)(2,1)S(1)}, bf16[1,256,2048]{2,1,0:T(8,128)(2,1)}, u32[]{:S(2)}) copy-start(bf16[1,256,2048]{2,1,0:T(8,128)(2,1)} %param.30) | copy-start | bytes 3145732
  52.7 88.4 %all-to-all-start = ((bf16[256,48,128]{2,1,0:T(8,128)(2,1)}), bf16[256,48,128]{2,1,0:T(8,128)(2,1)}, u32[]{:S(2)}, u32[]{:S(2)}) async-start(bf16[256,48,128]{2,1,0:T(8,128)(2,1)} %copy.71), calls=%async_computation | async-start | bytes 6291456 | tf_op jit(solution)/shard_map/all_to_all | solution.py:413
  143.8 1.8 copy-start.3
  150.4 7.5 %copy-start.9 = (f32[8,4,10]{2,1,0:T(4,128)S(1)}, f32[8,4,10]{2,1,0:T(4,128)}, u32[]{:S(2)}) copy-start(f32[8,4,10]{2,1,0:T(4,128)} %param.25) | copy-start | bytes 3844
  150.4 95.8 %all-to-all-start.1 = ((bf16[256,48,128]{2,1,0:T(8,128)(2,1)}), bf16[256,48,128]{2,1,0:T(8,128)(2,1)}, u32[]{:S(2)}, u32[]{:S(2)}) async-start(bf16[256,48,128]{2,1,0:T(8,128)(2,1)} %copy.74), calls=%async_computation.1 | async-start | bytes 6291456 | tf_op jit(solution)/shard_map/all_to_all | solution.py:424
  240.8 2.2 copy-start.1

commit v11 on v10

--- a/solution.py
+++ b/solution.py
@@ -18,7 +18,7 @@
     return hi, lo
 
 
-def recur_kernel(slot_ref, s_ref, kq_ref, v_ref, g_ref, dec_ref, beta_ref, gain_ref, so_ref, co_ref, n_ref, r_ref, u_ref):
+def recur_kernel(slot_ref, s_ref, kq_ref, v_ref, g_ref, dec_ref, beta_ref, gain_ref, so_ref, co_ref, n_ref, r_ref, u_ref, c_ref):
     heads = s_ref.shape[1]
     width = s_ref.shape[-1]
     steps = v_ref.shape[1]
@@ -66,9 +66,11 @@
             reading = reading + coef * updates[j]
         scaled = reading * lax.rsqrt(jnp.mean(reading * reading, -1, keepdims=True) + epsilon)
         gate_vals = g_ref[0, t].astype(f32)
-        co_ref[0, t] = (scaled * gain * (gate_vals * jax.nn.sigmoid(gate_vals))).astype(co_ref.dtype)
+        c_ref[pl.ds(t * heads, heads), :] = scaled * gain * (gate_vals * jax.nn.sigmoid(gate_vals))
     for j in range(steps):
         u_ref[pl.ds(j, heads, stride=span), :] = carried[j] * updates[j]
+    for h in range(heads):
+        co_ref[0, :, pl.ds(h * width, width)] = c_ref[pl.ds(h, steps, stride=heads), :].astype(co_ref.dtype)
     for h in range(heads):
         kt = n_ref[pl.ds(h * span, span), :].T
         w = u_ref[pl.ds(h * span, span), :]
@@ -115,15 +117,15 @@
                 coef_spec,
                 pl.BlockSpec((1, width), lambda i, slot: (0, 0)),
             ],
-            out_specs=[state_out, row_spec],
-            scratch_shapes=[pltpu.VMEM((heads * span, width), f32)] * 3,
+            out_specs=[state_out, pl.BlockSpec((1, steps, heads * width), lambda i, slot: (i, 0, 0))],
+            scratch_shapes=[pltpu.VMEM((heads * span, width), f32)] * 3 + [pltpu.VMEM((steps * heads, width), f32)],
         ),
         out_shape=[
             jax.ShapeDtypeStruct(states.shape, bf16),
-            jax.ShapeDtypeStruct((batch, steps, heads, width), bf16),
+            jax.ShapeDtypeStruct((batch, steps, heads * width), bf16),
         ],
     )(slots, states, kq, values, gates, decay, beta, gain)
-    return fresh, core.reshape(batch, steps, heads * width)
+    return fresh, core
 
 
 def unit_rows(values):

time: 250 us -> 250 us (level)
    unnamed x30 -> x29, local copies, waits for them, and re-layouts: 5.08 us -> 3.49 us
where the time goes in v11:
time: 250 us
  Pallas kernels  120 us (48%)
  waiting for transfers between devices  73.6 us (29%)
  local copies, waits for them, and re-layouts  23.5 us (9%)
  starting transfers between devices  21.1 us (8%)
  matrix products  6.46 us (3%)
  other arithmetic  3.66 us (1%)
    pallas_call x1, Pallas kernels, migrate(): pl.pallas_call(migrate_kernel, in_specs=[any_spec, any_spec], out_specs=[...  80.3 us
    all_to_all x1, waiting for transfers between devices, shards(): arrived = lax.all_to_all(outgoing, ('dp', 'ep'), 0, 0, tiled=True)  73.6 us
    pallas_call x1, Pallas kernels, project(): pl.pallas_call(project_kernel, in_specs=[vmem, vmem], out_specs=vmem, out...  23.9 us
    all_to_all x1, starting transfers between devices, shards(): arrived = lax.all_to_all(outgoing, ('dp', 'ep'), 0, 0, tiled=True)  13.6 us
    pallas_call x1, Pallas kernels, recurrence(): pl.pallas_call(recur_kernel, grid_spec=pltpu.PrefetchScalarGridSpec(num_s...  13.2 us
    all_to_all x1, starting transfers between devices, shards(): returned = lax.all_to_all(result, ('dp', 'ep'), 0, 0, tiled=True)  7.51 us
  transfers between devices with their start and end apart: 2, of which 1 were waited for; matrix products, arithmetic and copies ran while one was open for 2% of the time, Pallas kernels for 33%

profile of v11, /device:TPU:1, one launch (start us, length us, event | category | flops | bytes accessed | tf_op | source)
XLA Modules:
  0.0 249.6 jit_solution(15446173991999581359)
XLA Ops:
  0.7 1.0 eq.45
  1.7 0.7 broadcast_multiply_fusion
  2.6 0.3 fusion.13
  3.1 0.2 fusion.17
  3.5 0.5 compare_select_fusion.1
  4.2 0.7 reshape.126.v_ref
  5.0 0.7 reshape.127.g_ref
  5.7 0.7 copy.63
  6.5 0.7 copy.65
  7.2 0.7 broadcast_in_dim.14
  8.0 13.2 %shard_map.167 = (bf16[8,16,128,128]{3,2,1,0:T(8,128)(2,1)}, bf16[8,4,2048]{2,1,0:T(4,128)(2,1)}) custom-call(s32[8]{0:T(128)} %get-tuple-element.11.slot_ref, bf16[8,16,128,128]{3,2,1,0:T(8,128)(2,1)} %s_ref.1, bf16[8,128,128]{2,1,0:T(8,128)(2,1)} %bitcast.83, bf16[8,4,16,128]{3,2,1,0:T(8,128)(2,1)} %reshape.126.v_ref, ...), custom_call_target="tpu_custom_call" | custom-call | tf_op jit(solution)/shard_map/pallas_call | solution.py:106
  21.1 1.6 reshape.129.rows_ref
  22.7 23.9 %shard_map.168 = bf16[32,2048]{1,0:T(8,128)(2,1)} custom-call(bf16[32,2048]{1,0:T(8,128)(2,1)} %reshape.129.rows_ref, bf16[2048,256]{1,0:T(8,128)(2,1)} %weight_ref.1), custom_call_target="tpu_custom_call" | custom-call | tf_op jit(solution)/shard_map/pallas_call | solution.py:285
  46.6 1.1 fusion.18
  47.9 1.0 convolution_convert_fusion
  49.0 3.7 %copy.71 = bf16[256,48,128]{2,1,0:T(8,128)(2,1)} copy(bf16[256,48,128]{2,0,1:T(8,128)(2,1)S(1)} %bitcast.76) | data formatting | bytes 6291456 | tf_op jit(solution)/shard_map/reshape | solution.py:414
  52.7 13.6 %all-to-all-start = ((bf16[256,48,128]{2,1,0:T(8,128)(2,1)}), bf16[256,48,128]{2,1,0:T(8,128)(2,1)}, u32[]{:S(2)}, u32[]{:S(2)}) async-start(bf16[256,48,128]{2,1,0:T(8,128)(2,1)} %copy.71), calls=%async_computation | async-start | bytes 6291456 | tf_op jit(solution)/shard_map/all_to_all | solution.py:415
  66.3 1.2 copy.87
  67.6 73.6 %all-to-all-done = bf16[256,48,128]{2,1,0:T(8,128)(2,1)} async-done(((bf16[256,48,128]{2,1,0:T(8,128)(2,1)}), bf16[256,48,128]{2,1,0:T(8,128)(2,1)}, u32[]{:S(2)}, u32[]{:S(2)}) %all-to-all-start) | async-done | bytes 3145760 | tf_op jit(solution)/shard_map/all_to_all | solution.py:415
  141.1 2.7 %copy.72 = bf16[256,48,128]{2,0,1:T(8,128)(2,1)S(1)} copy(bf16[256,48,128]{2,1,0:T(8,128)(2,1)} %all-to-all-done) | data formatting | bytes 6291456 | tf_op jit(solution)/shard_map/all_to_all | solution.py:415
  143.9 1.8 convolution_bitcast_fusion
  145.6 1.1 convolution_convert_fusion.1
  146.7 3.7 %copy.74 = bf16[256,48,128]{2,1,0:T(8,128)(2,1)} copy(bf16[256,48,128]{2,0,1:T(8,128)(2,1)S(1)} %bitcast.77) | data formatting | bytes 6291456 | tf_op jit(solution)/shard_map/reshape | solution.py:425
  150.5 7.5 %all-to-all-start.1 = ((bf16[256,48,128]{2,1,0:T(8,128)(2,1)}), bf16[256,48,128]{2,1,0:T(8,128)(2,1)}, u32[]{:S(2)}, u32[]{:S(2)}) async-start(bf16[256,48,128]{2,1,0:T(8,128)(2,1)} %copy.74), calls=%async_computation.1 | async-start | bytes 6291456 | tf_op jit(solution)/shard_map/all_to_all | solution.py:426
  158.3 0.6 scatter_custom_fusion
  158.9 0.7 broadcast_in_dim.35.tag_hbm
  159.6 80.3 %shard_map.169 = (bf16[8,16,128,128]{3,2,1,0:T(8,128)(2,1)}, s32[8,8,128]{2,1,0:T(8,128)}) custom-call(bf16[8,16,128,128]{3,2,1,0:T(8,128)(2,1)} %get-tuple-element.7.src_hbm, s32[8,8,128]{2,1,0:T(8,128)} %broadcast_in_dim.35.tag_hbm), custom_call_target="tpu_custom_call" | custom-call | bytes 8388608 | tf_op jit(solution)/shard_map/pallas_call | solution.py:213
  239.9 1.0 slice_reduce_fusion.place_ref
  240.9 2.2 copy-done.1
  243.1 3.0 %shard_map.170 = bf16[8,16,128,128]{3,2,1,0:T(8,128)(2,1)} custom-call(s32[8]{0:T(128)S(1)} %slice_reduce_fusion.place_ref, bf16[8,16,128,128]{3,2,1,0:T(8,128)(2,1)S(1)} %copy-done.1), custom_call_target="tpu_custom_call" | custom-call | tf_op jit(solution)/shard_map/pallas_call | solution.py:323
  246.3 2.6 %fusion.6 = f32[32,16,128]{2,0,1:T(8,128)S(1)} fusion(bf16[256,3,16,128]{3,2,1,0:T(8,128)(2,1)} %bitcast.27, bf16[3,32,256,3,1]{2,1,0,3,4:T(8,128)(2,1)S(1)} %bitcast.86), kind=kOutput, calls=%fused_computation.10 | convolution fusion | flops 302120960 | bytes 3555328 | tf_op jit(solution)/shard_map/esk,escl->kcl/dot_general | solution.py:436
  248.9 0.7 reshape.139
  (56 shorter events, 1.4 us)
Async XLA Ops:
  0.6 143.2 %copy-start = (bf16[1,2048,512]{2,1,0:T(8,128)(2,1)S(1)}, bf16[1,2048,512]{2,1,0:T(8,128)(2,1)}, u32[]{:S(2)}) copy-start(bf16[1,2048,512]{2,1,0:T(8,128)(2,1)} %param.29) | copy-start | bytes 6291460
  0.6 2.9 %copy-start.13 = (s32[8]{0:T(128)S(1)}, s32[8]{0:T(128)}, u32[]{:S(2)}) copy-start(s32[8]{0:T(128)} %param.31) | copy-start | bytes 100
  0.7 3.4 %copy-start.7 = (bf16[8,4,1024]{2,1,0:T(4,128)(2,1)S(1)}, bf16[8,4,1024]{2,1,0:T(4,128)(2,1)}, u32[]{:S(2)}) copy-start(bf16[8,4,1024]{2,1,0:T(4,128)(2,1)} %param.18) | copy-start | bytes 196612
  0.7 3.4 %copy-start.8 = (bf16[8,4,1024]{2,1,0:T(4,128)(2,1)S(1)}, bf16[8,4,1024]{2,1,0:T(4,128)(2,1)}, u32[]{:S(2)}) copy-start(bf16[8,4,1024]{2,1,0:T(4,128)(2,1)} %param.17) | copy-start | bytes 196612
  0.7 3.5 %copy-start.5 = (bf16[8,4,2048]{2,1,0:T(4,128)(2,1)S(1)}, bf16[8,4,2048]{2,1,0:T(4,128)(2,1)}, u32[]{:S(2)}) copy-start(bf16[8,4,2048]{2,1,0:T(4,128)(2,1)} %param.19) | copy-start | bytes 393220
  0.7 4.3 %copy-start.6 = (bf16[8,4,2048]{2,1,0:T(4,128)(2,1)S(1)}, bf16[8,4,2048]{2,1,0:T(4,128)(2,1)}, u32[]{:S(2)}) copy-start(bf16[8,4,2048]{2,1,0:T(4,128)(2,1)} %param.20) | copy-start | bytes 393220
  0.7 5.0 %copy-start.11 = (bf16[8,4,16]{2,1,0:T(4,128)(2,1)S(1)}, bf16[8,4,16]{2,1,0:T(4,128)(2,1)}, u32[]{:S(2)}) copy-start(bf16[8,4,16]{2,1,0:T(4,128)(2,1)} %param.22) | copy-start | bytes 3076
  0.7 5.8 %copy-start.12 = (bf16[8,4,16]{2,1,0:T(4,128)(2,1)S(1)}, bf16[8,4,16]{2,1,0:T(4,128)(2,1)}, u32[]{:S(2)}) copy-start(bf16[8,4,16]{2,1,0:T(4,128)(2,1)} %param.21) | copy-start | bytes 3076
  4.2 18.5 %copy-start.4 = (bf16[8,4,2048]{2,1,0:T(4,128)(2,1)S(1)}, bf16[8,4,2048]{2,1,0:T(4,128)(2,1)}, u32[]{:S(2)}) copy-start(bf16[8,4,2048]{2,1,0:T(4,128)(2,1)} %param.23) | copy-start | bytes 393220
  8.0 39.9 %copy-start.10 = (f32[2048]{0:T(1024)S(1)}, f32[2048]{0:T(1024)}, u32[]{:S(2)}) copy-start(f32[2048]{0:T(1024)} %param.28) | copy-start | bytes 24580
  52.7 13.6 %copy-start.2 = (bf16[1,256,2048]{2,1,0:T(8,128)(2,1)S(1)}, bf16[1,256,2048]{2,1,0:T(8,128)(2,1)}, u32[]{:S(2)}) copy-start(bf16[1,256,2048]{2,1,0:T(8,128)(2,1)} %param.30) | copy-start | bytes 3145732
  52.7 88.4 %all-to-all-start = ((bf16[256,48,128]{2,1,0:T(8,128)(2,1)}), bf16[256,48,128]{2,1,0:T(8,128)(2,1)}, u32[]{:S(2)}, u32[]{:S(2)}) async-start(bf16[256,48,128]{2,1,0:T(8,128)(2,1)} %copy.71), calls=%async_computation | async-start | bytes 6291456 | tf_op jit(solution)/shard_map/all_to_all | solution.py:415
  143.8 1.8 copy-start.3
  150.5 7.5 %copy-start.9 = (f32[8,4,10]{2,1,0:T(4,128)S(1)}, f32[8,4,10]{2,1,0:T(4,128)}, u32[]{:S(2)}) copy-start(f32[8,4,10]{2,1,0:T(4,128)} %param.25) | copy-start | bytes 3844
  150.5 95.8 %all-to-all-start.1 = ((bf16[256,48,128]{2,1,0:T(8,128)(2,1)}), bf16[256,48,128]{2,1,0:T(8,128)(2,1)}, u32[]{:S(2)}, u32[]{:S(2)}) async-start(bf16[256,48,128]{2,1,0:T(8,128)(2,1)} %copy.74), calls=%async_computation.1 | async-start | bytes 6291456 | tf_op jit(solution)/shard_map/all_to_all | solution.py:426
  240.9 2.2 copy-start.1

commit v12 on v11

--- a/solution.py
+++ b/solution.py
@@ -310,7 +310,7 @@
     stores = []
     for j in range(count):
         loads[j].wait()
-        store = pltpu.make_async_copy(held.at[j], out_hbm.at[place_ref[j]], out_sem.at[j])
+        store = pltpu.make_async_copy(held.at[j], out_hbm.at[place_ref[j, 0, 0]], out_sem.at[j])
         store.start()
         stores.append(store)
     for store in stores:
@@ -383,9 +383,9 @@
         target, states, query_rows, key_rows, value_rows, gate_rows, beta_logit, decay_logit, core_gain
     )
     packed_place = jnp.zeros_like(new_place).at[target].set(new_place)
-    tags = jnp.broadcast_to(packed_place[:, None, None], (ep_size, 8, 128))
+    tags = jnp.broadcast_to(packed_place[:, None, None], (ep_size, 1, 128))
     moved_rows, moved_tags = migrate(fresh_states, tags)
-    moved_out = place_rows(moved_rows, moved_tags[:, 0, 0])
+    moved_out = place_rows(moved_rows, moved_tags)
     token_count = req_count * step_count
     core_flat = core_out.reshape(token_count, core_out.shape[-1])
     attention = project(core_flat, out_weight)

time: 250 us -> 250 us (level)
  transfers between devices with their start and end apart: 2 -> 2, of which waited for: 1 -> 1; matrix products, arithmetic and copies ran while one was open for 2% -> 1% of each run, Pallas kernels for 33% -> 33%
where the time goes in v12:
time: 250 us; the launch traced here: 249 us
  Pallas kernels  120 us (48%)
  waiting for transfers between devices  73.6 us (29%)
  local copies, waits for them, and re-layouts  23.1 us (9%)
  starting transfers between devices  21.1 us (8%)
  matrix products  6.46 us (3%)
  other arithmetic  3.66 us (1%)
    pallas_call x1, Pallas kernels, migrate(): pl.pallas_call(migrate_kernel, in_specs=[any_spec, any_spec], out_specs=[...  80 us
    all_to_all x1, waiting for transfers between devices, shards(): arrived = lax.all_to_all(outgoing, ('dp', 'ep'), 0, 0, tiled=True)  73.6 us
    pallas_call x1, Pallas kernels, project(): pl.pallas_call(project_kernel, in_specs=[vmem, vmem], out_specs=vmem, out...  23.9 us
    all_to_all x1, starting transfers between devices, shards(): arrived = lax.all_to_all(outgoing, ('dp', 'ep'), 0, 0, tiled=True)  13.6 us
    pallas_call x1, Pallas kernels, recurrence(): pl.pallas_call(recur_kernel, grid_spec=pltpu.PrefetchScalarGridSpec(num_s...  13.2 us
    all_to_all x1, starting transfers between devices, shards(): returned = lax.all_to_all(result, ('dp', 'ep'), 0, 0, tiled=True)  7.51 us
  transfers between devices with their start and end apart: 2, of which 1 were waited for; matrix products, arithmetic and copies ran while one was open for 1% of the time, Pallas kernels for 33%

profile of v12, /device:TPU:1, one launch (start us, length us, event | category | flops | bytes accessed | tf_op | source)
XLA Modules:
  0.0 249.0 jit_solution(8361992781982642125)
XLA Ops:
  0.7 1.0 eq.45
  1.7 0.7 broadcast_multiply_fusion
  2.6 0.3 fusion.13
  3.1 0.2 fusion.17
  3.5 0.5 compare_select_fusion.1
  4.2 0.7 reshape.128.v_ref
  5.0 0.7 reshape.129.g_ref
  5.7 0.7 copy.63
  6.5 0.7 copy.65
  7.2 0.7 broadcast_in_dim.14
  8.0 13.2 %shard_map.167 = (bf16[8,16,128,128]{3,2,1,0:T(8,128)(2,1)}, bf16[8,4,2048]{2,1,0:T(4,128)(2,1)}) custom-call(s32[8]{0:T(128)} %get-tuple-element.11.slot_ref, bf16[8,16,128,128]{3,2,1,0:T(8,128)(2,1)} %s_ref.1, bf16[8,128,128]{2,1,0:T(8,128)(2,1)} %bitcast.83, bf16[8,4,16,128]{3,2,1,0:T(8,128)(2,1)} %reshape.128.v_ref, ...), custom_call_target="tpu_custom_call" | custom-call | tf_op jit(solution)/shard_map/pallas_call | solution.py:106
  21.1 1.6 reshape.131.rows_ref
  22.7 23.9 %shard_map.168 = bf16[32,2048]{1,0:T(8,128)(2,1)} custom-call(bf16[32,2048]{1,0:T(8,128)(2,1)} %reshape.131.rows_ref, bf16[2048,256]{1,0:T(8,128)(2,1)} %weight_ref.1), custom_call_target="tpu_custom_call" | custom-call | tf_op jit(solution)/shard_map/pallas_call | solution.py:285
  46.6 1.1 fusion.18
  47.9 1.0 convolution_convert_fusion
  49.0 3.7 %copy.71 = bf16[256,48,128]{2,1,0:T(8,128)(2,1)} copy(bf16[256,48,128]{2,0,1:T(8,128)(2,1)S(1)} %bitcast.76) | data formatting | bytes 6291456 | tf_op jit(solution)/shard_map/reshape | solution.py:414
  52.7 13.6 %all-to-all-start = ((bf16[256,48,128]{2,1,0:T(8,128)(2,1)}), bf16[256,48,128]{2,1,0:T(8,128)(2,1)}, u32[]{:S(2)}, u32[]{:S(2)}) async-start(bf16[256,48,128]{2,1,0:T(8,128)(2,1)} %copy.71), calls=%async_computation | async-start | bytes 6291456 | tf_op jit(solution)/shard_map/all_to_all | solution.py:415
  66.3 1.2 copy.87
  67.6 73.6 %all-to-all-done = bf16[256,48,128]{2,1,0:T(8,128)(2,1)} async-done(((bf16[256,48,128]{2,1,0:T(8,128)(2,1)}), bf16[256,48,128]{2,1,0:T(8,128)(2,1)}, u32[]{:S(2)}, u32[]{:S(2)}) %all-to-all-start) | async-done | bytes 3145760 | tf_op jit(solution)/shard_map/all_to_all | solution.py:415
  141.1 2.7 %copy.72 = bf16[256,48,128]{2,0,1:T(8,128)(2,1)S(1)} copy(bf16[256,48,128]{2,1,0:T(8,128)(2,1)} %all-to-all-done) | data formatting | bytes 6291456 | tf_op jit(solution)/shard_map/all_to_all | solution.py:415
  143.9 1.8 convolution_bitcast_fusion
  145.6 1.1 convolution_convert_fusion.1
  146.7 3.7 %copy.74 = bf16[256,48,128]{2,1,0:T(8,128)(2,1)} copy(bf16[256,48,128]{2,0,1:T(8,128)(2,1)S(1)} %bitcast.77) | data formatting | bytes 6291456 | tf_op jit(solution)/shard_map/reshape | solution.py:425
  150.5 7.5 %all-to-all-start.1 = ((bf16[256,48,128]{2,1,0:T(8,128)(2,1)}), bf16[256,48,128]{2,1,0:T(8,128)(2,1)}, u32[]{:S(2)}, u32[]{:S(2)}) async-start(bf16[256,48,128]{2,1,0:T(8,128)(2,1)} %copy.74), calls=%async_computation.1 | async-start | bytes 6291456 | tf_op jit(solution)/shard_map/all_to_all | solution.py:426
  158.3 0.6 scatter_custom_fusion
  158.9 0.7 broadcast_in_dim.35.tag_hbm
  159.5 80.0 %shard_map.169 = (bf16[8,16,128,128]{3,2,1,0:T(8,128)(2,1)}, s32[8,1,128]{2,1,0:T(1,128)}) custom-call(bf16[8,16,128,128]{3,2,1,0:T(8,128)(2,1)} %get-tuple-element.7.src_hbm, s32[8,1,128]{2,1,0:T(1,128)} %broadcast_in_dim.35.tag_hbm), custom_call_target="tpu_custom_call" | custom-call | bytes 8388608 | tf_op jit(solution)/shard_map/pallas_call | solution.py:213
  239.6 2.2 copy-done.1
  241.8 0.7 copy-done.2
  242.4 3.0 %shard_map.170 = bf16[8,16,128,128]{3,2,1,0:T(8,128)(2,1)} custom-call(s32[8,1,128]{2,1,0:T(1,128)S(1)} %copy-done.2, bf16[8,16,128,128]{3,2,1,0:T(8,128)(2,1)S(1)} %copy-done.1), custom_call_target="tpu_custom_call" | custom-call | tf_op jit(solution)/shard_map/pallas_call | solution.py:323
  245.7 2.6 %fusion.6 = f32[32,16,128]{2,0,1:T(8,128)S(1)} fusion(bf16[256,3,16,128]{3,2,1,0:T(8,128)(2,1)} %bitcast.27, bf16[3,32,256,3,1]{2,1,0,3,4:T(8,128)(2,1)S(1)} %bitcast.86), kind=kOutput, calls=%fused_computation.10 | convolution fusion | flops 302120960 | bytes 3555328 | tf_op jit(solution)/shard_map/esk,escl->kcl/dot_general | solution.py:436
  248.3 0.7 reshape.141
  (57 shorter events, 1.4 us)
Async XLA Ops:
  0.6 143.2 %copy-start = (bf16[1,2048,512]{2,1,0:T(8,128)(2,1)S(1)}, bf16[1,2048,512]{2,1,0:T(8,128)(2,1)}, u32[]{:S(2)}) copy-start(bf16[1,2048,512]{2,1,0:T(8,128)(2,1)} %param.29) | copy-start | bytes 6291460
  0.6 2.9 %copy-start.14 = (s32[8]{0:T(128)S(1)}, s32[8]{0:T(128)}, u32[]{:S(2)}) copy-start(s32[8]{0:T(128)} %param.31) | copy-start | bytes 100
  0.7 3.4 %copy-start.8 = (bf16[8,4,1024]{2,1,0:T(4,128)(2,1)S(1)}, bf16[8,4,1024]{2,1,0:T(4,128)(2,1)}, u32[]{:S(2)}) copy-start(bf16[8,4,1024]{2,1,0:T(4,128)(2,1)} %param.18) | copy-start | bytes 196612
  0.7 3.4 %copy-start.9 = (bf16[8,4,1024]{2,1,0:T(4,128)(2,1)S(1)}, bf16[8,4,1024]{2,1,0:T(4,128)(2,1)}, u32[]{:S(2)}) copy-start(bf16[8,4,1024]{2,1,0:T(4,128)(2,1)} %param.17) | copy-start | bytes 196612
  0.7 3.5 %copy-start.6 = (bf16[8,4,2048]{2,1,0:T(4,128)(2,1)S(1)}, bf16[8,4,2048]{2,1,0:T(4,128)(2,1)}, u32[]{:S(2)}) copy-start(bf16[8,4,2048]{2,1,0:T(4,128)(2,1)} %param.19) | copy-start | bytes 393220
  0.7 4.3 %copy-start.7 = (bf16[8,4,2048]{2,1,0:T(4,128)(2,1)S(1)}, bf16[8,4,2048]{2,1,0:T(4,128)(2,1)}, u32[]{:S(2)}) copy-start(bf16[8,4,2048]{2,1,0:T(4,128)(2,1)} %param.20) | copy-start | bytes 393220
  0.7 5.0 %copy-start.12 = (bf16[8,4,16]{2,1,0:T(4,128)(2,1)S(1)}, bf16[8,4,16]{2,1,0:T(4,128)(2,1)}, u32[]{:S(2)}) copy-start(bf16[8,4,16]{2,1,0:T(4,128)(2,1)} %param.22) | copy-start | bytes 3076
  0.7 5.8 %copy-start.13 = (bf16[8,4,16]{2,1,0:T(4,128)(2,1)S(1)}, bf16[8,4,16]{2,1,0:T(4,128)(2,1)}, u32[]{:S(2)}) copy-start(bf16[8,4,16]{2,1,0:T(4,128)(2,1)} %param.21) | copy-start | bytes 3076
  4.2 18.5 %copy-start.5 = (bf16[8,4,2048]{2,1,0:T(4,128)(2,1)S(1)}, bf16[8,4,2048]{2,1,0:T(4,128)(2,1)}, u32[]{:S(2)}) copy-start(bf16[8,4,2048]{2,1,0:T(4,128)(2,1)} %param.23) | copy-start | bytes 393220
  8.0 39.9 %copy-start.11 = (f32[2048]{0:T(1024)S(1)}, f32[2048]{0:T(1024)}, u32[]{:S(2)}) copy-start(f32[2048]{0:T(1024)} %param.28) | copy-start | bytes 24580
  52.7 13.6 %copy-start.3 = (bf16[1,256,2048]{2,1,0:T(8,128)(2,1)S(1)}, bf16[1,256,2048]{2,1,0:T(8,128)(2,1)}, u32[]{:S(2)}) copy-start(bf16[1,256,2048]{2,1,0:T(8,128)(2,1)} %param.30) | copy-start | bytes 3145732
  52.7 88.4 %all-to-all-start = ((bf16[256,48,128]{2,1,0:T(8,128)(2,1)}), bf16[256,48,128]{2,1,0:T(8,128)(2,1)}, u32[]{:S(2)}, u32[]{:S(2)}) async-start(bf16[256,48,128]{2,1,0:T(8,128)(2,1)} %copy.71), calls=%async_computation | async-start | bytes 6291456 | tf_op jit(solution)/shard_map/all_to_all | solution.py:415
  143.8 1.8 copy-start.4
  150.5 7.5 %copy-start.10 = (f32[8,4,10]{2,1,0:T(4,128)S(1)}, f32[8,4,10]{2,1,0:T(4,128)}, u32[]{:S(2)}) copy-start(f32[8,4,10]{2,1,0:T(4,128)} %param.25) | copy-start | bytes 3844
  150.5 95.2 %all-to-all-start.1 = ((bf16[256,48,128]{2,1,0:T(8,128)(2,1)}), bf16[256,48,128]{2,1,0:T(8,128)(2,1)}, u32[]{:S(2)}, u32[]{:S(2)}) async-start(bf16[256,48,128]{2,1,0:T(8,128)(2,1)} %copy.74), calls=%async_computation.1 | async-start | bytes 6291456 | tf_op jit(solution)/shard_map/all_to_all | solution.py:426
  239.6 2.2 copy-start.1
  241.8 0.7 copy-start.2

commit v13 on v12

--- a/solution.py
+++ b/solution.py
@@ -37,8 +37,8 @@
         lhs = jnp.concatenate([hi, mid, lo], axis=0).astype(bf16)
         res = jnp.dot(lhs, s_ref[0, h], preferred_element_type=f32)
         r_ref[pl.ds(h * span, span), :] = (res[0:span] + res[span:2 * span]) + res[2 * span:3 * span]
-    decay = jax.nn.sigmoid(dec_ref[0])
-    strength = jax.nn.sigmoid(beta_ref[0])
+    decay = jax.nn.sigmoid(dec_ref[0].astype(f32)).T
+    strength = jax.nn.sigmoid(beta_ref[0].astype(f32)).T
     gain = gain_ref[...]
     keys = [n_ref[pl.ds(t, heads, stride=span), :] for t in range(steps)]
     queries = [n_ref[pl.ds(steps + t, heads, stride=span), :] for t in range(steps)]
@@ -96,13 +96,13 @@
     kq = jnp.repeat(kq.transpose(0, 2, 1, 3), repeats, axis=1).reshape(batch, heads * span, width)
     values = value_rows.reshape(batch, steps, heads, width)
     gates = gate_rows.reshape(batch, steps, heads, width)
-    decay = decay_logit.astype(f32).transpose(0, 2, 1)
-    beta = beta_logit.astype(f32).transpose(0, 2, 1)
+    decay = decay_logit
+    beta = beta_logit
     gain = core_gain.reshape(1, width)
     state_in = pl.BlockSpec((1, heads, width, width), lambda i, slot: (i, 0, 0, 0))
     state_out = pl.BlockSpec((1, heads, width, width), lambda i, slot: (slot[i], 0, 0, 0))
     row_spec = pl.BlockSpec((1, steps, heads, width), lambda i, slot: (i, 0, 0, 0))
-    coef_spec = pl.BlockSpec((1, heads, steps), lambda i, slot: (i, 0, 0))
+    coef_spec = pl.BlockSpec((1, steps, heads), lambda i, slot: (i, 0, 0))
     fresh, core = pl.pallas_call(
         recur_kernel,
         grid_spec=pltpu.PrefetchScalarGridSpec(

time: 250 us -> 248 us (level)
  transfers between devices with their start and end apart: 2 -> 2, of which waited for: 1 -> 1; matrix products, arithmetic and copies ran while one was open for 1% -> 1% of each run, Pallas kernels for 33% -> 34%
where the time goes in v13:
time: 248 us; the launch traced here: 247 us
  Pallas kernels  119 us (48%)
  waiting for transfers between devices  73.6 us (30%)
  local copies, waits for them, and re-layouts  21.6 us (9%)
  starting transfers between devices  21.1 us (9%)
  matrix products  6.45 us (3%)
  other arithmetic  3.73 us (2%)
    pallas_call x1, Pallas kernels, migrate(): pl.pallas_call(migrate_kernel, in_specs=[any_spec, any_spec], out_specs=[...  80 us
    all_to_all x1, waiting for transfers between devices, shards(): arrived = lax.all_to_all(outgoing, ('dp', 'ep'), 0, 0, tiled=True)  73.6 us
    pallas_call x1, Pallas kernels, project(): pl.pallas_call(project_kernel, in_specs=[vmem, vmem], out_specs=vmem, out...  23.9 us
    all_to_all x1, starting transfers between devices, shards(): arrived = lax.all_to_all(outgoing, ('dp', 'ep'), 0, 0, tiled=True)  13.6 us
    pallas_call x1, Pallas kernels, recurrence(): pl.pallas_call(recur_kernel, grid_spec=pltpu.PrefetchScalarGridSpec(num_s...  12.4 us
    all_to_all x1, starting transfers between devices, shards(): returned = lax.all_to_all(result, ('dp', 'ep'), 0, 0, tiled=True)  7.52 us
  transfers between devices with their start and end apart: 2, of which 1 were waited for; matrix products, arithmetic and copies ran while one was open for 1% of the time, Pallas kernels for 34%

profile of v13, /device:TPU:1, one launch (start us, length us, event | category | flops | bytes accessed | tf_op | source)
XLA Modules:
  0.0 246.8 jit_solution(17237579457575687270)
XLA Ops:
  0.7 1.0 eq.45
  1.7 0.7 broadcast_multiply_fusion
  2.6 0.3 fusion.13
  3.1 0.2 fusion.17
  3.5 0.6 compare_select_fusion.1
  4.3 0.7 reshape.128.v_ref
  5.0 0.7 reshape.129.g_ref
  5.8 0.7 broadcast_in_dim.14
  6.5 12.4 %shard_map.167 = (bf16[8,16,128,128]{3,2,1,0:T(8,128)(2,1)}, bf16[8,4,2048]{2,1,0:T(4,128)(2,1)}) custom-call(s32[8]{0:T(128)} %get-tuple-element.11.slot_ref, bf16[8,16,128,128]{3,2,1,0:T(8,128)(2,1)} %s_ref.1, bf16[8,128,128]{2,1,0:T(8,128)(2,1)} %bitcast.81, bf16[8,4,16,128]{3,2,1,0:T(8,128)(2,1)} %reshape.128.v_ref, ...), custom_call_target="tpu_custom_call" | custom-call | tf_op jit(solution)/shard_map/pallas_call | solution.py:106
  18.9 1.6 reshape.131.rows_ref
  20.6 23.9 %shard_map.168 = bf16[32,2048]{1,0:T(8,128)(2,1)} custom-call(bf16[32,2048]{1,0:T(8,128)(2,1)} %reshape.131.rows_ref, bf16[2048,256]{1,0:T(8,128)(2,1)} %weight_ref.1), custom_call_target="tpu_custom_call" | custom-call | tf_op jit(solution)/shard_map/pallas_call | solution.py:285
  44.4 1.1 fusion.18
  45.5 0.2 compare_reduce_fusion
  45.7 1.0 convolution_convert_fusion
  46.8 3.7 %copy.46 = bf16[256,48,128]{2,1,0:T(8,128)(2,1)} copy(bf16[256,48,128]{2,0,1:T(8,128)(2,1)S(1)} %bitcast.74) | data formatting | bytes 6291456 | tf_op jit(solution)/shard_map/reshape | solution.py:414
  50.5 13.6 %all-to-all-start = ((bf16[256,48,128]{2,1,0:T(8,128)(2,1)}), bf16[256,48,128]{2,1,0:T(8,128)(2,1)}, u32[]{:S(2)}, u32[]{:S(2)}) async-start(bf16[256,48,128]{2,1,0:T(8,128)(2,1)} %copy.46), calls=%async_computation | async-start | bytes 6291456 | tf_op jit(solution)/shard_map/all_to_all | solution.py:415
  64.1 1.2 copy.62
  65.4 73.6 %all-to-all-done = bf16[256,48,128]{2,1,0:T(8,128)(2,1)} async-done(((bf16[256,48,128]{2,1,0:T(8,128)(2,1)}), bf16[256,48,128]{2,1,0:T(8,128)(2,1)}, u32[]{:S(2)}, u32[]{:S(2)}) %all-to-all-start) | async-done | bytes 3145760 | tf_op jit(solution)/shard_map/all_to_all | solution.py:415
  139.0 2.7 %copy.47 = bf16[256,48,128]{2,0,1:T(8,128)(2,1)S(1)} copy(bf16[256,48,128]{2,1,0:T(8,128)(2,1)} %all-to-all-done) | data formatting | bytes 6291456 | tf_op jit(solution)/shard_map/all_to_all | solution.py:415
  141.7 1.8 convolution_bitcast_fusion
  143.5 1.1 convolution_convert_fusion.1
  144.5 3.7 %copy.49 = bf16[256,48,128]{2,1,0:T(8,128)(2,1)} copy(bf16[256,48,128]{2,0,1:T(8,128)(2,1)S(1)} %bitcast.75) | data formatting | bytes 6291456 | tf_op jit(solution)/shard_map/reshape | solution.py:425
  148.3 7.5 %all-to-all-start.1 = ((bf16[256,48,128]{2,1,0:T(8,128)(2,1)}), bf16[256,48,128]{2,1,0:T(8,128)(2,1)}, u32[]{:S(2)}, u32[]{:S(2)}) async-start(bf16[256,48,128]{2,1,0:T(8,128)(2,1)} %copy.49), calls=%async_computation.1 | async-start | bytes 6291456 | tf_op jit(solution)/shard_map/all_to_all | solution.py:426
  156.1 0.6 scatter_custom_fusion
  156.7 0.7 broadcast_in_dim.35.tag_hbm
  157.4 80.0 %shard_map.169 = (bf16[8,16,128,128]{3,2,1,0:T(8,128)(2,1)}, s32[8,1,128]{2,1,0:T(1,128)}) custom-call(bf16[8,16,128,128]{3,2,1,0:T(8,128)(2,1)} %get-tuple-element.7.src_hbm, s32[8,1,128]{2,1,0:T(1,128)} %broadcast_in_dim.35.tag_hbm), custom_call_target="tpu_custom_call" | custom-call | bytes 8388608 | tf_op jit(solution)/shard_map/pallas_call | solution.py:213
  237.4 2.2 copy-done.1
  239.6 0.7 copy-done.2
  240.2 3.0 %shard_map.170 = bf16[8,16,128,128]{3,2,1,0:T(8,128)(2,1)} custom-call(s32[8,1,128]{2,1,0:T(1,128)S(1)} %copy-done.2, bf16[8,16,128,128]{3,2,1,0:T(8,128)(2,1)S(1)} %copy-done.1), custom_call_target="tpu_custom_call" | custom-call | tf_op jit(solution)/shard_map/pallas_call | solution.py:323
  243.3 0.2 fusion.11
  243.5 2.6 %fusion.6 = f32[32,16,128]{2,0,1:T(8,128)S(1)} fusion(bf16[256,3,16,128]{3,2,1,0:T(8,128)(2,1)} %bitcast.25, bf16[3,32,256,3,1]{2,1,0,3,4:T(8,128)(2,1)S(1)} %bitcast.82), kind=kOutput, calls=%fused_computation.10 | convolution fusion | flops 302120960 | bytes 3555328 | tf_op jit(solution)/shard_map/esk,escl->kcl/dot_general | solution.py:436
  246.1 0.7 reshape.141
  (49 shorter events, 1.1 us)
Async XLA Ops:
  0.6 141.0 %copy-start = (bf16[1,2048,512]{2,1,0:T(8,128)(2,1)S(1)}, bf16[1,2048,512]{2,1,0:T(8,128)(2,1)}, u32[]{:S(2)}) copy-start(bf16[1,2048,512]{2,1,0:T(8,128)(2,1)} %param.29) | copy-start | bytes 6291460
  0.6 2.9 %copy-start.12 = (s32[8]{0:T(128)S(1)}, s32[8]{0:T(128)}, u32[]{:S(2)}) copy-start(s32[8]{0:T(128)} %param.31) | copy-start | bytes 100
  0.7 3.5 %copy-start.8 = (bf16[8,4,1024]{2,1,0:T(4,128)(2,1)S(1)}, bf16[8,4,1024]{2,1,0:T(4,128)(2,1)}, u32[]{:S(2)}) copy-start(bf16[8,4,1024]{2,1,0:T(4,128)(2,1)} %param.18) | copy-start | bytes 196612
  0.7 3.5 %copy-start.9 = (bf16[8,4,1024]{2,1,0:T(4,128)(2,1)S(1)}, bf16[8,4,1024]{2,1,0:T(4,128)(2,1)}, u32[]{:S(2)}) copy-start(bf16[8,4,1024]{2,1,0:T(4,128)(2,1)} %param.17) | copy-start | bytes 196612
  0.7 3.6 %copy-start.6 = (bf16[8,4,2048]{2,1,0:T(4,128)(2,1)S(1)}, bf16[8,4,2048]{2,1,0:T(4,128)(2,1)}, u32[]{:S(2)}) copy-start(bf16[8,4,2048]{2,1,0:T(4,128)(2,1)} %param.19) | copy-start | bytes 393220
  0.7 4.3 %copy-start.7 = (bf16[8,4,2048]{2,1,0:T(4,128)(2,1)S(1)}, bf16[8,4,2048]{2,1,0:T(4,128)(2,1)}, u32[]{:S(2)}) copy-start(bf16[8,4,2048]{2,1,0:T(4,128)(2,1)} %param.20) | copy-start | bytes 393220
  4.2 16.3 %copy-start.5 = (bf16[8,4,2048]{2,1,0:T(4,128)(2,1)S(1)}, bf16[8,4,2048]{2,1,0:T(4,128)(2,1)}, u32[]{:S(2)}) copy-start(bf16[8,4,2048]{2,1,0:T(4,128)(2,1)} %param.23) | copy-start | bytes 393220
  6.5 39.2 %copy-start.11 = (f32[2048]{0:T(1024)S(1)}, f32[2048]{0:T(1024)}, u32[]{:S(2)}) copy-start(f32[2048]{0:T(1024)} %param.28) | copy-start | bytes 24580
  50.5 13.6 %copy-start.3 = (bf16[1,256,2048]{2,1,0:T(8,128)(2,1)S(1)}, bf16[1,256,2048]{2,1,0:T(8,128)(2,1)}, u32[]{:S(2)}) copy-start(bf16[1,256,2048]{2,1,0:T(8,128)(2,1)} %param.30) | copy-start | bytes 3145732
  50.5 88.4 %all-to-all-start = ((bf16[256,48,128]{2,1,0:T(8,128)(2,1)}), bf16[256,48,128]{2,1,0:T(8,128)(2,1)}, u32[]{:S(2)}, u32[]{:S(2)}) async-start(bf16[256,48,128]{2,1,0:T(8,128)(2,1)} %copy.46), calls=%async_computation | async-start | bytes 6291456 | tf_op jit(solution)/shard_map/all_to_all | solution.py:415
  141.7 1.8 copy-start.4
  148.3 7.5 %copy-start.10 = (f32[8,4,10]{2,1,0:T(4,128)S(1)}, f32[8,4,10]{2,1,0:T(4,128)}, u32[]{:S(2)}) copy-start(f32[8,4,10]{2,1,0:T(4,128)} %param.25) | copy-start | bytes 3844
  148.3 95.2 %all-to-all-start.1 = ((bf16[256,48,128]{2,1,0:T(8,128)(2,1)}), bf16[256,48,128]{2,1,0:T(8,128)(2,1)}, u32[]{:S(2)}, u32[]{:S(2)}) async-start(bf16[256,48,128]{2,1,0:T(8,128)(2,1)} %copy.49), calls=%async_computation.1 | async-start | bytes 6291456 | tf_op jit(solution)/shard_map/all_to_all | solution.py:426
  237.4 2.2 copy-start.1
  239.6 0.7 copy-start.2

commit v14 on v13

--- a/solution.py
+++ b/solution.py
@@ -55,7 +55,7 @@
         for j in range(t):
             kk = jnp.sum(keys[j] * keys[t], -1, keepdims=True)
             memory = memory + (carried[j] * kk) * updates[j]
-        values = v_ref[0, t].astype(f32)
+        values = jnp.concatenate([v_ref[0, pl.ds(t, 1), pl.ds(h * width, width)] for h in range(heads)], axis=0).astype(f32)
         update = (values - memory) * b_t
         updates.append(update)
         carried.append(jnp.ones_like(a_t))
@@ -65,7 +65,7 @@
             coef = qk if j == t else carried[j] * qk
             reading = reading + coef * updates[j]
         scaled = reading * lax.rsqrt(jnp.mean(reading * reading, -1, keepdims=True) + epsilon)
-        gate_vals = g_ref[0, t].astype(f32)
+        gate_vals = jnp.concatenate([g_ref[0, pl.ds(t, 1), pl.ds(h * width, width)] for h in range(heads)], axis=0).astype(f32)
         c_ref[pl.ds(t * heads, heads), :] = scaled * gain * (gate_vals * jax.nn.sigmoid(gate_vals))
     for j in range(steps):
         u_ref[pl.ds(j, heads, stride=span), :] = carried[j] * updates[j]
@@ -94,8 +94,8 @@
         [key_rows.reshape(batch, steps, key_heads, width), query_rows.reshape(batch, steps, key_heads, width)], axis=1
     )
     kq = jnp.repeat(kq.transpose(0, 2, 1, 3), repeats, axis=1).reshape(batch, heads * span, width)
-    values = value_rows.reshape(batch, steps, heads, width)
-    gates = gate_rows.reshape(batch, steps, heads, width)
+    values = value_rows
+    gates = gate_rows
     decay = decay_logit
     beta = beta_logit
     gain = core_gain.reshape(1, width)
@@ -111,8 +111,8 @@
             in_specs=[
                 state_in,
                 pl.BlockSpec((1, heads * span, width), lambda i, slot: (i, 0, 0)),
-                row_spec,
-                row_spec,
+                pl.BlockSpec((1, steps, heads * width), lambda i, slot: (i, 0, 0)),
+                pl.BlockSpec((1, steps, heads * width), lambda i, slot: (i, 0, 0)),
                 coef_spec,
                 coef_spec,
                 pl.BlockSpec((1, width), lambda i, slot: (0, 0)),

time: 248 us -> 246 us (level)
  no operation moved by 1% of the time
where the time goes in v14:
time: 246 us; the launch traced here: 245 us
  Pallas kernels  119 us (48%)
  waiting for transfers between devices  73.6 us (30%)
  starting transfers between devices  21.1 us (9%)
  local copies, waits for them, and re-layouts  20.1 us (8%)
  matrix products  6.45 us (3%)
  other arithmetic  3.7 us (2%)
    pallas_call x1, Pallas kernels, migrate(): pl.pallas_call(migrate_kernel, in_specs=[any_spec, any_spec], out_specs=[...  80 us
    all_to_all x1, waiting for transfers between devices, shards(): arrived = lax.all_to_all(outgoing, ('dp', 'ep'), 0, 0, tiled=True)  73.6 us
    pallas_call x1, Pallas kernels, project(): pl.pallas_call(project_kernel, in_specs=[vmem, vmem], out_specs=vmem, out...  23.9 us
    all_to_all x1, starting transfers between devices, shards(): arrived = lax.all_to_all(outgoing, ('dp', 'ep'), 0, 0, tiled=True)  13.6 us
    pallas_call x1, Pallas kernels, recurrence(): pl.pallas_call(recur_kernel, grid_spec=pltpu.PrefetchScalarGridSpec(num_s...  12.4 us
    all_to_all x1, starting transfers between devices, shards(): returned = lax.all_to_all(result, ('dp', 'ep'), 0, 0, tiled=True)  7.52 us
  transfers between devices with their start and end apart: 2, of which 1 were waited for; matrix products, arithmetic and copies ran while one was open for 1% of the time, Pallas kernels for 34%

profile of v14, /device:TPU:1, one launch (start us, length us, event | category | flops | bytes accessed | tf_op | source)
XLA Modules:
  0.0 245.3 jit_solution(17418278723548457266)
XLA Ops:
  0.7 1.0 eq.45
  1.7 0.7 broadcast_multiply_fusion
  2.4 0.1 iota_compare_fusion
  2.5 0.3 fusion.13
  3.1 0.2 fusion.17
  3.3 0.1 sub.18
  3.5 0.6 compare_select_fusion.1
  4.2 0.7 broadcast_in_dim.14
  5.0 12.4 %shard_map.167 = (bf16[8,16,128,128]{3,2,1,0:T(8,128)(2,1)}, bf16[8,4,2048]{2,1,0:T(4,128)(2,1)}) custom-call(s32[8]{0:T(128)} %get-tuple-element.11.slot_ref, bf16[8,16,128,128]{3,2,1,0:T(8,128)(2,1)} %s_ref.1, bf16[8,128,128]{2,1,0:T(8,128)(2,1)} %bitcast.81, bf16[8,4,2048]{2,1,0:T(4,128)(2,1)} %v_ref.1, bf16[8,4,2048]{2,1,0:T(4,128)(2,1)} %g_ref.1, ...), custom_call_target="tpu_custom_call" | custom-call | tf_op jit(solution)/shard_map/pallas_call | solution.py:106
  17.4 1.6 reshape.123.rows_ref
  19.0 23.9 %shard_map.168 = bf16[32,2048]{1,0:T(8,128)(2,1)} custom-call(bf16[32,2048]{1,0:T(8,128)(2,1)} %reshape.123.rows_ref, bf16[2048,256]{1,0:T(8,128)(2,1)} %weight_ref.1), custom_call_target="tpu_custom_call" | custom-call | tf_op jit(solution)/shard_map/pallas_call | solution.py:285
  42.9 1.1 fusion.18
  44.0 0.2 compare_reduce_fusion
  44.2 1.0 convolution_convert_fusion
  45.2 3.7 %copy.46 = bf16[256,48,128]{2,1,0:T(8,128)(2,1)} copy(bf16[256,48,128]{2,0,1:T(8,128)(2,1)S(1)} %bitcast.74) | data formatting | bytes 6291456 | tf_op jit(solution)/shard_map/reshape | solution.py:414
  49.0 13.6 %all-to-all-start = ((bf16[256,48,128]{2,1,0:T(8,128)(2,1)}), bf16[256,48,128]{2,1,0:T(8,128)(2,1)}, u32[]{:S(2)}, u32[]{:S(2)}) async-start(bf16[256,48,128]{2,1,0:T(8,128)(2,1)} %copy.46), calls=%async_computation | async-start | bytes 6291456 | tf_op jit(solution)/shard_map/all_to_all | solution.py:415
  62.6 1.2 copy.62
  63.8 73.6 %all-to-all-done = bf16[256,48,128]{2,1,0:T(8,128)(2,1)} async-done(((bf16[256,48,128]{2,1,0:T(8,128)(2,1)}), bf16[256,48,128]{2,1,0:T(8,128)(2,1)}, u32[]{:S(2)}, u32[]{:S(2)}) %all-to-all-start) | async-done | bytes 3145760 | tf_op jit(solution)/shard_map/all_to_all | solution.py:415
  137.4 2.7 %copy.47 = bf16[256,48,128]{2,0,1:T(8,128)(2,1)S(1)} copy(bf16[256,48,128]{2,1,0:T(8,128)(2,1)} %all-to-all-done) | data formatting | bytes 6291456 | tf_op jit(solution)/shard_map/all_to_all | solution.py:415
  140.1 1.8 convolution_bitcast_fusion
  141.9 1.1 convolution_convert_fusion.1
  143.0 3.7 %copy.49 = bf16[256,48,128]{2,1,0:T(8,128)(2,1)} copy(bf16[256,48,128]{2,0,1:T(8,128)(2,1)S(1)} %bitcast.75) | data formatting | bytes 6291456 | tf_op jit(solution)/shard_map/reshape | solution.py:425
  146.7 7.5 %all-to-all-start.1 = ((bf16[256,48,128]{2,1,0:T(8,128)(2,1)}), bf16[256,48,128]{2,1,0:T(8,128)(2,1)}, u32[]{:S(2)}, u32[]{:S(2)}) async-start(bf16[256,48,128]{2,1,0:T(8,128)(2,1)} %copy.49), calls=%async_computation.1 | async-start | bytes 6291456 | tf_op jit(solution)/shard_map/all_to_all | solution.py:426
  154.5 0.6 scatter_custom_fusion
  155.2 0.7 broadcast_in_dim.35.tag_hbm
  155.8 80.0 %shard_map.169 = (bf16[8,16,128,128]{3,2,1,0:T(8,128)(2,1)}, s32[8,1,128]{2,1,0:T(1,128)}) custom-call(bf16[8,16,128,128]{3,2,1,0:T(8,128)(2,1)} %get-tuple-element.7.src_hbm, s32[8,1,128]{2,1,0:T(1,128)} %broadcast_in_dim.35.tag_hbm), custom_call_target="tpu_custom_call" | custom-call | bytes 8388608 | tf_op jit(solution)/shard_map/pallas_call | solution.py:213
  235.9 2.2 copy-done.1
  238.0 0.7 copy-done.2
  238.7 3.0 %shard_map.170 = bf16[8,16,128,128]{3,2,1,0:T(8,128)(2,1)} custom-call(s32[8,1,128]{2,1,0:T(1,128)S(1)} %copy-done.2, bf16[8,16,128,128]{3,2,1,0:T(8,128)(2,1)S(1)} %copy-done.1), custom_call_target="tpu_custom_call" | custom-call | tf_op jit(solution)/shard_map/pallas_call | solution.py:323
  241.8 0.2 fusion.11
  242.0 2.6 %fusion.6 = f32[32,16,128]{2,0,1:T(8,128)S(1)} fusion(bf16[256,3,16,128]{3,2,1,0:T(8,128)(2,1)} %bitcast.25, bf16[3,32,256,3,1]{2,1,0,3,4:T(8,128)(2,1)S(1)} %bitcast.82), kind=kOutput, calls=%fused_computation.10 | convolution fusion | flops 302120960 | bytes 3555328 | tf_op jit(solution)/shard_map/esk,escl->kcl/dot_general | solution.py:436
  244.6 0.7 reshape.133
  (43 shorter events, 0.8 us)
Async XLA Ops:
  0.6 139.5 %copy-start = (bf16[1,2048,512]{2,1,0:T(8,128)(2,1)S(1)}, bf16[1,2048,512]{2,1,0:T(8,128)(2,1)}, u32[]{:S(2)}) copy-start(bf16[1,2048,512]{2,1,0:T(8,128)(2,1)} %param.29) | copy-start | bytes 6291460
  0.6 2.8 %copy-start.10 = (s32[8]{0:T(128)S(1)}, s32[8]{0:T(128)}, u32[]{:S(2)}) copy-start(s32[8]{0:T(128)} %param.31) | copy-start | bytes 100
  0.7 3.4 %copy-start.6 = (bf16[8,4,1024]{2,1,0:T(4,128)(2,1)S(1)}, bf16[8,4,1024]{2,1,0:T(4,128)(2,1)}, u32[]{:S(2)}) copy-start(bf16[8,4,1024]{2,1,0:T(4,128)(2,1)} %param.18) | copy-start | bytes 196612
  0.7 3.5 %copy-start.7 = (bf16[8,4,1024]{2,1,0:T(4,128)(2,1)S(1)}, bf16[8,4,1024]{2,1,0:T(4,128)(2,1)}, u32[]{:S(2)}) copy-start(bf16[8,4,1024]{2,1,0:T(4,128)(2,1)} %param.17) | copy-start | bytes 196612
  3.3 15.7 %copy-start.5 = (bf16[8,4,2048]{2,1,0:T(4,128)(2,1)S(1)}, bf16[8,4,2048]{2,1,0:T(4,128)(2,1)}, u32[]{:S(2)}) copy-start(bf16[8,4,2048]{2,1,0:T(4,128)(2,1)} %param.23) | copy-start | bytes 393220
  5.0 39.2 %copy-start.9 = (f32[2048]{0:T(1024)S(1)}, f32[2048]{0:T(1024)}, u32[]{:S(2)}) copy-start(f32[2048]{0:T(1024)} %param.28) | copy-start | bytes 24580
  49.0 13.6 %copy-start.3 = (bf16[1,256,2048]{2,1,0:T(8,128)(2,1)S(1)}, bf16[1,256,2048]{2,1,0:T(8,128)(2,1)}, u32[]{:S(2)}) copy-start(bf16[1,256,2048]{2,1,0:T(8,128)(2,1)} %param.30) | copy-start | bytes 3145732
  49.0 88.4 %all-to-all-start = ((bf16[256,48,128]{2,1,0:T(8,128)(2,1)}), bf16[256,48,128]{2,1,0:T(8,128)(2,1)}, u32[]{:S(2)}, u32[]{:S(2)}) async-start(bf16[256,48,128]{2,1,0:T(8,128)(2,1)} %copy.46), calls=%async_computation | async-start | bytes 6291456 | tf_op jit(solution)/shard_map/all_to_all | solution.py:415
  140.1 1.8 copy-start.4
  146.7 7.5 %copy-start.8 = (f32[8,4,10]{2,1,0:T(4,128)S(1)}, f32[8,4,10]{2,1,0:T(4,128)}, u32[]{:S(2)}) copy-start(f32[8,4,10]{2,1,0:T(4,128)} %param.25) | copy-start | bytes 3844
  146.7 95.2 %all-to-all-start.1 = ((bf16[256,48,128]{2,1,0:T(8,128)(2,1)}), bf16[256,48,128]{2,1,0:T(8,128)(2,1)}, u32[]{:S(2)}, u32[]{:S(2)}) async-start(bf16[256,48,128]{2,1,0:T(8,128)(2,1)} %copy.49), calls=%async_computation.1 | async-start | bytes 6291456 | tf_op jit(solution)/shard_map/all_to_all | solution.py:426
  235.8 2.2 copy-start.1
  238.0 0.7 copy-start.2
